TPU v7x, 256 devices: a whole 4x4x8 slice. The times are simulated.
256 devices in a mesh: expert: 128 (over x, z, y), dp: 2 (over core).
Axes of the slice: x: 4, y: 4, z: 8, core: 2. Of those that a mesh axis runs over, the one named last changes fastest.
Arguments:
- tokens: bfloat16 [16384, 4096], P(('expert', 'dp')), may hold values from -6 to 6
- routes: int32 [16384, 8], P(('expert', 'dp')), may hold values from 0 to 127, all different within a row; in each aligned block of 64 rows (0 to 63, 64 to 127, ...) at most 8 rows name the same one
- gate_probs: float32 [16384, 8], P(('expert', 'dp')), may hold values from 0.05 to 0.35
- gate_w: bfloat16 [128, 4096, 768], P('expert', None, 'dp'), may hold values from -0.09375 to 0.09375
- up_w: bfloat16 [128, 4096, 768], P('expert', None, 'dp'), may hold values from -0.09375 to 0.09375
- down_w: bfloat16 [128, 768, 4096], P('expert', 'dp'), may hold values from -0.21875 to 0.21875
Outputs:
- mixed_out: bfloat16 [16384, 4096], P(('expert', 'dp'))
Inputs may be any that keep to these rules, and one draw needn't show every extreme that they name: `routes`: each token names 8 different experts. Among the 64 tokens of one device (aligned blocks of rows), no expert is named by more than 8 tokens; in some block an expert is named by exactly 8 tokens.
All inputs are finite; a program needn't handle non-finite values.
Results may differ from a plain program's by a relative error of at most 0.0057.
Values may be sent and summed in bfloat16 or wider, within the bound.
No kernel may reach another device: no remote copies, remote signals or barrier semaphores. Data moves between devices by JAX's collectives and lax.ppermute only.
A program may use at most 192 MiB of HBM per device.

v0:
```python
import jax
import jax.numpy as jnp
from jax import lax
from jax.sharding import PartitionSpec as P


def swiglu(row_block, w_gate, w_up, w_down):
    gate_act = jnp.dot(row_block, w_gate, preferred_element_type=jnp.float32)
    up_act = jnp.dot(row_block, w_up, preferred_element_type=jnp.float32)
    hidden = (jax.nn.silu(gate_act) * up_act).astype(jnp.bfloat16)
    return jnp.dot(hidden, w_down, preferred_element_type=jnp.float32)


def apply_expert(row_block, w_gate, w_up, w_down):
    return swiglu(row_block, w_gate, w_up, w_down)


def body(tokens, routes, gate_probs, gate_w, up_w, down_w):
    experts = lax.axis_size("expert")
    tok_count, model_width = tokens.shape
    top_count = routes.shape[1]
    capacity = 2 * tok_count * top_count // experts
    expert_ids = jnp.arange(experts, dtype=jnp.int32)
    named_hits = jnp.sum((routes[:, :, None] == expert_ids).astype(jnp.int32), axis=1)
    before = jnp.cumsum(named_hits, axis=0) - named_hits
    slot_index = jnp.take_along_axis(before, routes, axis=1)
    target = routes * capacity + slot_index
    buffer_rows = jnp.arange(experts * capacity, dtype=jnp.int32)
    placer = jnp.sum(
        (target[None, :, :] == buffer_rows[:, None, None]).astype(jnp.float32), axis=2
    ).astype(jnp.bfloat16)
    outgoing = jnp.dot(placer, tokens, preferred_element_type=jnp.float32).astype(jnp.bfloat16)
    outgoing = outgoing.reshape(experts, capacity, model_width)
    present = (
        jnp.sum(placer.astype(jnp.float32), axis=1).astype(jnp.bfloat16).reshape(experts, capacity)
    )
    w_gate = gate_w[0]
    w_up = up_w[0]
    w_down = down_w[0]
    row_block = lax.all_to_all(outgoing, "expert", split_axis=0, concat_axis=0, tiled=True)
    flag_block = lax.all_to_all(present, "expert", split_axis=0, concat_axis=0, tiled=True)
    source_count = row_block.shape[0]
    item_count = row_block.shape[1]
    flat_rows = row_block.reshape(-1, model_width)
    flat_flags = flag_block.reshape(-1)
    both_rows = lax.all_gather(flat_rows, "dp", axis=0, tiled=True)
    partial_out = apply_expert(both_rows, w_gate, w_up, w_down)
    result = lax.psum_scatter(partial_out, "dp", scatter_dimension=0, tiled=True)
    masked = result * flat_flags.astype(jnp.float32)[:, None]
    answered = masked.astype(jnp.bfloat16).reshape(source_count, item_count, model_width)
    returned = lax.all_to_all(answered, "expert", split_axis=0, concat_axis=0, tiled=True)
    picked = returned.reshape(experts * capacity, model_width)[target]
    mixed_out = jnp.einsum(
        "tk,tkd->td", gate_probs, picked.astype(jnp.float32), precision=lax.Precision.HIGHEST
    )
    return mixed_out.astype(jnp.bfloat16)


def solution(mesh):
    return jax.shard_map(
        body,
        mesh=mesh,
        in_specs=(
            P(("expert", "dp"), None),
            P(("expert", "dp"), None),
            P(("expert", "dp"), None),
            P("expert", None, "dp"),
            P("expert", None, "dp"),
            P("expert", "dp", None),
        ),
        out_specs=P(("expert", "dp"), None),
        check_vma=False,
    )
```

profile of v0, /device:TPU:2, one launch (start us, length us, event | category | flops | bytes accessed | tf_op | source)
XLA Modules:
  0.0 579.9 jit_solution(941686837038767233)
XLA Ops:
  6.5 0.0 copy-start
  6.5 0.0 all-gather.2.cloned.1.call-start
  6.5 0.8 bitcast_or_fusion
  7.4 0.9 copy.35
  8.3 0.1 copy.36
  8.4 0.1 reshape.50
  8.4 0.1 convert_reduce_fusion.1
  8.6 0.1 reduce_window_sum.11
  8.7 0.0 copy-start.2
  8.7 3.6 gather_fusion.1
  12.3 0.1 reshape.53
  12.4 0.1 copy.37
  12.5 0.0 copy-done.2
  12.5 0.1 copy.38
  12.6 0.7 convert_reduce_fusion
  13.3 3.4 convert_bitcast_fusion
  16.7 201.5 %all_to_all.20 = bf16[128,8,4096]{2,1,0:T(8,128)(2,1)} all-to-all(bf16[128,8,4096]{2,1,0:T(8,128)(2,1)S(1)} %convert_bitcast_fusion), channel_id=1, replica_groups=mesh['expert'=128,'dp'=2] {'expert'}, dimensions={0} | all-to-all | bytes 16777216 | tf_op jit(solution)/shard_map/all_to_all | solution.py:40
  218.2 0.0 all-gather.2.cloned.1.call-update
  218.3 0.2 reduce-scatter.2.cloned.1.call-start
  218.5 31.1 %all-gather.2.cloned.1.call-done = bf16[2048,4096]{1,0:T(8,128)(2,1)} async-done(((bf16[1024,4096]{1,0:T(8,128)(2,1)}), bf16[2048,4096]{1,0:T(8,128)(2,1)}) %all-gather.2.cloned.1.call-update) | async-done | bytes 16777232 | tf_op jit(solution)/shard_map/all_gather | solution.py:46
  249.6 0.0 copy-start.4
  249.6 13.0 %fusion.6 = f32[2048,384]{1,0:T(8,128)S(1)} fusion(bf16[2048,4096]{1,0:T(8,128)(2,1)} %all-gather.2.cloned.1.call-done, bf16[1,4096,384]{2,1,0:T(8,128)(2,1)} %param.9), kind=kOutput, calls=%fused_computation.11 | convolution fusion | flops 6442450944 | bytes 23068672 | tf_op jit(solution)/shard_map/dot_general | solution.py:8
  262.6 0.0 copy-done.4
  262.6 12.5 %fusion.8 = bf16[2048,384]{1,0:T(8,128)(2,1)S(1)} fusion(bf16[2048,4096]{1,0:T(8,128)(2,1)} %all-gather.2.cloned.1.call-done, bf16[1,4096,384]{2,1,0:T(8,128)(2,1)S(1)} %copy-done.4, f32[2048,384]{1,0:T(8,128)S(1)} %fusion.6), kind=kOutput, calls=%fused_computation.13 | convolution fusion | flops 6447169536 | bytes 24641536 | tf_op jit(solution)/shard_map/dot_general | solution.py:9
  275.2 0.0 copy-done
  275.2 14.5 %fusion.3 = f32[2048,4096]{1,0:T(8,128)} fusion(bf16[2048,384]{1,0:T(8,128)(2,1)S(1)} %fusion.8, bf16[1,384,4096]{2,1,0:T(8,128)(2,1)S(1)} %copy-done), kind=kOutput, calls=%fused_computation.8 | convolution fusion | flops 6442450944 | bytes 38273024 | tf_op jit(solution)/shard_map/dot_general | solution.py:11
  289.6 0.0 reduce-scatter.2.cloned.1.call-update
  289.7 0.1 all_to_all.16
  289.8 24.6 %all_to_all.21 = bf16[128,1,8]{2,1,0:T(2,128)(2,1)S(1)} all-to-all(bf16[128,1,8]{2,1,0:T(2,128)(2,1)S(1)} %all_to_all.16), channel_id=1, replica_groups=mesh['expert'=128,'dp'=2] {'expert'}, dimensions={0} | all-to-all | bytes 4096 | tf_op jit(solution)/shard_map/all_to_all | solution.py:41
  314.4 0.2 convert_reduce_fusion.2
  314.6 0.1 reshape.41
  314.7 27.0 %reduce-scatter.2.cloned.1.call-done = f32[1024,4096]{1,0:T(8,128)} async-done(((f32[2048,4096]{1,0:T(8,128)}), f32[1024,4096]{1,0:T(8,128)}) %reduce-scatter.2.cloned.1.call-update) | async-done | bytes 16777232 | tf_op jit(solution)/shard_map/reduce_scatter | solution.py:48
  341.6 9.3 %fusion = bf16[128,8,4096]{2,1,0:T(8,128)(2,1)} fusion(f32[1024,4096]{1,0:T(8,128)} %reduce-scatter.2.cloned.1.call-done, f32[1024]{0:T(1024)S(1)} %reshape.41), kind=kLoop, calls=%fused_computation.3 | loop fusion | flops 8388608 | bytes 25169920 | tf_op jit(solution)/shard_map/reshape | solution.py:50
  350.9 0.0 copy-start.3
  350.9 14.5 %all-to-all-start.2 = ((bf16[128,8,4096]{2,1,0:T(8,128)(2,1)}), bf16[128,8,4096]{2,1,0:T(8,128)(2,1)}, u32[]{:S(2)}, u32[]{:S(2)}) async-start(bf16[128,8,4096]{2,1,0:T(8,128)(2,1)} %fusion), calls=%async_computation.3 | async-start | bytes 16777216 | tf_op jit(solution)/shard_map/all_to_all | solution.py:51
  365.4 0.0 copy-done.3
  365.4 0.1 copy.41
  365.5 0.1 copy.40
  365.6 0.1 reshape.44
  365.7 187.1 %all-to-all-done.2 = bf16[128,8,4096]{2,1,0:T(8,128)(2,1)} async-done(((bf16[128,8,4096]{2,1,0:T(8,128)(2,1)}), bf16[128,8,4096]{2,1,0:T(8,128)(2,1)}, u32[]{:S(2)}, u32[]{:S(2)}) %all-to-all-start.2) | async-done | bytes 8388640 | tf_op jit(solution)/shard_map/all_to_all | solution.py:51
  552.8 0.0 copy-start.1
  552.8 13.2 %gather_fusion = bf16[512,4096]{1,0:T(8,128)(2,1)} fusion(bf16[1024,4096]{1,0:T(8,128)(2,1)} %bitcast.7, s32[1024]{0:T(1024)S(1)} %pad_clamp_fusion), kind=kCustom, calls=%fused_computation | custom fusion | bytes 8390656 | tf_op jit(solution)/shard_map/gather | solution.py:52
  565.9 5.7 fusion.1
  571.6 1.4 copy.44
  573.0 0.0 copy-done.1
  (4 shorter events, 0.1 us)
Async XLA Ops:
  6.5 268.6 %copy-start = (bf16[1,384,4096]{2,1,0:T(8,128)(2,1)S(1)}, bf16[1,384,4096]{2,1,0:T(8,128)(2,1)}, u32[]{:S(2)}) copy-start(bf16[1,384,4096]{2,1,0:T(8,128)(2,1)} %param.11) | copy-start | bytes 9437188
  6.5 243.1 %all-gather.2.cloned.1.call-start = ((), (), s32[]{:S(2)}) async-start(), calls=%async_computation.4 | async-start | bytes 25165824 | tf_op jit(solution)/shard_map/all_gather | solution.py:46
  8.7 3.8 copy-start.2
  218.3 123.3 %reduce-scatter.2.cloned.1.call-start = ((), (), s32[]{:S(2)}) async-start(), calls=%async_computation.5 | async-start | bytes 50331648 | tf_op jit(solution)/shard_map/reduce_scatter | solution.py:48
  249.6 13.0 %copy-start.4 = (bf16[1,4096,384]{2,1,0:T(8,128)(2,1)S(1)}, bf16[1,4096,384]{2,1,0:T(8,128)(2,1)}, u32[]{:S(2)}) copy-start(bf16[1,4096,384]{2,1,0:T(8,128)(2,1)} %param.10) | copy-start | bytes 9437188
  350.9 14.5 %copy-start.3 = (f32[64,8]{0,1:T(8,128)S(1)}, f32[64,8]{0,1:T(8,128)}, u32[]{:S(2)}) copy-start(f32[64,8]{0,1:T(8,128)} %param.8) | copy-start | bytes 6148
  350.9 201.8 %all-to-all-start.2 = ((bf16[128,8,4096]{2,1,0:T(8,128)(2,1)}), bf16[128,8,4096]{2,1,0:T(8,128)(2,1)}, u32[]{:S(2)}, u32[]{:S(2)}) async-start(bf16[128,8,4096]{2,1,0:T(8,128)(2,1)} %fusion), calls=%async_computation.3 | async-start | bytes 16777216 | tf_op jit(solution)/shard_map/all_to_all | solution.py:51
  552.8 20.3 %copy-start.1 = (bf16[1,384,4096]{2,1,0:T(8,128)(2,1)S(1)}, bf16[1,384,4096]{2,1,0:T(8,128)(2,1)}, u32[]{:S(2)}) copy-start(bf16[1,384,4096]{2,1,0:T(8,128)(2,1)} %param.11) | copy-start | bytes 9437188
Sparse Core Ops, SparseCore 0:
  218.4 31.1 all-gather.1
  289.8 51.7 reduce-scatter.1
where the time goes:
time: 580 us
  waiting for transfers between devices  245 us (42%)
  blocking collectives  226 us (39%)
  matrix products  49.1 us (8%)
  local copies, waits for them, and re-layouts  19.9 us (3%)
  starting transfers between devices  14.7 us (3%)
  between operations  13.5 us (2%)
  other arithmetic  11.3 us (2%)
    all_to_all x1, blocking collectives, body(): lax.all_to_all(outgoing, 'expert', split_axis=0, concat_axis=0, tiled=True)  202 us
    all_to_all x1, waiting for transfers between devices, body(): lax.all_to_all(answered, 'expert', split_axis=0, concat_axis=0, tiled=True)  187 us
    all_gather x1, waiting for transfers between devices, body(): both_rows = lax.all_gather(flat_rows, 'dp', axis=0, tiled=True)  31.1 us
    reduce_scatter x1, waiting for transfers between devices, body(): lax.psum_scatter(partial_out, 'dp', scatter_dimension=0, tiled=True)  27 us
    all_to_all x1, blocking collectives, body(): lax.all_to_all(present, 'expert', split_axis=0, concat_axis=0, tiled=True)  24.6 us
    dot_general x1, matrix products, swiglu(): return jnp.dot(hidden, w_down, preferred_element_type=jnp.float32)  14.5 us
    all_to_all x1, starting transfers between devices, body(): lax.all_to_all(answered, 'expert', split_axis=0, concat_axis=0, tiled=True)  14.5 us
    gather x1, local copies, waits for them, and re-layouts, body(): picked = returned.reshape(experts * capacity, model_width)[target]  13.2 us
  transfers between devices with their start and end apart: 3, of which 3 were waited for; matrix products, arithmetic and copies ran while one was open for 0% of the time, Pallas kernels for 0%

commit v1 on v0

v1 whole, which is shorter than its diff:
```python
import jax
import jax.numpy as jnp
from jax import lax
from jax.experimental import pallas as pl
from jax.experimental.pallas import tpu as pltpu
from jax.sharding import Mesh
from jax.sharding import PartitionSpec as P

PLANE = ("x", "y")


def slot_table(routes, gate_probs, experts, capacity):
    tok_count, top_count = routes.shape
    flat = routes.T.reshape(-1)
    token = jnp.arange(tok_count * top_count, dtype=jnp.int32) % tok_count
    earlier = (flat[:, None] == flat[None, :]) & (token[None, :] < token[:, None])
    slot = jnp.sum(earlier.astype(jnp.int32), axis=1)
    target = flat * capacity + slot
    slots = jnp.arange(experts * capacity, dtype=jnp.int32)
    here = target[None, :] == slots[:, None]
    held = jnp.sum(jnp.where(here, (token + 1).astype(jnp.float32)[None, :], 0.0), axis=1)
    prob = jnp.sum(jnp.where(here, gate_probs.T.reshape(-1)[None, :], 0.0), axis=1)
    return held, prob


def mix_kernel(weight_ref, rows_ref, out_ref):
    sums = jnp.dot(weight_ref[...], rows_ref[...], preferred_element_type=jnp.float32)
    half = out_ref.shape[0]
    out_ref[...] = (sums[:half] + sums[half:]).astype(out_ref.dtype)


def mix(weight, rows, width=512):
    high = weight.astype(jnp.bfloat16)
    low = (weight - high.astype(jnp.float32)).astype(jnp.bfloat16)
    parts = jnp.concatenate([high, low], axis=0)
    return pl.pallas_call(
        mix_kernel,
        grid=(rows.shape[1] // width,),
        in_specs=[
            pl.BlockSpec(parts.shape, lambda i: (0, 0), pipeline_mode=pl.Buffered(1)),
            pl.BlockSpec((rows.shape[0], width), lambda i: (0, i)),
        ],
        out_specs=pl.BlockSpec((weight.shape[0], width), lambda i: (0, i)),
        out_shape=jax.ShapeDtypeStruct((weight.shape[0], rows.shape[1]), jnp.bfloat16),
        name="mix",
    )(parts, rows)


def body(tokens, routes, gate_probs, gate_w, up_w, down_w):
    x_size, z_size, y_size = lax.axis_size("x"), lax.axis_size("z"), lax.axis_size("y")
    experts = x_size * z_size * y_size
    plane = x_size * y_size
    tok_count, model_width = tokens.shape
    capacity = 2 * tok_count * routes.shape[1] // experts
    my_z = lax.axis_index("z")

    all_tokens = lax.all_gather(tokens, "z", axis=0, tiled=True)

    swap = [(0, 1), (1, 0)]
    w_gate = jnp.concatenate([gate_w[0], lax.ppermute(gate_w[0], "dp", swap)], axis=1)
    w_up = jnp.concatenate([up_w[0], lax.ppermute(up_w[0], "dp", swap)], axis=1)
    w_down = jnp.concatenate([down_w[0], lax.ppermute(down_w[0], "dp", swap)], axis=0)

    held, prob = slot_table(routes, gate_probs, experts, capacity)
    table = jnp.stack([held, prob]).reshape(2, x_size, z_size, y_size * capacity)
    table = table.transpose(2, 0, 1, 3)
    parts, sources = [], []
    for d in range(z_size):
        mine = lax.dynamic_index_in_dim(table, (my_z + d) % z_size, 0, keepdims=False)
        if d:
            mine = lax.ppermute(mine, "z", [(i, (i + d) % z_size) for i in range(z_size)])
        parts.append(mine.reshape(2, plane, capacity))
        sources.append((my_z - d) % z_size)
    parts = jnp.stack(parts, axis=2)
    source = jnp.stack(sources)[None, :, None]
    rows_here = plane * z_size * capacity
    held_row = parts[0].astype(jnp.int32)
    token_id = jnp.where(held_row > 0, source * tok_count + held_row - 1, -1).reshape(rows_here)
    weight = parts[1].reshape(rows_here)

    ring_ids = jnp.arange(z_size * tok_count, dtype=jnp.int32)
    placer = (token_id[:, None] == ring_ids[None, :]).astype(jnp.bfloat16)
    mixer = jnp.where(ring_ids[:, None] == token_id[None, :], weight[None, :], 0.0)

    outgoing = jnp.dot(placer, all_tokens, preferred_element_type=jnp.float32).astype(jnp.bfloat16)
    outgoing = outgoing.reshape(plane, rows_here // plane, model_width)
    rows = lax.all_to_all(outgoing, PLANE, split_axis=0, concat_axis=0, tiled=True)
    rows = rows.reshape(rows_here, model_width)
    gate_act = jnp.dot(rows, w_gate, preferred_element_type=jnp.float32)
    up_act = jnp.dot(rows, w_up, preferred_element_type=jnp.float32)
    hidden = (jax.nn.silu(gate_act) * up_act).astype(jnp.bfloat16)
    answers = jnp.dot(hidden, w_down, preferred_element_type=jnp.float32).astype(jnp.bfloat16)
    answers = answers.reshape(plane, rows_here // plane, model_width)
    returned = lax.all_to_all(answers, PLANE, split_axis=0, concat_axis=0, tiled=True)
    partial = mix(mixer, returned.reshape(rows_here, model_width))
    return lax.psum_scatter(partial, "z", scatter_dimension=0, tiled=True)


def solution(mesh):
    experts, dp = mesh.shape["expert"], mesh.shape["dp"]
    x_size = y_size = 4
    z_size = experts // (x_size * y_size)
    grid = Mesh(mesh.devices.reshape(x_size, z_size, y_size, dp), ("x", "z", "y", "dp"))
    every, owner = ("x", "z", "y", "dp"), ("x", "z", "y")
    return jax.shard_map(
        body,
        mesh=grid,
        in_specs=(
            P(every, None),
            P(every, None),
            P(every, None),
            P(owner, None, "dp"),
            P(owner, None, "dp"),
            P(owner, "dp", None),
        ),
        out_specs=P(every, None),
        check_vma=False,
    )
```

time: 580 us -> 482 us (0.83)
  blocking collectives: 226 us -> 0 us
  waiting for transfers between devices: 245 us -> 329 us
  starting transfers between devices: 14.7 us -> 77.5 us
  local copies, waits for them, and re-layouts: 19.9 us -> 3.53 us
  Pallas kernels: 0 us -> 13.4 us
  matrix products: 49.1 us -> 40.3 us
  other arithmetic: 11.3 us -> 3.15 us
    all_to_all x2 -> x0, blocking collectives: 226 us -> none  [the longest x1 202 us: body(): lax.all_to_all(outgoing, 'expert', split_axis=0, concat_axis=0, tiled=True)]
    reduce_scatter x1, waiting for transfers between devices: 27 us -> 85 us  [body(): return lax.psum_scatter(partial, 'z', scatter_dimension=0, tiled=True)]
    all_to_all x1 -> x2, starting transfers between devices: 14.5 us -> 58.3 us  [the longest x1 50.7 us: body(): lax.all_to_all(answers, PLANE, split_axis=0, concat_axis=0, tiled=True)]
    ppermute x0 -> x10, starting transfers between devices: none -> 19.2 us  [the longest x7 18.5 us: body(): lax.ppermute(mine, 'z', [(i, (i + d) % z_size) for i in range(z_size)])]
    gather x6 -> x0, local copies, waits for them, and re-layouts: 17.1 us -> none  [the longest x1 13.2 us: body(): picked = returned.reshape(experts * capacity, model_width)[target]]
    pallas_call x0 -> x1, Pallas kernels: none -> 13.4 us  [mix(): pl.pallas_call(mix_kernel, grid=(rows.shape[1] // width,), in_specs=[pl.B...]
    all_to_all x1 -> x2, waiting for transfers between devices: 187 us -> 198 us  [the longest x1 103 us: body(): lax.all_to_all(answers, PLANE, split_axis=0, concat_axis=0, tiled=True)]
    ppermute x0 -> x10, waiting for transfers between devices: none -> 10.3 us  [the longest x1 8.66 us: body(): lax.ppermute(gate_w[0], 'dp', swap)]
  transfers between devices with their start and end apart: 3 -> 14, of which waited for: 3 -> 6; matrix products, arithmetic and copies ran while one was open for 0% -> 6% of each run, Pallas kernels for 0% -> 0%
where the time goes in v1:
time: 482 us; the launch traced here: 481 us
  waiting for transfers between devices  329 us (68%)
  starting transfers between devices  77.5 us (16%)
  matrix products  40.3 us (8%)
  between operations  13.7 us (3%)
  Pallas kernels  13.4 us (3%)
    all_to_all x1, waiting for transfers between devices, body(): lax.all_to_all(answers, PLANE, split_axis=0, concat_axis=0, tiled=True)  103 us
    all_to_all x1, waiting for transfers between devices, body(): lax.all_to_all(outgoing, PLANE, split_axis=0, concat_axis=0, tiled=True)  95.5 us
    reduce_scatter x1, waiting for transfers between devices, body(): return lax.psum_scatter(partial, 'z', scatter_dimension=0, tiled=True)  85 us
    all_to_all x1, starting transfers between devices, body(): lax.all_to_all(answers, PLANE, split_axis=0, concat_axis=0, tiled=True)  50.7 us
    all_gather x1, waiting for transfers between devices, body(): all_tokens = lax.all_gather(tokens, 'z', axis=0, tiled=True)  35.1 us
    ppermute x7, starting transfers between devices, body(): lax.ppermute(mine, 'z', [(i, (i + d) % z_size) for i in range(z_size)])  18.5 us
    pallas_call x1, Pallas kernels, mix(): pl.pallas_call(mix_kernel, grid=(rows.shape[1] // width,), in_specs=[pl.B...  13.4 us
    dot_general x1, matrix products, body(): jnp.dot(hidden, w_down, preferred_element_type=jnp.float32)  10.8 us
  transfers between devices with their start and end apart: 14, of which 6 were waited for; matrix products, arithmetic and copies ran while one was open for 6% of the time, Pallas kernels for 0%

profile of v1, /device:TPU:2, one launch (start us, length us, event | category | flops | bytes accessed | tf_op | source)
XLA Modules:
  0.0 480.6 jit_solution(16164960074842158035)
XLA Ops:
  6.5 0.7 all-gather.2.cloned.1.call-update
  7.4 0.8 reshape.168
  8.1 0.8 broadcast_in_dim.46
  8.9 0.3 convert_reduce_fusion
  9.2 0.6 select_reduce_fusion
  9.9 0.1 stack.39
  10.1 2.0 collective-permute-start
  12.1 3.3 collective-permute-start.1
  15.4 4.0 collective-permute-start.2
  19.4 0.5 collective-permute-start.3
  19.9 4.9 %collective-permute-start.4 = (f32[2,4,32]{2,1,0:T(4,128)S(1)}, f32[2,4,32]{2,1,0:T(4,128)S(1)}, u32[]{:S(2)}, u32[]{:S(2)}) collective-permute-start(f32[2,4,32]{2,1,0:T(4,128)S(1)} %bitcast.35), channel_id=1, source_target_pairs={{0,40},{8,48},{16,56},{24,0},{32,8},{40,16},{48,24},{56,32},{1,41}... | collective-permute-start | bytes 3080 | tf_op jit(solution)/shard_map/ppermute | solution.py:71
  24.9 0.1 stack.51
  25.0 0.1 stack_reshape.24
  25.1 2.7 collective-permute-start.5
  27.8 1.0 collective-permute-start.6
  28.8 0.1 add.203
  28.9 0.1 add.204
  29.0 0.1 stack_reshape.25
  29.1 0.1 stack_reshape.26
  29.3 0.1 stack_reshape.27
  29.4 0.1 stack_reshape.28
  29.5 0.1 copy.17
  29.6 0.1 stack_reshape.29
  29.7 0.1 stack_reshape.30
  29.9 1.6 collective-permute-done.6
  31.5 0.1 stack_reshape.31
  31.7 0.1 copy.21
  31.8 0.1 convert_element_type.46
  31.9 35.1 %all-gather.2.cloned.1.call-done = bf16[512,4096]{1,0:T(8,128)(2,1)} async-done(((bf16[64,4096]{1,0:T(8,128)(2,1)}), bf16[512,4096]{1,0:T(8,128)(2,1)}) %all-gather.2.cloned.1.call-update) | async-done | bytes 4194320 | tf_op jit(solution)/shard_map/all_gather | solution.py:57
  66.9 9.0 %convolution_convert_fusion.1 = bf16[1024,4096]{1,0:T(8,128)(2,1)} fusion(bf16[512,4096]{1,0:T(8,128)(2,1)} %all-gather.2.cloned.1.call-done, s32[1024]{0:T(1024)S(1)} %add_select_fusion), kind=kOutput, calls=%fused_computation.1 | convolution fusion | flops 4299685888 | bytes 12587008 | tf_op jit(solution)/shard_map/dot_general | solution.py:85
  75.9 7.6 %all-to-all-start = ((bf16[16,64,4096]{2,1,0:T(8,128)(2,1)}), bf16[16,64,4096]{2,1,0:T(8,128)(2,1)}, u32[]{:S(2)}, u32[]{:S(2)}) async-start(bf16[16,64,4096]{2,1,0:T(8,128)(2,1)} %bitcast.32), calls=%async_computation | async-start | bytes 16777216 | tf_op jit(solution)/shard_map/all_to_all | solution.py:87
  83.5 0.1 collective-permute-start.7
  83.6 0.5 collective-permute-start.8
  84.1 0.1 collective-permute-start.9
  84.2 8.7 %collective-permute-done.7 = bf16[4096,384]{1,0:T(8,128)(2,1)} collective-permute-done((bf16[4096,384]{1,0:T(8,128)(2,1)S(1)}, bf16[4096,384]{1,0:T(8,128)(2,1)}, u32[]{:S(2)}, u32[]{:S(2)}) %collective-permute-start.7) | collective-permute-done | bytes 3145760 | tf_op jit(solution)/shard_map/ppermute | solution.py:60
  92.9 95.5 %all-to-all-done = bf16[16,64,4096]{2,1,0:T(8,128)(2,1)} async-done(((bf16[16,64,4096]{2,1,0:T(8,128)(2,1)}), bf16[16,64,4096]{2,1,0:T(8,128)(2,1)}, u32[]{:S(2)}, u32[]{:S(2)}) %all-to-all-start) | async-done | bytes 8388640 | tf_op jit(solution)/shard_map/all_to_all | solution.py:87
  188.4 10.3 %fusion = f32[1024,768]{1,0:T(8,128)S(1)} fusion(bf16[1024,4096]{1,0:T(8,128)(2,1)} %bitcast.18, bf16[4096,384]{1,0:T(8,128)(2,1)} %collective-permute-done.7, bf16[4096,384]{1,0:T(8,128)(2,1)S(1)} %bitcast.43), kind=kOutput, calls=%fused_computation.2 | convolution fusion | flops 6455033856 | bytes 17825792 | tf_op jit(solution)/shard_map/dot_general | solution.py:89
  198.7 10.3 %fusion.4 = f32[1024,768]{1,0:T(8,128)S(1)} fusion(bf16[1024,4096]{1,0:T(8,128)(2,1)} %bitcast.18, bf16[4096,384]{1,0:T(8,128)(2,1)} %collective-permute-done.8, bf16[4096,384]{1,0:T(8,128)(2,1)S(1)} %bitcast.45), kind=kOutput, calls=%fused_computation.6 | convolution fusion | flops 6455033856 | bytes 17825792 | tf_op jit(solution)/shard_map/dot_general | solution.py:90
  209.0 10.8 %convolution_convert_fusion = bf16[1024,4096]{1,0:T(8,128)(2,1)} fusion(bf16[384,4096]{1,0:T(8,128)(2,1)} %collective-permute-done.9, bf16[384,4096]{1,0:T(8,128)(2,1)S(1)} %bitcast.47, f32[1024,768]{1,0:T(8,128)S(1)} %fusion.4, f32[1024,768]{1,0:T(8,128)S(1)} %fusion), kind=kOutput, calls=%fused_computation | convolution fusion | flops 6463946752 | bytes 20971520 | tf_op jit(solution)/shard_map/dot_general | solution.py:92
  219.8 50.7 %all-to-all-start.1 = ((bf16[16,64,4096]{2,1,0:T(8,128)(2,1)}), bf16[16,64,4096]{2,1,0:T(8,128)(2,1)}, u32[]{:S(2)}, u32[]{:S(2)}) async-start(bf16[16,64,4096]{2,1,0:T(8,128)(2,1)} %bitcast.31), calls=%async_computation.1 | async-start | bytes 16777216 | tf_op jit(solution)/shard_map/all_to_all | solution.py:94
  270.5 0.1 copy.22
  270.6 0.1 broadcast_in_dim.48
  270.7 0.3 select_convert_fusion
  271.1 0.3 fusion.11
  271.4 1.5 pad_maximum_fusion.weight_ref
  272.9 102.5 %all-to-all-done.1 = bf16[16,64,4096]{2,1,0:T(8,128)(2,1)} async-done(((bf16[16,64,4096]{2,1,0:T(8,128)(2,1)}), bf16[16,64,4096]{2,1,0:T(8,128)(2,1)}, u32[]{:S(2)}, u32[]{:S(2)}) %all-to-all-start.1) | async-done | bytes 8388640 | tf_op jit(solution)/shard_map/all_to_all | solution.py:94
  375.4 13.4 %mix.1 = bf16[512,4096]{1,0:T(8,128)(2,1)} custom-call(bf16[1024,1024]{1,0:T(8,128)(2,1)} %pad_maximum_fusion.weight_ref, bf16[1024,4096]{1,0:T(8,128)(2,1)} %bitcast.23.rows_ref), custom_call_target="tpu_custom_call" | custom-call | tf_op jit(solution)/shard_map/mix/pallas_call | solution.py:36
  388.8 85.0 %reduce-scatter.2.cloned.1.call-done = bf16[64,4096]{1,0:T(8,128)(2,1)} async-done(((bf16[512,4096]{1,0:T(8,128)(2,1)}), bf16[64,4096]{1,0:T(8,128)(2,1)}) %reduce-scatter.2.cloned.1.call-update) | async-done | bytes 524304 | tf_op jit(solution)/shard_map/reduce_scatter | solution.py:96
  (41 shorter events, 0.8 us)
Async XLA Ops:
  6.5 60.4 %all-gather.2.cloned.1.call-start = ((), (), s32[]{:S(2)}) async-start(), calls=%async_computation.3 | async-start | bytes 4718592 | tf_op jit(solution)/shard_map/all_gather | solution.py:57
  10.1 15.0 %collective-permute-start = (f32[2,4,32]{2,1,0:T(4,128)S(1)}, f32[2,4,32]{2,1,0:T(4,128)S(1)}, u32[]{:S(2)}, u32[]{:S(2)}) collective-permute-start(f32[2,4,32]{2,1,0:T(4,128)S(1)} %bitcast.39), channel_id=1, source_target_pairs={{0,8},{8,16},{16,24},{24,32},{32,40},{40,48},{48,56},{56,0},{1,9},... | collective-permute-start | bytes 3080 | tf_op jit(solution)/shard_map/ppermute | solution.py:71
  12.1 15.7 %collective-permute-start.1 = (f32[2,4,32]{2,1,0:T(4,128)S(1)}, f32[2,4,32]{2,1,0:T(4,128)S(1)}, u32[]{:S(2)}, u32[]{:S(2)}) collective-permute-start(f32[2,4,32]{2,1,0:T(4,128)S(1)} %bitcast.38), channel_id=1, source_target_pairs={{0,16},{8,24},{16,32},{24,40},{32,48},{40,56},{48,0},{56,8},{1,17}... | collective-permute-start | bytes 3080 | tf_op jit(solution)/shard_map/ppermute | solution.py:71
  15.4 13.9 %collective-permute-start.2 = (f32[2,4,32]{2,1,0:T(4,128)S(1)}, f32[2,4,32]{2,1,0:T(4,128)S(1)}, u32[]{:S(2)}, u32[]{:S(2)}) collective-permute-start(f32[2,4,32]{2,1,0:T(4,128)S(1)} %bitcast.37), channel_id=1, source_target_pairs={{0,24},{8,32},{16,40},{24,48},{32,56},{40,0},{48,8},{56,16},{1,25}... | collective-permute-start | bytes 3080 | tf_op jit(solution)/shard_map/ppermute | solution.py:71
  19.4 10.0 %collective-permute-start.3 = (f32[2,4,32]{2,1,0:T(4,128)S(1)}, f32[2,4,32]{2,1,0:T(4,128)S(1)}, u32[]{:S(2)}, u32[]{:S(2)}) collective-permute-start(f32[2,4,32]{2,1,0:T(4,128)S(1)} %bitcast.36), channel_id=1, source_target_pairs={{0,32},{8,40},{16,48},{24,56},{32,0},{40,8},{48,16},{56,24},{1,33}... | collective-permute-start | bytes 3080 | tf_op jit(solution)/shard_map/ppermute | solution.py:71
  19.9 9.6 %collective-permute-start.4 = (f32[2,4,32]{2,1,0:T(4,128)S(1)}, f32[2,4,32]{2,1,0:T(4,128)S(1)}, u32[]{:S(2)}, u32[]{:S(2)}) collective-permute-start(f32[2,4,32]{2,1,0:T(4,128)S(1)} %bitcast.35), channel_id=1, source_target_pairs={{0,40},{8,48},{16,56},{24,0},{32,8},{40,16},{48,24},{56,32},{1,41}... | collective-permute-start | bytes 3080 | tf_op jit(solution)/shard_map/ppermute | solution.py:71
  25.1 4.6 collective-permute-start.5
  27.8 3.7 collective-permute-start.6
  75.9 7.6 %copy-start = (bf16[1,4096,384]{2,1,0:T(8,128)(2,1)S(1)}, bf16[1,4096,384]{2,1,0:T(8,128)(2,1)}, u32[]{:S(2)}) copy-start(bf16[1,4096,384]{2,1,0:T(8,128)(2,1)} %param.9) | copy-start | bytes 9437188
  75.9 112.4 %all-to-all-start = ((bf16[16,64,4096]{2,1,0:T(8,128)(2,1)}), bf16[16,64,4096]{2,1,0:T(8,128)(2,1)}, u32[]{:S(2)}, u32[]{:S(2)}) async-start(bf16[16,64,4096]{2,1,0:T(8,128)(2,1)} %bitcast.32), calls=%async_computation | async-start | bytes 16777216 | tf_op jit(solution)/shard_map/all_to_all | solution.py:87
  83.5 9.4 %collective-permute-start.7 = (bf16[4096,384]{1,0:T(8,128)(2,1)S(1)}, bf16[4096,384]{1,0:T(8,128)(2,1)}, u32[]{:S(2)}, u32[]{:S(2)}) collective-permute-start(bf16[4096,384]{1,0:T(8,128)(2,1)S(1)} %bitcast.42), channel_id=1, source_target_pairs={{0,1},{1,0},{2,3},{3,2},{4,5},{5,4},{6,7},{7,6},{8,9},{9,8},{10,11... | collective-permute-start | bytes 9437192 | tf_op jit(solution)/shard_map/ppermute | solution.py:60
  83.6 115.0 %collective-permute-start.8 = (bf16[4096,384]{1,0:T(8,128)(2,1)}, bf16[4096,384]{1,0:T(8,128)(2,1)}, u32[]{:S(2)}, u32[]{:S(2)}) collective-permute-start(bf16[4096,384]{1,0:T(8,128)(2,1)} %bitcast.44), channel_id=1, source_target_pairs={{0,1},{1,0},{2,3},{3,2},{4,5},{5,4},{6,7},{7,6},{8,9},{9,8},{10,11... | collective-permute-start | bytes 9437192 | tf_op jit(solution)/shard_map/ppermute | solution.py:61
  84.1 124.8 %collective-permute-start.9 = (bf16[384,4096]{1,0:T(8,128)(2,1)}, bf16[384,4096]{1,0:T(8,128)(2,1)}, u32[]{:S(2)}, u32[]{:S(2)}) collective-permute-start(bf16[384,4096]{1,0:T(8,128)(2,1)} %bitcast.46), channel_id=1, source_target_pairs={{0,1},{1,0},{2,3},{3,2},{4,5},{5,4},{6,7},{7,6},{8,9},{9,8},{10,11... | collective-permute-start | bytes 9437192 | tf_op jit(solution)/shard_map/ppermute | solution.py:62
  188.4 10.3 %copy-start.1 = (bf16[1,4096,384]{2,1,0:T(8,128)(2,1)S(1)}, bf16[1,4096,384]{2,1,0:T(8,128)(2,1)}, u32[]{:S(2)}) copy-start(bf16[1,4096,384]{2,1,0:T(8,128)(2,1)} %param.10) | copy-start | bytes 9437188
  198.6 10.3 %copy-start.2 = (bf16[1,384,4096]{2,1,0:T(8,128)(2,1)S(1)}, bf16[1,384,4096]{2,1,0:T(8,128)(2,1)}, u32[]{:S(2)}) copy-start(bf16[1,384,4096]{2,1,0:T(8,128)(2,1)} %param.11) | copy-start | bytes 9437188
  219.8 155.6 %all-to-all-start.1 = ((bf16[16,64,4096]{2,1,0:T(8,128)(2,1)}), bf16[16,64,4096]{2,1,0:T(8,128)(2,1)}, u32[]{:S(2)}, u32[]{:S(2)}) async-start(bf16[16,64,4096]{2,1,0:T(8,128)(2,1)} %bitcast.31), calls=%async_computation.1 | async-start | bytes 16777216 | tf_op jit(solution)/shard_map/all_to_all | solution.py:94
  270.5 203.3 %reduce-scatter.2.cloned.1.call-start = ((), (), s32[]{:S(2)}) async-start(), calls=%async_computation.4 | async-start | bytes 4718592 | tf_op jit(solution)/shard_map/reduce_scatter | solution.py:96
Sparse Core Ops, SparseCore 0:
  9.1 57.7 all-gather.1
  388.9 84.8 reduce-scatter.1

commit v2 on v1

v2 whole, which is shorter than its diff:
```python
import functools

import jax
import jax.numpy as jnp
from jax import lax
from jax.experimental import pallas as pl
from jax.experimental.pallas import tpu as pltpu
from jax.sharding import Mesh
from jax.sharding import PartitionSpec as P

WIDTH = 256
DIRECT = 768


def slot_table(routes, gate_probs, sizes, capacity):
    x_size, z_size, y_size = sizes
    tok_count, top_count = routes.shape
    flat = routes.T.reshape(-1)
    token = jnp.arange(tok_count * top_count, dtype=jnp.int32) % tok_count
    earlier = (flat[:, None] == flat[None, :]) & (token[None, :] < token[:, None])
    slot = jnp.sum(earlier.astype(jnp.int32), axis=1)
    ex, ez, ey = flat // (z_size * y_size), flat // y_size % z_size, flat % y_size
    target = ((ez * x_size + ex) * y_size + ey) * capacity + slot
    slots = jnp.arange(x_size * z_size * y_size * capacity, dtype=jnp.int32)
    here = target[None, :] == slots[:, None]
    held = jnp.sum(jnp.where(here, (token + 1).astype(jnp.float32)[None, :], 0.0), axis=1)
    prob = jnp.sum(jnp.where(here, gate_probs.T.reshape(-1)[None, :], 0.0), axis=1)
    return jnp.stack([held.reshape(z_size, -1), prob.reshape(z_size, -1)], axis=1)


def hits(table_ref, i, tok_count):
    row_token = table_ref[i, 0:1, :].astype(jnp.int32) - 1
    lanes = row_token.shape[1]
    return lax.broadcasted_iota(jnp.int32, (tok_count, lanes), 0) == row_token


def pack_kernel(order_ref, table_ref, tok_ref, out_ref):
    groups = table_ref.shape[0]
    sources, tok_count, width = tok_ref.shape
    plane, _, capacity, _ = out_ref.shape
    for i in range(groups):
        src = order_ref[i]
        block = tok_ref[src] if sources > 1 else tok_ref[0]
        place = jnp.where(hits(table_ref, i, tok_count), 1.0, 0.0).astype(jnp.bfloat16)
        rows = lax.dot_general(
            place, block, (((0,), (0,)), ((), ())), preferred_element_type=jnp.float32
        )
        out_ref[:, src] = rows.astype(jnp.bfloat16).reshape(plane, capacity, width)


def pack(order, table, tok, plane, capacity):
    groups = table.shape[0]
    sources, tok_count, width = tok.shape
    return pl.pallas_call(
        pack_kernel,
        grid_spec=pltpu.PrefetchScalarGridSpec(
            num_scalar_prefetch=1,
            grid=(width // WIDTH,),
            in_specs=[
                pl.BlockSpec(table.shape, lambda i, order: (0, 0, 0)),
                pl.BlockSpec((sources, tok_count, WIDTH), lambda i, order: (0, 0, i)),
            ],
            out_specs=pl.BlockSpec((plane, groups, capacity, WIDTH), lambda i, order: (0, 0, 0, i)),
        ),
        out_shape=jax.ShapeDtypeStruct((plane, groups, capacity, width), tok.dtype),
        name="pack",
    )(order, table, tok)


def mix_kernel(order_ref, table_ref, rows_ref, out_ref):
    groups = table_ref.shape[0]
    outs, tok_count, width = out_ref.shape
    plane, _, capacity, _ = rows_ref.shape
    total = None
    for i in range(groups):
        src = order_ref[i]
        prob = jnp.where(hits(table_ref, i, tok_count), table_ref[i, 1:2, :], 0.0)
        high = prob.astype(jnp.bfloat16)
        low = (prob - high.astype(jnp.float32)).astype(jnp.bfloat16)
        rows = rows_ref[:, src].reshape(plane * capacity, width)
        both = jnp.concatenate([high, low], axis=0)
        sums = jnp.dot(both, rows, preferred_element_type=jnp.float32)
        sums = sums[:tok_count] + sums[tok_count:]
        if outs > 1:
            out_ref[src] = sums.astype(out_ref.dtype)
        else:
            total = sums if total is None else total + sums
    if outs == 1:
        out_ref[0] = total.astype(out_ref.dtype)


def mix(order, table, rows, tok_count, outs):
    plane, groups, capacity, width = rows.shape
    return pl.pallas_call(
        mix_kernel,
        grid_spec=pltpu.PrefetchScalarGridSpec(
            num_scalar_prefetch=1,
            grid=(width // WIDTH,),
            in_specs=[
                pl.BlockSpec(table.shape, lambda i, order: (0, 0, 0)),
                pl.BlockSpec((plane, groups, capacity, WIDTH), lambda i, order: (0, 0, 0, i)),
            ],
            out_specs=pl.BlockSpec((outs, tok_count, WIDTH), lambda i, order: (0, 0, i)),
        ),
        out_shape=jax.ShapeDtypeStruct((outs, tok_count, width), jnp.bfloat16),
        name="mix",
    )(order, table, rows)


def dot(a, b):
    return jnp.dot(a, b, preferred_element_type=jnp.float32)


def body(tokens, routes, gate_probs, gate_w, up_w, down_w):
    sizes = tuple(lax.axis_size(a) for a in ("x", "z", "y"))
    x_size, z_size, y_size = sizes
    plane = x_size * y_size
    tok_count, model_width = tokens.shape
    capacity = 2 * tok_count * routes.shape[1] // (plane * z_size)
    rows_here = plane * z_size * capacity
    my_z = lax.axis_index("z")
    exchange = functools.partial(lax.all_to_all, split_axis=0, concat_axis=0, tiled=True)

    def in_plane(rows):
        width = rows.shape[-1]
        rows = exchange(rows.reshape(plane, z_size * capacity, width), ("x", "y"))
        return rows.reshape(plane, z_size, capacity, width)

    def direct(rows):
        width = rows.shape[-1]
        rows = exchange(rows.reshape(plane * z_size, capacity, width), ("x", "y", "z"))
        return rows.reshape(plane, z_size, capacity, width)

    first, rest = tokens[:, :DIRECT], tokens[:, DIRECT:]
    all_rest = lax.all_gather(rest, "z", axis=0, tiled=False)

    table = slot_table(routes, gate_probs, sizes, capacity)
    plain = jnp.arange(z_size, dtype=jnp.int32)
    rows_first = direct(pack(plain, table, first[None], plane, capacity))

    swap = [(0, 1), (1, 0)]

    def whole(w, axis):
        return jnp.concatenate([w, lax.ppermute(w, "dp", swap)], axis=axis)

    w_gate, w_up, w_down = whole(gate_w[0], 1), whole(up_w[0], 1), whole(down_w[0], 0)

    parts = []
    for d in range(z_size):
        mine = lax.dynamic_index_in_dim(table, (my_z + d) % z_size, 0, keepdims=False)
        if d:
            mine = lax.ppermute(mine, "z", [(i, (i + d) % z_size) for i in range(z_size)])
        parts.append(mine)
    ring_table = jnp.stack(parts)
    ring_order = (my_z - plain) % z_size

    flat_first = rows_first.reshape(rows_here, DIRECT)
    gate_first, up_first = dot(flat_first, w_gate[:DIRECT]), dot(flat_first, w_up[:DIRECT])
    all_rest, gate_first, up_first, w_gate, w_up, w_down, ring_table, ring_order = (
        lax.optimization_barrier(
            (all_rest, gate_first, up_first, w_gate, w_up, w_down, ring_table, ring_order)
        )
    )
    rows_rest = in_plane(pack(ring_order, ring_table, all_rest, plane, capacity))
    flat_rest = rows_rest.reshape(rows_here, model_width - DIRECT)
    gate_act = gate_first + dot(flat_rest, w_gate[DIRECT:])
    up_act = up_first + dot(flat_rest, w_up[DIRECT:])
    hidden = (jax.nn.silu(gate_act) * up_act).astype(jnp.bfloat16)

    answers = dot(hidden, w_down[:, DIRECT:]).astype(jnp.bfloat16)
    back_rest = in_plane(answers.reshape(plane, z_size, capacity, model_width - DIRECT))
    partial = mix(ring_order, ring_table, back_rest, tok_count, z_size)
    partial, hidden = lax.optimization_barrier((partial, hidden))
    out_rest = lax.psum_scatter(partial, "z", scatter_dimension=0, tiled=True)[0]

    answers = dot(hidden, w_down[:, :DIRECT]).astype(jnp.bfloat16)
    back_first = direct(answers.reshape(plane, z_size, capacity, DIRECT))
    out_first = mix(plain, table, back_first, tok_count, 1)[0]
    return jnp.concatenate([out_first, out_rest], axis=1)


def solution(mesh):
    experts, dp = mesh.shape["expert"], mesh.shape["dp"]
    x_size = y_size = 4
    z_size = experts // (x_size * y_size)
    grid = Mesh(mesh.devices.reshape(x_size, z_size, y_size, dp), ("x", "z", "y", "dp"))
    every, owner = ("x", "z", "y", "dp"), ("x", "z", "y")
    return jax.shard_map(
        body,
        mesh=grid,
        in_specs=(
            P(every, None),
            P(every, None),
            P(every, None),
            P(owner, None, "dp"),
            P(owner, None, "dp"),
            P(owner, "dp", None),
        ),
        out_specs=P(every, None),
        check_vma=False,
    )
```

time: 482 us -> 427 us (0.89)
  waiting for transfers between devices: 329 us -> 48.5 us
  blocking collectives: 0 us -> 233 us
  starting transfers between devices: 77.5 us -> 38.1 us
  other arithmetic: 3.15 us -> 22.6 us
  Pallas kernels: 13.4 us -> 31.3 us
  matrix products: 40.3 us -> 32 us
    all_to_all x0 -> x3, blocking collectives: none -> 233 us  [the longest x2 166 us: in_plane(): rows = exchange(rows.reshape(plane, z_size * capacity, width), ('x', 'y'))]
    all_to_all x2 -> x1, waiting for transfers between devices: 198 us -> 0.01 us  [direct(): exchange(rows.reshape(plane * z_size, capacity, width), ('x', 'y', 'z'))]
    reduce_scatter x1, waiting for transfers between devices: 85 us -> 4.97 us  [body(): lax.psum_scatter(partial, 'z', scatter_dimension=0, tiled=True)[0]]
    all_to_all x2 -> x1, starting transfers between devices: 58.3 us -> 15.5 us  [direct(): exchange(rows.reshape(plane * z_size, capacity, width), ('x', 'y', 'z'))]
    ppermute x7, waiting for transfers between devices: 1.6 us -> 43.5 us  [body(): lax.ppermute(mine, 'z', [(i, (i + d) % z_size) for i in range(z_size)])]
    all_gather x1, waiting for transfers between devices: 35.1 us -> 0.01 us  [body(): all_rest = lax.all_gather(rest, 'z', axis=0, tiled=False)]
    pallas_call x1 -> x4, Pallas kernels: 13.4 us -> 31.3 us  [the longest x2 15.7 us: pack(): pl.pallas_call(pack_kernel, grid_spec=pltpu.PrefetchScalarGridSpec(num_sc...]
    concatenate x1 -> x4, other arithmetic: 1.5 us -> 17.6 us  [the longest x3 15.7 us: whole(): return jnp.concatenate([w, lax.ppermute(w, 'dp', swap)], axis=axis)]
  transfers between devices with their start and end apart: 14 -> 13, of which waited for: 6 -> 3; matrix products, arithmetic and copies ran while one was open for 6% -> 8% of each run, Pallas kernels for 0% -> 2%
where the time goes in v2:
time: 427 us; the launch traced here: 425 us
  blocking collectives  233 us (55%)
  waiting for transfers between devices  48.5 us (11%)
  starting transfers between devices  38.1 us (9%)
  matrix products  32 us (7%)
  Pallas kernels  31.3 us (7%)
  other arithmetic  22.6 us (5%)
  between operations  13.7 us (3%)
  local copies, waits for them, and re-layouts  6 us (1%)
    all_to_all x2, blocking collectives, in_plane(): rows = exchange(rows.reshape(plane, z_size * capacity, width), ('x', 'y'))  166 us
    all_to_all x1, blocking collectives, direct(): exchange(rows.reshape(plane * z_size, capacity, width), ('x', 'y', 'z'))  66.1 us
    ppermute x7, waiting for transfers between devices, body(): lax.ppermute(mine, 'z', [(i, (i + d) % z_size) for i in range(z_size)])  43.5 us
    dot_general x6, matrix products, dot(): return jnp.dot(a, b, preferred_element_type=jnp.float32)  32 us
    ppermute x7, starting transfers between devices, body(): lax.ppermute(mine, 'z', [(i, (i + d) % z_size) for i in range(z_size)])  22.4 us
    concatenate x3, other arithmetic, whole(): return jnp.concatenate([w, lax.ppermute(w, 'dp', swap)], axis=axis)  15.7 us
    pallas_call x2, Pallas kernels, pack(): pl.pallas_call(pack_kernel, grid_spec=pltpu.PrefetchScalarGridSpec(num_sc...  15.7 us
    pallas_call x2, Pallas kernels, mix(): pl.pallas_call(mix_kernel, grid_spec=pltpu.PrefetchScalarGridSpec(num_sca...  15.6 us
  transfers between devices with their start and end apart: 13, of which 3 were waited for; matrix products, arithmetic and copies ran while one was open for 8% of the time, Pallas kernels for 2%

profile of v2, /device:TPU:2, one launch (start us, length us, event | category | flops | bytes accessed | tf_op | source)
XLA Modules:
  0.0 424.8 jit_solution(14946161529286838494)
XLA Ops:
  6.5 0.0 collective-permute-start.1
  6.5 1.8 slice.24
  8.3 0.0 all-gather.3.cloned.1.call-update
  8.4 0.8 reshape.117
  9.1 0.3 convert_reduce_fusion
  9.5 0.8 broadcast_in_dim.30
  10.3 0.6 select_reduce_fusion.1
  10.9 1.5 slice_bitcast_fusion.tok_ref
  12.4 0.6 pad_maximum_fusion.4.table_ref
  13.1 0.5 iota.24.order_ref
  13.6 3.7 pack.2
  17.3 15.5 %all-to-all-start = ((bf16[128,8,768]{2,1,0:T(8,128)(2,1)}), bf16[128,8,768]{2,1,0:T(8,128)(2,1)S(1)}, u32[]{:S(2)}, u32[]{:S(2)}) async-start(bf16[128,8,768]{2,1,0:T(8,128)(2,1)} %bitcast.72), calls=%async_computation | async-start | bytes 3145728 | tf_op jit(solution)/shard_map/all_to_all | solution.py:131
  32.9 0.0 reduce-scatter.2.cloned.1.call-start
  32.9 0.1 collective-permute-start
  33.1 1.5 collective-permute-start.3
  34.7 2.4 collective-permute-start.4
  37.1 2.7 collective-permute-start.5
  39.8 0.6 and_select_fusion.order_ref
  40.3 41.8 %collective-permute-done.3 = f32[2,128]{1,0:T(2,128)S(1)} collective-permute-done((f32[2,128]{1,0:T(2,128)S(1)}, f32[2,128]{1,0:T(2,128)S(1)}, u32[]{:S(2)}, u32[]{:S(2)}) %collective-permute-start.3) | collective-permute-done | bytes 1056 | tf_op jit(solution)/shard_map/ppermute | solution.py:152
  82.2 6.3 %collective-permute-start.6 = (f32[2,128]{1,0:T(2,128)S(1)}, f32[2,128]{1,0:T(2,128)S(1)}, u32[]{:S(2)}, u32[]{:S(2)}) collective-permute-start(f32[2,128]{1,0:T(2,128)S(1)} %get-tuple-element.32), channel_id=1, source_target_pairs={{0,32},{8,40},{16,48},{24,56},{32,0},{40,8},{48,16},{56,24},{1,33}... | collective-permute-start | bytes 3080 | tf_op jit(solution)/shard_map/ppermute | solution.py:152
  88.5 0.0 collective-permute-done.5
  88.6 1.7 collective-permute-start.7
  90.2 3.7 collective-permute-start.8
  94.0 0.0 collective-permute-done.7
  94.0 4.1 collective-permute-start.9
  98.1 1.6 collective-permute-done.9
  99.7 0.0 all-to-all-done
  99.8 0.0 collective-permute-done.1
  99.8 4.4 %fusion.5 = f32[1024,768]{1,0:T(8,128)} fusion(bf16[128,8,768]{2,1,0:T(8,128)(2,1)S(1)} %all-to-all-done, bf16[4096,384]{1,0:T(8,128)(2,1)} %bitcast.63, bf16[4096,384]{1,0:T(8,128)(2,1)} %collective-permute-done.1), kind=kOutput, calls=%fused_computation.18 | convolution fusion | flops 1210318848 | bytes 11010048 | tf_op jit(solution)/shard_map/dot_general | solution.py:111
  104.2 4.1 fusion.7
  108.3 5.1 %pad_maximum_fusion = bf16[4096,768]{1,0:T(8,128)(2,1)} fusion(bf16[4096,384]{1,0:T(8,128)(2,1)} %collective-permute-done, bf16[4096,384]{1,0:T(8,128)(2,1)S(1)} %bitcast.61), kind=kLoop, calls=%fused_computation.2 | loop fusion | flops 12582912 | bytes 12582912 | tf_op jit(solution)/shard_map/concatenate | solution.py:144
  113.5 5.2 %pad_maximum_fusion.1 = bf16[4096,768]{1,0:T(8,128)(2,1)} fusion(bf16[4096,384]{1,0:T(8,128)(2,1)} %collective-permute-done.1, bf16[4096,384]{1,0:T(8,128)(2,1)S(1)} %bitcast.64), kind=kLoop, calls=%fused_computation.5 | loop fusion | flops 12582912 | bytes 12582912 | tf_op jit(solution)/shard_map/concatenate | solution.py:144
  118.7 5.4 %pad_maximum_fusion.2 = bf16[768,4096]{1,0:T(8,128)(2,1)} fusion(bf16[384,4096]{1,0:T(8,128)(2,1)} %collective-permute-done.2, bf16[384,4096]{1,0:T(8,128)(2,1)S(1)} %bitcast.76), kind=kLoop, calls=%fused_computation.7 | loop fusion | flops 12582912 | bytes 12582912 | tf_op jit(solution)/shard_map/concatenate | solution.py:144
  124.1 11.9 %pack.3 = bf16[16,8,8,3328]{3,2,1,0:T(8,128)(2,1)} custom-call(s32[8]{0:T(128)} %and_select_fusion.order_ref, f32[8,2,128]{2,1,0:T(2,128)} %copy-done.5, bf16[8,64,3328]{2,1,0:T(8,128)(2,1)} %bitcast.74), custom_call_target="tpu_custom_call" | custom-call | tf_op jit(solution)/shard_map/pack/pallas_call | solution.py:54
  136.0 84.1 %all_to_all.20 = bf16[16,64,3328]{2,1,0:T(8,128)(2,1)S(1)} all-to-all(bf16[16,64,3328]{2,1,0:T(8,128)(2,1)} %bitcast.58), channel_id=1, replica_groups=mesh['x'=4,'z'=8,'y'=4,'dp'=2] {'x','y'}, dimensions={0} | all-to-all | bytes 13631488 | tf_op jit(solution)/shard_map/all_to_all | solution.py:126
  220.1 8.0 %fusion.3 = f32[1024,768]{1,0:T(8,128)S(1)} fusion(bf16[1024,3328]{1,0:T(8,128)(2,1)S(1)} %bitcast.65, bf16[4096,768]{1,0:T(8,128)(2,1)} %pad_maximum_fusion), kind=kOutput, calls=%fused_computation.11 | convolution fusion | flops 5234491392 | bytes 15073280 | tf_op jit(solution)/shard_map/dot_general | solution.py:111
  228.2 7.1 %fusion.1 = f32[1024,768]{1,0:T(8,128)} fusion(bf16[1024,3328]{1,0:T(8,128)(2,1)S(1)} %bitcast.66, bf16[4096,768]{1,0:T(8,128)(2,1)S(1)} %bitcast.71), kind=kOutput, calls=%fused_computation.9 | convolution fusion | flops 5234491392 | bytes 15073280 | tf_op jit(solution)/shard_map/dot_general | solution.py:111
  235.3 2.8 multiply_convert_fusion
  238.1 5.7 %convolution_convert_fusion = bf16[1024,3328]{1,0:T(8,128)(2,1)S(1)} fusion(bf16[1024,768]{1,0:T(8,128)(2,1)S(1)} %multiply_convert_fusion, bf16[768,4096]{1,0:T(8,128)(2,1)S(1)} %bitcast.69), kind=kOutput, calls=%fused_computation | convolution fusion | flops 5237899264 | bytes 13500416 | tf_op jit(solution)/shard_map/dot_general | solution.py:111
  243.8 82.3 %all_to_all.21 = bf16[16,64,3328]{2,1,0:T(8,128)(2,1)} all-to-all(bf16[16,64,3328]{2,1,0:T(8,128)(2,1)S(1)} %bitcast.67), channel_id=1, replica_groups=mesh['x'=4,'z'=8,'y'=4,'dp'=2] {'x','y'}, dimensions={0} | all-to-all | bytes 13631488 | tf_op jit(solution)/shard_map/all_to_all | solution.py:126
  326.2 11.6 %mix.2 = bf16[8,64,3328]{2,1,0:T(8,128)(2,1)} custom-call(s32[8]{0:T(128)} %and_select_fusion.order_ref, f32[8,2,128]{2,1,0:T(2,128)} %copy-done.5, bf16[16,8,8,3328]{3,2,1,0:T(8,128)(2,1)} %bitcast.57), custom_call_target="tpu_custom_call" | custom-call | tf_op jit(solution)/shard_map/mix/pallas_call | solution.py:94
  337.8 0.0 reduce-scatter.2.cloned.1.call-update
  337.8 2.7 fusion.9
  340.5 66.1 %all_to_all.22 = bf16[128,8,768]{2,1,0:T(8,128)(2,1)} all-to-all(bf16[128,8,768]{2,1,0:T(8,128)(2,1)S(1)} %fusion.9), channel_id=1, replica_groups=mesh['x'=4,'z'=8,'y'=4,'dp'=2] {'x','y','z'}, dimensions={0} | all-to-all | bytes 3145728 | tf_op jit(solution)/shard_map/all_to_all | solution.py:131
  406.6 0.5 iota.22.order_ref
  407.1 4.0 mix.3
  411.2 5.0 %reduce-scatter.2.cloned.1.call-done = bf16[1,64,3328]{2,1,0:T(8,128)(2,1)} async-done(((bf16[8,64,3328]{2,1,0:T(8,128)(2,1)}), bf16[1,64,3328]{2,1,0:T(8,128)(2,1)}) %reduce-scatter.2.cloned.1.call-update) | async-done | bytes 426000 | tf_op jit(solution)/shard_map/reduce_scatter | solution.py:174
  416.1 1.9 pad_maximum_fusion.3
  (41 shorter events, 0.2 us)
Async XLA Ops:
  6.5 117.5 %all-gather.3.cloned.1.call-start = ((), (), s32[]{:S(2)}) async-start(), calls=%async_computation.6 | async-start | bytes 3833856 | tf_op jit(solution)/shard_map/all_gather | solution.py:135
  6.5 93.2 %collective-permute-start.1 = (bf16[4096,384]{1,0:T(8,128)(2,1)}, bf16[4096,384]{1,0:T(8,128)(2,1)}, u32[]{:S(2)}, u32[]{:S(2)}) collective-permute-start(bf16[4096,384]{1,0:T(8,128)(2,1)} %bitcast.62), channel_id=1, source_target_pairs={{0,1},{1,0},{2,3},{3,2},{4,5},{5,4},{6,7},{7,6},{8,9},{9,8},{10,11... | collective-permute-start | bytes 9437192 | tf_op jit(solution)/shard_map/ppermute | solution.py:144
  17.3 82.4 %all-to-all-start = ((bf16[128,8,768]{2,1,0:T(8,128)(2,1)}), bf16[128,8,768]{2,1,0:T(8,128)(2,1)S(1)}, u32[]{:S(2)}, u32[]{:S(2)}) async-start(bf16[128,8,768]{2,1,0:T(8,128)(2,1)} %bitcast.72), calls=%async_computation | async-start | bytes 3145728 | tf_op jit(solution)/shard_map/all_to_all | solution.py:131
  32.9 383.3 %reduce-scatter.2.cloned.1.call-start = ((), (), s32[]{:S(2)}) async-start(), calls=%async_computation.5 | async-start | bytes 3833856 | tf_op jit(solution)/shard_map/reduce_scatter | solution.py:174
  32.9 71.3 %collective-permute-start = (bf16[4096,384]{1,0:T(8,128)(2,1)}, bf16[4096,384]{1,0:T(8,128)(2,1)}, u32[]{:S(2)}, u32[]{:S(2)}) collective-permute-start(bf16[4096,384]{1,0:T(8,128)(2,1)} %bitcast.59), channel_id=1, source_target_pairs={{0,1},{1,0},{2,3},{3,2},{4,5},{5,4},{6,7},{7,6},{8,9},{9,8},{10,11... | collective-permute-start | bytes 9437192 | tf_op jit(solution)/shard_map/ppermute | solution.py:144
  33.1 49.0 %collective-permute-start.3 = (f32[2,128]{1,0:T(2,128)S(1)}, f32[2,128]{1,0:T(2,128)S(1)}, u32[]{:S(2)}, u32[]{:S(2)}) collective-permute-start(f32[2,128]{1,0:T(2,128)S(1)} %get-tuple-element.29), channel_id=1, source_target_pairs={{0,8},{8,16},{16,24},{24,32},{32,40},{40,48},{48,56},{56,0},{1,9},... | collective-permute-start | bytes 3080 | tf_op jit(solution)/shard_map/ppermute | solution.py:152
  34.7 53.8 %collective-permute-start.4 = (f32[2,128]{1,0:T(2,128)S(1)}, f32[2,128]{1,0:T(2,128)S(1)}, u32[]{:S(2)}, u32[]{:S(2)}) collective-permute-start(f32[2,128]{1,0:T(2,128)S(1)} %get-tuple-element.30), channel_id=1, source_target_pairs={{0,16},{8,24},{16,32},{24,40},{32,48},{40,56},{48,0},{56,8},{1,17}... | collective-permute-start | bytes 3080 | tf_op jit(solution)/shard_map/ppermute | solution.py:152
  37.1 51.5 %collective-permute-start.5 = (f32[2,128]{1,0:T(2,128)S(1)}, f32[2,128]{1,0:T(2,128)S(1)}, u32[]{:S(2)}, u32[]{:S(2)}) collective-permute-start(f32[2,128]{1,0:T(2,128)S(1)} %get-tuple-element.31), channel_id=1, source_target_pairs={{0,24},{8,32},{16,40},{24,48},{32,56},{40,0},{48,8},{56,16},{1,25}... | collective-permute-start | bytes 3080 | tf_op jit(solution)/shard_map/ppermute | solution.py:152
  82.2 8.1 %collective-permute-start.6 = (f32[2,128]{1,0:T(2,128)S(1)}, f32[2,128]{1,0:T(2,128)S(1)}, u32[]{:S(2)}, u32[]{:S(2)}) collective-permute-start(f32[2,128]{1,0:T(2,128)S(1)} %get-tuple-element.32), channel_id=1, source_target_pairs={{0,32},{8,40},{16,48},{24,56},{32,0},{40,8},{48,16},{56,24},{1,33}... | collective-permute-start | bytes 3080 | tf_op jit(solution)/shard_map/ppermute | solution.py:152
  88.5 30.2 %collective-permute-start.2 = (bf16[384,4096]{1,0:T(8,128)(2,1)}, bf16[384,4096]{1,0:T(8,128)(2,1)}, u32[]{:S(2)}, u32[]{:S(2)}) collective-permute-start(bf16[384,4096]{1,0:T(8,128)(2,1)} %bitcast.75), channel_id=1, source_target_pairs={{0,1},{1,0},{2,3},{3,2},{4,5},{5,4},{6,7},{7,6},{8,9},{9,8},{10,11... | collective-permute-start | bytes 9437192 | tf_op jit(solution)/shard_map/ppermute | solution.py:144
  88.6 5.4 %collective-permute-start.7 = (f32[2,128]{1,0:T(2,128)S(1)}, f32[2,128]{1,0:T(2,128)S(1)}, u32[]{:S(2)}, u32[]{:S(2)}) collective-permute-start(f32[2,128]{1,0:T(2,128)S(1)} %get-tuple-element.34), channel_id=1, source_target_pairs={{0,40},{8,48},{16,56},{24,0},{32,8},{40,16},{48,24},{56,32},{1,41}... | collective-permute-start | bytes 3080 | tf_op jit(solution)/shard_map/ppermute | solution.py:152
  90.2 7.8 %collective-permute-start.8 = (f32[2,128]{1,0:T(2,128)S(1)}, f32[2,128]{1,0:T(2,128)S(1)}, u32[]{:S(2)}, u32[]{:S(2)}) collective-permute-start(f32[2,128]{1,0:T(2,128)S(1)} %get-tuple-element.33), channel_id=1, source_target_pairs={{0,48},{8,56},{16,0},{24,8},{32,16},{40,24},{48,32},{56,40},{1,49}... | collective-permute-start | bytes 3080 | tf_op jit(solution)/shard_map/ppermute | solution.py:152
  94.0 5.7 %collective-permute-start.9 = (f32[2,128]{1,0:T(2,128)S(1)}, f32[2,128]{1,0:T(2,128)S(1)}, u32[]{:S(2)}, u32[]{:S(2)}) collective-permute-start(f32[2,128]{1,0:T(2,128)S(1)} %get-tuple-element.27), channel_id=1, source_target_pairs={{0,56},{8,0},{16,8},{24,16},{32,24},{40,32},{48,40},{56,48},{1,57}... | collective-permute-start | bytes 3080 | tf_op jit(solution)/shard_map/ppermute | solution.py:152
  99.7 4.5 %copy-start.5 = (f32[8,2,128]{2,1,0:T(2,128)}, f32[8,2,128]{2,1,0:T(2,128)S(1)}, u32[]{:S(2)}) copy-start(f32[8,2,128]{2,1,0:T(2,128)S(1)} %constant_dynamic-update-slice_fusion.table_ref) | copy-start | bytes 24580
  99.7 4.5 %copy-start.2 = (bf16[1,4096,384]{2,1,0:T(8,128)(2,1)S(1)}, bf16[1,4096,384]{2,1,0:T(8,128)(2,1)}, u32[]{:S(2)}) copy-start(bf16[1,4096,384]{2,1,0:T(8,128)(2,1)} %param.9) | copy-start | bytes 9437188
  108.3 5.1 %copy-start.3 = (bf16[1,4096,384]{2,1,0:T(8,128)(2,1)S(1)}, bf16[1,4096,384]{2,1,0:T(8,128)(2,1)}, u32[]{:S(2)}) copy-start(bf16[1,4096,384]{2,1,0:T(8,128)(2,1)} %param.10) | copy-start | bytes 9437188
  113.5 5.2 %copy-start.4 = (bf16[1,384,4096]{2,1,0:T(8,128)(2,1)S(1)}, bf16[1,384,4096]{2,1,0:T(8,128)(2,1)}, u32[]{:S(2)}) copy-start(bf16[1,384,4096]{2,1,0:T(8,128)(2,1)} %param.11) | copy-start | bytes 9437188
  136.0 92.2 %slice-start.2 = ((s8[6291456]{0:T(1024)(128)(4,1)}), s8[4194304]{0:T(1024)(128)(4,1)S(1)}, s32[]{:S(2)}) async-start(s8[6291456]{0:T(1024)(128)(4,1)} %bitcast.70), calls=%async_computation.9 | async-start | bytes 8388608
  220.1 8.1 %slice-start.3 = ((s8[6291456]{0:T(1024)(128)(4,1)}), s8[2097152]{0:T(1024)(128)(4,1)S(1)}, s32[]{:S(2)}) async-start(s8[6291456]{0:T(1024)(128)(4,1)} %bitcast.70), calls=%async_computation.10 | async-start | bytes 4194304
  220.1 18.0 %slice-start = ((s8[6291456]{0:T(1024)(128)(4,1)}), s8[4194304]{0:T(1024)(128)(4,1)S(1)}, s32[]{:S(2)}) async-start(s8[6291456]{0:T(1024)(128)(4,1)} %bitcast.68), calls=%async_computation.7 | async-start | bytes 8388608
  228.2 7.1 %copy-start = (f32[1024,768]{1,0:T(8,128)S(1)}, f32[1024,768]{1,0:T(8,128)}, u32[]{:S(2)}) copy-start(f32[1024,768]{1,0:T(8,128)} %fusion.5) | copy-start | bytes 9437188
  228.2 7.1 %copy-start.1 = (f32[1024,768]{1,0:T(8,128)S(1)}, f32[1024,768]{1,0:T(8,128)}, u32[]{:S(2)}) copy-start(f32[1024,768]{1,0:T(8,128)} %fusion.7) | copy-start | bytes 9437188
  228.2 9.9 %slice-start.1 = ((s8[6291456]{0:T(1024)(128)(4,1)}), s8[2097152]{0:T(1024)(128)(4,1)S(1)}, s32[]{:S(2)}) async-start(s8[6291456]{0:T(1024)(128)(4,1)} %bitcast.68), calls=%async_computation.8 | async-start | bytes 4194304
Sparse Core Ops, SparseCore 0:
  9.1 84.2 all-gather.2
  337.9 78.1 reduce-scatter.1

commit v3 on v2

v3 whole, which is shorter than its diff:
```python
import jax
import jax.numpy as jnp
import numpy as np
from jax import lax
from jax.experimental import pallas as pl
from jax.experimental.pallas import tpu as pltpu
from jax.sharding import Mesh
from jax.sharding import PartitionSpec as P

ARRIVE = (1536, 2560)
LEAVE = (2048, 2048)


def slot_table(routes, gate_probs, sizes, capacity):
    x_size, z_size, y_size = sizes
    tok_count, top_count = routes.shape
    flat = routes.T.reshape(-1)
    token = jnp.arange(tok_count * top_count, dtype=jnp.int32) % tok_count
    earlier = (flat[:, None] == flat[None, :]) & (token[None, :] < token[:, None])
    slot = jnp.sum(earlier.astype(jnp.int32), axis=1)
    ex, ez, ey = flat // (z_size * y_size), flat // y_size % z_size, flat % y_size
    target = ((ez * x_size + ex) * y_size + ey) * capacity + slot
    slots = jnp.arange(x_size * z_size * y_size * capacity, dtype=jnp.int32)
    here = target[None, :] == slots[:, None]
    held = jnp.sum(jnp.where(here, (token + 1).astype(jnp.float32)[None, :], 0.0), axis=1)
    prob = jnp.sum(jnp.where(here, gate_probs.T.reshape(-1)[None, :], 0.0), axis=1)
    return jnp.stack([held.reshape(z_size, -1), prob.reshape(z_size, -1)], axis=1)


def hits(table_ref, i, tok_count):
    row_token = table_ref[i, 0:1, :].astype(jnp.int32) - 1
    lanes = row_token.shape[1]
    return lax.broadcasted_iota(jnp.int32, (tok_count, lanes), 0) == row_token


def pack_kernel(order_ref, table_ref, tok_ref, out_ref):
    plane, _, capacity, width = out_ref.shape
    tok_count = tok_ref.shape[1]
    place = jnp.where(hits(table_ref, 0, tok_count), 1.0, 0.0).astype(jnp.bfloat16)
    rows = lax.dot_general(
        place, tok_ref[0], (((0,), (0,)), ((), ())), preferred_element_type=jnp.float32
    )
    out_ref[:, 0] = rows.astype(jnp.bfloat16).reshape(plane, capacity, width)


def pack(order, table, tok, plane, capacity):
    sources, tok_count, width = tok.shape
    return pl.pallas_call(
        pack_kernel,
        grid_spec=pltpu.PrefetchScalarGridSpec(
            num_scalar_prefetch=1,
            grid=(sources,),
            in_specs=[
                pl.BlockSpec((1,) + table.shape[1:], lambda i, order: (i, 0, 0)),
                pl.BlockSpec((1, tok_count, width), lambda i, order: (order[i], 0, 0)),
            ],
            out_specs=pl.BlockSpec(
                (plane, 1, capacity, width), lambda i, order: (0, order[i], 0, 0)
            ),
        ),
        out_shape=jax.ShapeDtypeStruct((plane, sources, capacity, width), tok.dtype),
        name="pack",
    )(order, table, tok)


def mix_kernel(order_ref, table_ref, rows_ref, out_ref):
    plane, _, capacity, width = rows_ref.shape
    tok_count = out_ref.shape[1]
    prob = jnp.where(hits(table_ref, 0, tok_count), table_ref[0, 1:2, :], 0.0)
    high = prob.astype(jnp.bfloat16)
    low = (prob - high.astype(jnp.float32)).astype(jnp.bfloat16)
    rows = rows_ref[:, 0].reshape(plane * capacity, width)
    sums = jnp.dot(jnp.concatenate([high, low], axis=0), rows, preferred_element_type=jnp.float32)
    out_ref[0] = (sums[:tok_count] + sums[tok_count:]).astype(out_ref.dtype)


def mix(order, table, rows, tok_count):
    plane, sources, capacity, width = rows.shape
    return pl.pallas_call(
        mix_kernel,
        grid_spec=pltpu.PrefetchScalarGridSpec(
            num_scalar_prefetch=1,
            grid=(sources,),
            in_specs=[
                pl.BlockSpec((1,) + table.shape[1:], lambda i, order: (i, 0, 0)),
                pl.BlockSpec((plane, 1, capacity, width), lambda i, order: (0, order[i], 0, 0)),
            ],
            out_specs=pl.BlockSpec((1, tok_count, width), lambda i, order: (order[i], 0, 0)),
        ),
        out_shape=jax.ShapeDtypeStruct((sources, tok_count, width), jnp.bfloat16),
        name="mix",
    )(order, table, rows)


def cuts(widths):
    ends = np.cumsum(widths)
    return [slice(int(end) - width, int(end)) for width, end in zip(widths, ends, strict=True)]


def dot(a, b):
    return jnp.dot(a, b, preferred_element_type=jnp.float32)


def body(tokens, routes, gate_probs, gate_w, up_w, down_w):
    sizes = tuple(lax.axis_size(a) for a in ("x", "z", "y"))
    x_size, z_size, y_size = sizes
    plane = x_size * y_size
    tok_count, model_width = tokens.shape
    capacity = 2 * tok_count * routes.shape[1] // (plane * z_size)
    rows_here = plane * z_size * capacity
    my_z = lax.axis_index("z")
    def in_plane(rows):
        width = rows.shape[-1]
        rows = rows.reshape(plane, z_size * capacity, width)
        rows = lax.all_to_all(rows, ("x", "y"), split_axis=0, concat_axis=0, tiled=True)
        return rows.reshape(plane, z_size, capacity, width)

    into, back = cuts(ARRIVE), cuts(LEAVE)
    gathered = [lax.all_gather(tokens[:, part], "z", axis=0, tiled=False) for part in into]

    table = slot_table(routes, gate_probs, sizes, capacity)
    swap = [(0, 1), (1, 0)]

    def whole(w, axis):
        return jnp.concatenate([w, lax.ppermute(w, "dp", swap)], axis=axis)

    w_gate, w_up, w_down = whole(gate_w[0], 1), whole(up_w[0], 1), whole(down_w[0], 0)

    parts = []
    for d in range(z_size):
        mine = lax.dynamic_index_in_dim(table, (my_z + d) % z_size, 0, keepdims=False)
        if d:
            mine = lax.ppermute(mine, "z", [(i, (i + d) % z_size) for i in range(z_size)])
        parts.append(mine)
    ring_table = jnp.stack(parts)
    ring_order = (my_z - jnp.arange(z_size, dtype=jnp.int32)) % z_size

    ready = (w_gate, w_up, w_down, ring_table, ring_order)
    gate_act = up_act = 0.0
    for part, block in zip(into, gathered, strict=True):
        block, ready, gate_act, up_act = lax.optimization_barrier((block, ready, gate_act, up_act))
        w_gate, w_up, w_down, ring_table, ring_order = ready
        rows = in_plane(pack(ring_order, ring_table, block, plane, capacity))
        rows = rows.reshape(rows_here, -1)
        gate_act += dot(rows, w_gate[part])
        up_act += dot(rows, w_up[part])
    hidden = (jax.nn.silu(gate_act) * up_act).astype(jnp.bfloat16)

    outs = []
    for part in back:
        answers = dot(hidden, w_down[:, part]).astype(jnp.bfloat16)
        rows = in_plane(answers.reshape(plane, z_size, capacity, -1))
        partial = mix(ring_order, ring_table, rows, tok_count)
        partial, hidden = lax.optimization_barrier((partial, hidden))
        outs.append(lax.psum_scatter(partial, "z", scatter_dimension=0, tiled=True)[0])
    return jnp.concatenate(outs, axis=1)


def solution(mesh):
    experts, dp = mesh.shape["expert"], mesh.shape["dp"]
    x_size = y_size = 4
    z_size = experts // (x_size * y_size)
    grid = Mesh(mesh.devices.reshape(x_size, z_size, y_size, dp), ("x", "z", "y", "dp"))
    every, owner = ("x", "z", "y", "dp"), ("x", "z", "y")
    return jax.shard_map(
        body,
        mesh=grid,
        in_specs=(
            P(every, None),
            P(every, None),
            P(every, None),
            P(owner, None, "dp"),
            P(owner, None, "dp"),
            P(owner, "dp", None),
        ),
        out_specs=P(every, None),
        check_vma=False,
    )
```

time: 427 us -> 380 us (0.89)
  blocking collectives: 233 us -> 189 us
  starting transfers between devices: 38.1 us -> 9.88 us
  waiting for transfers between devices: 48.5 us -> 75.2 us
  other arithmetic: 22.6 us -> 18.1 us
    all_to_all x3 -> x4, blocking collectives: 233 us -> 189 us  [in_plane(): lax.all_to_all(rows, ('x', 'y'), split_axis=0, concat_axis=0, tiled=True)]
    reduce_scatter x1 -> x2, waiting for transfers between devices: 4.97 us -> 46.4 us  [body(): lax.psum_scatter(partial, 'z', scatter_dimension=0, tiled=True)[0]]
    all_to_all x1 -> x0, starting transfers between devices: 15.5 us -> none  [direct(): exchange(rows.reshape(plane * z_size, capacity, width), ('x', 'y', 'z'))]
    ppermute x7, waiting for transfers between devices: 43.5 us -> 28.8 us  [body(): lax.ppermute(mine, 'z', [(i, (i + d) % z_size) for i in range(z_size)])]
    ppermute x7, starting transfers between devices: 22.4 us -> 9.07 us  [body(): lax.ppermute(mine, 'z', [(i, (i + d) % z_size) for i in range(z_size)])]
  transfers between devices with their start and end apart: 13 -> 14, of which waited for: 3 -> 7; matrix products, arithmetic and copies ran while one was open for 8% -> 10% of each run, Pallas kernels for 2% -> 4%
where the time goes in v3:
time: 380 us; the launch traced here: 378 us
  blocking collectives  189 us (50%)
  waiting for transfers between devices  75.2 us (20%)
  matrix products  36 us (9%)
  Pallas kernels  31.5 us (8%)
  other arithmetic  18.1 us (5%)
  between operations  13.4 us (4%)
  starting transfers between devices  9.88 us (3%)
  local copies, waits for them, and re-layouts  4.96 us (1%)
    all_to_all x4, blocking collectives, in_plane(): lax.all_to_all(rows, ('x', 'y'), split_axis=0, concat_axis=0, tiled=True)  189 us
    reduce_scatter x2, waiting for transfers between devices, body(): lax.psum_scatter(partial, 'z', scatter_dimension=0, tiled=True)[0]  46.4 us
    dot_general x6, matrix products, dot(): return jnp.dot(a, b, preferred_element_type=jnp.float32)  36 us
    ppermute x7, waiting for transfers between devices, body(): lax.ppermute(mine, 'z', [(i, (i + d) % z_size) for i in range(z_size)])  28.8 us
    pallas_call x2, Pallas kernels, pack(): pl.pallas_call(pack_kernel, grid_spec=pltpu.PrefetchScalarGridSpec(num_sc...  15.8 us
    pallas_call x2, Pallas kernels, mix(): pl.pallas_call(mix_kernel, grid_spec=pltpu.PrefetchScalarGridSpec(num_sca...  15.7 us
    concatenate x3, other arithmetic, whole(): return jnp.concatenate([w, lax.ppermute(w, 'dp', swap)], axis=axis)  14.6 us
    ppermute x7, starting transfers between devices, body(): lax.ppermute(mine, 'z', [(i, (i + d) % z_size) for i in range(z_size)])  9.07 us
  transfers between devices with their start and end apart: 14, of which 7 were waited for; matrix products, arithmetic and copies ran while one was open for 10% of the time, Pallas kernels for 4%

profile of v3, /device:TPU:2, one launch (start us, length us, event | category | flops | bytes accessed | tf_op | source)
XLA Modules:
  0.0 378.2 jit_solution(56344900596698847)
XLA Ops:
  6.5 1.6 slice.25
  8.2 0.0 all-gather.7.cloned.1.call-update
  8.2 0.0 all-gather.5.cloned.1.call-start
  8.2 0.1 collective-permute-start
  8.3 0.5 collective-permute-start.1
  8.8 0.1 collective-permute-start.2
  8.9 0.8 reshape.117
  9.7 0.8 broadcast_in_dim.27
  10.5 0.3 convert_reduce_fusion
  10.8 0.6 select_reduce_fusion
  11.6 5.9 %collective-permute-start.9 = (f32[2,128]{1,0:T(2,128)S(1)}, f32[2,128]{1,0:T(2,128)S(1)}, u32[]{:S(2)}, u32[]{:S(2)}) collective-permute-start(f32[2,128]{1,0:T(2,128)S(1)} %get-tuple-element.45), channel_id=1, source_target_pairs={{0,56},{8,0},{16,8},{24,16},{32,24},{40,32},{48,40},{56,48},{1,57}... | collective-permute-start | bytes 3080 | tf_op jit(solution)/shard_map/ppermute | solution.py:133
  17.5 1.7 slice.24
  19.3 0.0 all-gather.5.cloned.1.call-update
  19.3 0.0 reduce-scatter.3.cloned.1.call-start
  19.4 0.6 and_select_fusion.order_ref
  20.0 2.3 collective-permute-done.3
  22.3 5.7 %collective-permute-done.4 = f32[2,128]{1,0:T(2,128)S(1)} collective-permute-done((f32[2,128]{1,0:T(2,128)S(1)}, f32[2,128]{1,0:T(2,128)S(1)}, u32[]{:S(2)}, u32[]{:S(2)}) %collective-permute-start.4) | collective-permute-done | bytes 1056 | tf_op jit(solution)/shard_map/ppermute | solution.py:133
  28.0 6.6 %collective-permute-done.5 = f32[2,128]{1,0:T(2,128)S(1)} collective-permute-done((f32[2,128]{1,0:T(2,128)S(1)}, f32[2,128]{1,0:T(2,128)S(1)}, u32[]{:S(2)}, u32[]{:S(2)}) %collective-permute-start.5) | collective-permute-done | bytes 1056 | tf_op jit(solution)/shard_map/ppermute | solution.py:133
  34.6 1.5 collective-permute-start.6
  36.1 6.0 %collective-permute-done.6 = f32[2,128]{1,0:T(2,128)S(1)} collective-permute-done((f32[2,128]{1,0:T(2,128)S(1)}, f32[2,128]{1,0:T(2,128)S(1)}, u32[]{:S(2)}, u32[]{:S(2)}) %collective-permute-start.6) | collective-permute-done | bytes 1056 | tf_op jit(solution)/shard_map/ppermute | solution.py:133
  42.1 0.7 collective-permute-start.7
  42.8 4.7 %collective-permute-done.7 = f32[2,128]{1,0:T(2,128)S(1)} collective-permute-done((f32[2,128]{1,0:T(2,128)S(1)}, f32[2,128]{1,0:T(2,128)S(1)}, u32[]{:S(2)}, u32[]{:S(2)}) %collective-permute-start.7) | collective-permute-done | bytes 1056 | tf_op jit(solution)/shard_map/ppermute | solution.py:133
  47.4 1.0 collective-permute-start.8
  48.4 3.5 collective-permute-done.8
  51.9 0.0 copy-start
  52.0 6.1 %pad_maximum_fusion = bf16[4096,768]{1,0:T(8,128)(2,1)} fusion(bf16[4096,384]{1,0:T(8,128)(2,1)} %collective-permute-done, bf16[4096,384]{1,0:T(8,128)(2,1)} %bitcast.68), kind=kLoop, calls=%fused_computation | loop fusion | flops 12582912 | bytes 12582912 | tf_op jit(solution)/shard_map/concatenate | solution.py:125
  58.1 5.1 %pad_maximum_fusion.1 = bf16[4096,768]{1,0:T(8,128)(2,1)} fusion(bf16[4096,384]{1,0:T(8,128)(2,1)} %collective-permute-done.1, bf16[4096,384]{1,0:T(8,128)(2,1)S(1)} %bitcast.70), kind=kLoop, calls=%fused_computation.1 | loop fusion | flops 12582912 | bytes 12582912 | tf_op jit(solution)/shard_map/concatenate | solution.py:125
  63.2 3.4 pad_maximum_fusion.2
  66.6 7.5 %pack.2 = bf16[16,8,8,1536]{3,2,1,0:T(8,128)(2,1)} custom-call(s32[8]{0:T(128)} %and_select_fusion.order_ref, f32[8,2,128]{2,1,0:T(2,128)} %copy-done.2, bf16[8,64,1536]{2,1,0:T(8,128)(2,1)} %bitcast.74), custom_call_target="tpu_custom_call" | custom-call | tf_op jit(solution)/shard_map/pack/pallas_call | solution.py:48
  74.1 38.6 %all_to_all.20 = bf16[16,64,1536]{2,1,0:T(8,128)(2,1)S(1)} all-to-all(bf16[16,64,1536]{2,1,0:T(8,128)(2,1)} %bitcast.56), channel_id=1, replica_groups=mesh['x'=4,'z'=8,'y'=4,'dp'=2] {'x','y'}, dimensions={0} | all-to-all | bytes 6291456 | tf_op jit(solution)/shard_map/all_to_all | solution.py:115
  112.7 6.0 %broadcast_add_fusion = f32[1024,768]{1,0:T(8,128)} fusion(f32[]{:T(128)} %constant.141.clone.1, bf16[1024,1536]{1,0:T(8,128)(2,1)S(1)} %bitcast.65, bf16[4096,768]{1,0:T(8,128)(2,1)} %pad_maximum_fusion.1), kind=kOutput, calls=%fused_computation.19 | convolution fusion | flops 2416705536 | bytes 8651264 | tf_op jit(solution)/shard_map/dot_general | solution.py:101
  118.7 6.0 %broadcast_add_fusion.1 = f32[1024,768]{1,0:T(8,128)} fusion(f32[]{:T(128)} %constant.141.clone.1, bf16[1024,1536]{1,0:T(8,128)(2,1)S(1)} %bitcast.66, bf16[4096,768]{1,0:T(8,128)(2,1)} %pad_maximum_fusion), kind=kOutput, calls=%fused_computation.20 | convolution fusion | flops 2416705536 | bytes 8651264 | tf_op jit(solution)/shard_map/dot_general | solution.py:101
  124.8 8.3 %pack.3 = bf16[16,8,8,2560]{3,2,1,0:T(8,128)(2,1)} custom-call(s32[8]{0:T(128)} %and_select_fusion.order_ref, f32[8,2,128]{2,1,0:T(2,128)} %copy-done.2, bf16[8,64,2560]{2,1,0:T(8,128)(2,1)} %bitcast.73), custom_call_target="tpu_custom_call" | custom-call | tf_op jit(solution)/shard_map/pack/pallas_call | solution.py:48
  133.1 59.9 %all_to_all.21 = bf16[16,64,2560]{2,1,0:T(8,128)(2,1)S(1)} all-to-all(bf16[16,64,2560]{2,1,0:T(8,128)(2,1)} %bitcast.53), channel_id=1, replica_groups=mesh['x'=4,'z'=8,'y'=4,'dp'=2] {'x','y'}, dimensions={0} | all-to-all | bytes 10485760 | tf_op jit(solution)/shard_map/all_to_all | solution.py:115
  193.0 8.2 %fusion = f32[1024,768]{1,0:T(8,128)} fusion(bf16[1024,2560]{1,0:T(8,128)(2,1)S(1)} %bitcast.61, bf16[4096,768]{1,0:T(8,128)(2,1)} %pad_maximum_fusion.1), kind=kOutput, calls=%fused_computation.3 | convolution fusion | flops 4026531840 | bytes 12320768 | tf_op jit(solution)/shard_map/dot_general | solution.py:101
  201.2 6.5 %multiply_convert_fusion = bf16[1024,768]{1,0:T(8,128)(2,1)S(1)} fusion(f32[1024,768]{1,0:T(8,128)S(1)} %copy-done.3, f32[1024,768]{1,0:T(8,128)} %fusion, f32[1024,768]{1,0:T(8,128)S(1)} %copy-done.4, bf16[1024,2560]{1,0:T(8,128)(2,1)S(1)} %bitcast.62, bf16[4096,768]{1,0:T(8,128)(2,1)S(1)} %bitcast.60), kind=kOutput, calls=%fused_computation.11 | convolution fusion | flops 4032823296 | bytes 20185088 | tf_op jit(solution)/shard_map/dot_general | solution.py:101
  207.7 3.7 convolution_convert_fusion.1
  211.4 45.8 %all_to_all.22 = bf16[16,64,2048]{2,1,0:T(8,128)(2,1)} all-to-all(bf16[16,64,2048]{2,1,0:T(8,128)(2,1)S(1)} %bitcast.64), channel_id=1, replica_groups=mesh['x'=4,'z'=8,'y'=4,'dp'=2] {'x','y'}, dimensions={0} | all-to-all | bytes 8388608 | tf_op jit(solution)/shard_map/all_to_all | solution.py:115
  257.3 7.9 %mix.2 = bf16[8,64,2048]{2,1,0:T(8,128)(2,1)} custom-call(s32[8]{0:T(128)} %and_select_fusion.order_ref, f32[8,2,128]{2,1,0:T(2,128)} %copy-done.2, bf16[16,8,8,2048]{3,2,1,0:T(8,128)(2,1)} %bitcast.55), custom_call_target="tpu_custom_call" | custom-call | tf_op jit(solution)/shard_map/mix/pallas_call | solution.py:79
  265.1 0.0 reduce-scatter.3.cloned.1.call-update
  265.2 0.0 reduce-scatter.5.cloned.1.call-start
  265.2 5.5 %convolution_convert_fusion = bf16[1024,2048]{1,0:T(8,128)(2,1)S(1)} fusion(bf16[1024,768]{1,0:T(8,128)(2,1)S(1)} %copy-done.6, bf16[768,4096]{1,0:T(8,128)(2,1)} %pad_maximum_fusion.2), kind=kOutput, calls=%fused_computation.7 | convolution fusion | flops 3223322624 | bytes 8912896 | tf_op jit(solution)/shard_map/dot_general | solution.py:101
  270.8 44.9 %all_to_all.23 = bf16[16,64,2048]{2,1,0:T(8,128)(2,1)} all-to-all(bf16[16,64,2048]{2,1,0:T(8,128)(2,1)S(1)} %bitcast.63), channel_id=1, replica_groups=mesh['x'=4,'z'=8,'y'=4,'dp'=2] {'x','y'}, dimensions={0} | all-to-all | bytes 8388608 | tf_op jit(solution)/shard_map/all_to_all | solution.py:115
  315.6 7.8 %mix.3 = bf16[8,64,2048]{2,1,0:T(8,128)(2,1)} custom-call(s32[8]{0:T(128)} %and_select_fusion.order_ref, f32[8,2,128]{2,1,0:T(2,128)} %copy-done.2, bf16[16,8,8,2048]{3,2,1,0:T(8,128)(2,1)} %bitcast.54), custom_call_target="tpu_custom_call" | custom-call | tf_op jit(solution)/shard_map/mix/pallas_call | solution.py:79
  323.4 0.0 reduce-scatter.5.cloned.1.call-update
  323.4 0.0 reduce-scatter.3.cloned.1.call-done
  323.5 46.4 %reduce-scatter.5.cloned.1.call-done = bf16[1,64,2048]{2,1,0:T(8,128)(2,1)} async-done(((bf16[8,64,2048]{2,1,0:T(8,128)(2,1)}), bf16[1,64,2048]{2,1,0:T(8,128)(2,1)}) %reduce-scatter.5.cloned.1.call-update) | async-done | bytes 262160 | tf_op jit(solution)/shard_map/reduce_scatter | solution.py:155
  369.8 1.9 pad_maximum_fusion.3
  (44 shorter events, 0.2 us)
Async XLA Ops:
  6.5 60.0 %all-gather.7.cloned.1.call-start = ((), (), s32[]{:S(2)}) async-start(), calls=%async_computation.9 | async-start | bytes 1769472 | tf_op jit(solution)/shard_map/all_gather | solution.py:119
  8.2 116.6 %all-gather.5.cloned.1.call-start = ((), (), s32[]{:S(2)}) async-start(), calls=%async_computation.8 | async-start | bytes 2949120 | tf_op jit(solution)/shard_map/all_gather | solution.py:119
  8.2 43.7 %collective-permute-start = (bf16[4096,384]{1,0:T(8,128)(2,1)}, bf16[4096,384]{1,0:T(8,128)(2,1)}, u32[]{:S(2)}, u32[]{:S(2)}) collective-permute-start(bf16[4096,384]{1,0:T(8,128)(2,1)} %bitcast.67), channel_id=1, source_target_pairs={{0,1},{1,0},{2,3},{3,2},{4,5},{5,4},{6,7},{7,6},{8,9},{9,8},{10,11... | collective-permute-start | bytes 9437192 | tf_op jit(solution)/shard_map/ppermute | solution.py:125
  8.3 49.7 %collective-permute-start.1 = (bf16[4096,384]{1,0:T(8,128)(2,1)}, bf16[4096,384]{1,0:T(8,128)(2,1)}, u32[]{:S(2)}, u32[]{:S(2)}) collective-permute-start(bf16[4096,384]{1,0:T(8,128)(2,1)} %bitcast.69), channel_id=1, source_target_pairs={{0,1},{1,0},{2,3},{3,2},{4,5},{5,4},{6,7},{7,6},{8,9},{9,8},{10,11... | collective-permute-start | bytes 9437192 | tf_op jit(solution)/shard_map/ppermute | solution.py:125
  8.8 54.4 %collective-permute-start.2 = (bf16[384,4096]{1,0:T(8,128)(2,1)}, bf16[384,4096]{1,0:T(8,128)(2,1)S(1)}, u32[]{:S(2)}, u32[]{:S(2)}) collective-permute-start(bf16[384,4096]{1,0:T(8,128)(2,1)} %bitcast.71), channel_id=1, source_target_pairs={{0,1},{1,0},{2,3},{3,2},{4,5},{5,4},{6,7},{7,6},{8,9},{9,8},{10,11... | collective-permute-start | bytes 9437192 | tf_op jit(solution)/shard_map/ppermute | solution.py:125
  11.6 40.3 %collective-permute-start.9 = (f32[2,128]{1,0:T(2,128)S(1)}, f32[2,128]{1,0:T(2,128)S(1)}, u32[]{:S(2)}, u32[]{:S(2)}) collective-permute-start(f32[2,128]{1,0:T(2,128)S(1)} %get-tuple-element.45), channel_id=1, source_target_pairs={{0,56},{8,0},{16,8},{24,16},{32,24},{40,32},{48,40},{56,48},{1,57}... | collective-permute-start | bytes 3080 | tf_op jit(solution)/shard_map/ppermute | solution.py:133
  17.5 4.8 %collective-permute-start.3 = (f32[2,128]{1,0:T(2,128)S(1)}, f32[2,128]{1,0:T(2,128)S(1)}, u32[]{:S(2)}, u32[]{:S(2)}) collective-permute-start(f32[2,128]{1,0:T(2,128)S(1)} %get-tuple-element.47), channel_id=1, source_target_pairs={{0,8},{8,16},{16,24},{24,32},{32,40},{40,48},{48,56},{56,0},{1,9},... | collective-permute-start | bytes 3080 | tf_op jit(solution)/shard_map/ppermute | solution.py:133
  19.3 304.2 %reduce-scatter.3.cloned.1.call-start = ((), (), s32[]{:S(2)}) async-start(), calls=%async_computation.6 | async-start | bytes 2359296 | tf_op jit(solution)/shard_map/reduce_scatter | solution.py:155
  22.3 5.7 %collective-permute-start.4 = (f32[2,128]{1,0:T(2,128)S(1)}, f32[2,128]{1,0:T(2,128)S(1)}, u32[]{:S(2)}, u32[]{:S(2)}) collective-permute-start(f32[2,128]{1,0:T(2,128)S(1)} %get-tuple-element.48), channel_id=1, source_target_pairs={{0,16},{8,24},{16,32},{24,40},{32,48},{40,56},{48,0},{56,8},{1,17}... | collective-permute-start | bytes 3080 | tf_op jit(solution)/shard_map/ppermute | solution.py:133
  28.0 6.6 %collective-permute-start.5 = (f32[2,128]{1,0:T(2,128)S(1)}, f32[2,128]{1,0:T(2,128)S(1)}, u32[]{:S(2)}, u32[]{:S(2)}) collective-permute-start(f32[2,128]{1,0:T(2,128)S(1)} %get-tuple-element.49), channel_id=1, source_target_pairs={{0,24},{8,32},{16,40},{24,48},{32,56},{40,0},{48,8},{56,16},{1,25}... | collective-permute-start | bytes 3080 | tf_op jit(solution)/shard_map/ppermute | solution.py:133
  34.6 7.5 %collective-permute-start.6 = (f32[2,128]{1,0:T(2,128)S(1)}, f32[2,128]{1,0:T(2,128)S(1)}, u32[]{:S(2)}, u32[]{:S(2)}) collective-permute-start(f32[2,128]{1,0:T(2,128)S(1)} %get-tuple-element.50), channel_id=1, source_target_pairs={{0,32},{8,40},{16,48},{24,56},{32,0},{40,8},{48,16},{56,24},{1,33}... | collective-permute-start | bytes 3080 | tf_op jit(solution)/shard_map/ppermute | solution.py:133
  42.1 5.4 %collective-permute-start.7 = (f32[2,128]{1,0:T(2,128)S(1)}, f32[2,128]{1,0:T(2,128)S(1)}, u32[]{:S(2)}, u32[]{:S(2)}) collective-permute-start(f32[2,128]{1,0:T(2,128)S(1)} %get-tuple-element.52), channel_id=1, source_target_pairs={{0,40},{8,48},{16,56},{24,0},{32,8},{40,16},{48,24},{56,32},{1,41}... | collective-permute-start | bytes 3080 | tf_op jit(solution)/shard_map/ppermute | solution.py:133
  47.4 4.5 %collective-permute-start.8 = (f32[2,128]{1,0:T(2,128)S(1)}, f32[2,128]{1,0:T(2,128)S(1)}, u32[]{:S(2)}, u32[]{:S(2)}) collective-permute-start(f32[2,128]{1,0:T(2,128)S(1)} %get-tuple-element.51), channel_id=1, source_target_pairs={{0,48},{8,56},{16,0},{24,8},{32,16},{40,24},{48,32},{56,40},{1,49}... | collective-permute-start | bytes 3080 | tf_op jit(solution)/shard_map/ppermute | solution.py:133
  51.9 6.1 %copy-start.2 = (f32[8,2,128]{2,1,0:T(2,128)}, f32[8,2,128]{2,1,0:T(2,128)S(1)}, u32[]{:S(2)}) copy-start(f32[8,2,128]{2,1,0:T(2,128)S(1)} %constant_dynamic-update-slice_fusion.table_ref) | copy-start | bytes 24580
  51.9 6.1 %copy-start = (bf16[1,4096,384]{2,1,0:T(8,128)(2,1)S(1)}, bf16[1,4096,384]{2,1,0:T(8,128)(2,1)}, u32[]{:S(2)}) copy-start(bf16[1,4096,384]{2,1,0:T(8,128)(2,1)} %param.10) | copy-start | bytes 9437188
  58.0 5.2 %copy-start.1 = (bf16[1,384,4096]{2,1,0:T(8,128)(2,1)S(1)}, bf16[1,384,4096]{2,1,0:T(8,128)(2,1)}, u32[]{:S(2)}) copy-start(bf16[1,384,4096]{2,1,0:T(8,128)(2,1)} %param.11) | copy-start | bytes 9437188
  133.1 68.1 %slice-start.2 = ((s8[6291456]{0:T(1024)(128)(4,1)}), s8[4194304]{0:T(1024)(128)(4,1)S(1)}, s32[]{:S(2)}) async-start(s8[6291456]{0:T(1024)(128)(4,1)} %bitcast.59), calls=%async_computation.12 | async-start | bytes 8388608
  193.0 8.2 %slice-start.3 = ((s8[6291456]{0:T(1024)(128)(4,1)}), s8[2097152]{0:T(1024)(128)(4,1)S(1)}, s32[]{:S(2)}) async-start(s8[6291456]{0:T(1024)(128)(4,1)} %bitcast.59), calls=%async_computation.13 | async-start | bytes 4194304
  193.0 8.2 %copy-start.3 = (f32[1024,768]{1,0:T(8,128)S(1)}, f32[1024,768]{1,0:T(8,128)}, u32[]{:S(2)}) copy-start(f32[1024,768]{1,0:T(8,128)} %broadcast_add_fusion) | copy-start | bytes 9437188
  193.0 8.2 %copy-start.4 = (f32[1024,768]{1,0:T(8,128)S(1)}, f32[1024,768]{1,0:T(8,128)}, u32[]{:S(2)}) copy-start(f32[1024,768]{1,0:T(8,128)} %broadcast_add_fusion.1) | copy-start | bytes 9437188
  193.0 14.8 %slice-start = ((s8[6291456]{0:T(1024)(128)(4,1)}), s8[4194304]{0:T(1024)(128)(4,1)S(1)}, s32[]{:S(2)}) async-start(s8[6291456]{0:T(1024)(128)(4,1)} %bitcast.57), calls=%async_computation.10 | async-start | bytes 8388608
  201.2 6.5 %slice-start.1 = ((s8[6291456]{0:T(1024)(128)(4,1)}), s8[2097152]{0:T(1024)(128)(4,1)S(1)}, s32[]{:S(2)}) async-start(s8[6291456]{0:T(1024)(128)(4,1)} %bitcast.57), calls=%async_computation.11 | async-start | bytes 4194304
  207.7 3.7 copy-start.5
  257.3 8.0 %copy-start.6 = (bf16[1024,768]{1,0:T(8,128)(2,1)S(1)}, bf16[1024,768]{1,0:T(8,128)(2,1)}, u32[]{:S(2)}) copy-start(bf16[1024,768]{1,0:T(8,128)(2,1)} %copy-done.5) | copy-start | bytes 4718596
  265.2 104.7 %reduce-scatter.5.cloned.1.call-start = ((), (), s32[]{:S(2)}) async-start(), calls=%async_computation.7 | async-start | bytes 2359296 | tf_op jit(solution)/shard_map/reduce_scatter | solution.py:155
Sparse Core Ops, SparseCore 0:
  9.1 42.9 all-gather.6
  53.9 40.9 all-gather.4
  265.3 42.2 reduce-scatter.2
  323.6 46.2 reduce-scatter.4

commit v4 on v3

v4 whole, which is shorter than its diff:
```python
import functools

import jax
import jax.numpy as jnp
import numpy as np
from jax import lax
from jax.experimental import pallas as pl
from jax.experimental.pallas import tpu as pltpu
from jax.sharding import Mesh
from jax.sharding import PartitionSpec as P

GROUP = 4
DEPTH = 512
ARRIVE = (1536, 2560)
LEAVE = (2048, 2048)


def slot_table(routes, gate_probs, sizes, capacity):
    x_size, z_size, y_size = sizes
    tok_count, top_count = routes.shape
    flat = routes.T.reshape(-1)
    token = jnp.arange(tok_count * top_count, dtype=jnp.int32) % tok_count
    earlier = (flat[:, None] == flat[None, :]) & (token[None, :] < token[:, None])
    slot = jnp.sum(earlier.astype(jnp.int32), axis=1)
    ex, ez, ey = flat // (z_size * y_size), flat // y_size % z_size, flat % y_size
    target = ((ez * x_size + ex) * y_size + ey) * capacity + slot
    slots = jnp.arange(x_size * z_size * y_size * capacity, dtype=jnp.int32)
    here = target[None, :] == slots[:, None]
    held = jnp.sum(jnp.where(here, (token + 1).astype(jnp.float32)[None, :], 0.0), axis=1)
    prob = jnp.sum(jnp.where(here, gate_probs.T.reshape(-1)[None, :], 0.0), axis=1)
    high = lax.reduce_precision(prob, 8, 7)
    table = jnp.stack([held, high, prob - high]).reshape(3, z_size, -1)
    return table.transpose(1, 0, 2).astype(jnp.bfloat16)


def hits(table_ref, i, tok_count):
    row_token = table_ref[i, 0:1, :].astype(jnp.float32).astype(jnp.int32) - 1
    lanes = row_token.shape[1]
    return lax.broadcasted_iota(jnp.int32, (tok_count, lanes), 0) == row_token


def pack_kernel(table_ref, tok_ref, _, out_ref):
    plane, sources, capacity, width = out_ref.shape
    for i in range(sources):
        block = tok_ref[i]
        place = jnp.where(hits(table_ref, i, block.shape[0]), 1.0, 0.0).astype(jnp.bfloat16)
        rows = lax.dot_general(
            place, block, (((0,), (0,)), ((), ())), preferred_element_type=jnp.float32
        )
        out_ref[:, i] = rows.astype(jnp.bfloat16).reshape(plane, capacity, width)


def pack(table, tok, after, tok_count, plane, capacity):
    sources, _, width = tok.shape
    return pl.pallas_call(
        pack_kernel,
        grid=(sources // GROUP,),
        in_specs=[
            pl.BlockSpec((GROUP,) + table.shape[1:], lambda i: (i, 0, 0)),
            pl.BlockSpec((GROUP, tok_count, width), lambda i: (i, 0, 0)),
            pl.BlockSpec(after.shape, lambda i: (0, 0)),
        ],
        out_specs=pl.BlockSpec((plane, GROUP, capacity, width), lambda i: (0, i, 0, 0)),
        out_shape=jax.ShapeDtypeStruct((plane, sources, capacity, width), tok.dtype),
        name="pack",
    )(table, tok, after)


def mix_kernel(table_ref, rows_ref, out_ref):
    plane, sources, capacity, width = rows_ref.shape
    tok_count = out_ref.shape[1]
    for i in range(sources):
        here = hits(table_ref, i, tok_count)
        both = [
            jnp.where(here, table_ref[i, r : r + 1, :].astype(jnp.float32), 0.0) for r in (1, 2)
        ]
        both = jnp.concatenate(both, axis=0).astype(jnp.bfloat16)
        rows = rows_ref[:, i].reshape(plane * capacity, width)
        sums = jnp.dot(both, rows, preferred_element_type=jnp.float32)
        out_ref[i] = (sums[:tok_count] + sums[tok_count:]).astype(out_ref.dtype)


def mix(table, rows, tok_count):
    plane, sources, capacity, width = rows.shape
    return pl.pallas_call(
        mix_kernel,
        grid=(sources // GROUP,),
        in_specs=[
            pl.BlockSpec((GROUP,) + table.shape[1:], lambda i: (i, 0, 0)),
            pl.BlockSpec((plane, GROUP, capacity, width), lambda i: (0, i, 0, 0)),
        ],
        out_specs=pl.BlockSpec((GROUP, tok_count, width), lambda i: (i, 0, 0)),
        out_shape=jax.ShapeDtypeStruct((sources, tok_count, width), jnp.bfloat16),
        name="mix",
    )(table, rows)


def hidden_kernel(first_ref, second_ref, gate_ref, up_ref, out_ref, gate_acc, up_acc, *, split):
    step, steps = pl.program_id(0), pl.num_programs(0)

    def products(rows_ref):
        return dot(rows_ref[...], gate_ref[...]), dot(rows_ref[...], up_ref[...])

    @pl.when(step == 0)
    def _():
        gate_acc[...], up_acc[...] = products(first_ref)

    @pl.when((step > 0) & (step < split))
    def _():
        gate, up = products(first_ref)
        gate_acc[...] += gate
        up_acc[...] += up

    @pl.when((step >= split) & (step < steps - 1))
    def _():
        gate, up = products(second_ref)
        gate_acc[...] += gate
        up_acc[...] += up

    @pl.when(step == steps - 1)
    def _():
        gate, up = products(second_ref)
        out_ref[...] = (jax.nn.silu(gate_acc[...] + gate) * (up_acc[...] + up)).astype(out_ref.dtype)


def hidden_of(first, second, w_gate, w_up):
    count = first.shape[0]
    depth, units = w_gate.shape
    split = first.shape[1] // DEPTH
    weight = pl.BlockSpec((DEPTH, units), lambda i: (i, 0))
    return pl.pallas_call(
        functools.partial(hidden_kernel, split=split),
        grid=(depth // DEPTH,),
        in_specs=[
            pl.BlockSpec((count, DEPTH), lambda i: (0, jnp.minimum(i, split - 1))),
            pl.BlockSpec((count, DEPTH), lambda i: (0, jnp.maximum(i - split, 0))),
            weight,
            weight,
        ],
        out_specs=pl.BlockSpec((count, units), lambda i: (0, 0)),
        out_shape=jax.ShapeDtypeStruct((count, units), jnp.bfloat16),
        scratch_shapes=[pltpu.VMEM((count, units), jnp.float32)] * 2,
        compiler_params=pltpu.CompilerParams(vmem_limit_bytes=56 << 20),
        name="hidden",
    )(first, second, w_gate, w_up)


def cuts(widths):
    ends = np.cumsum(widths)
    return [slice(int(end) - width, int(end)) for width, end in zip(widths, ends, strict=True)]


def dot(a, b):
    return jnp.dot(a, b, preferred_element_type=jnp.float32)


def body(tokens, routes, gate_probs, gate_w, up_w, down_w):
    sizes = tuple(lax.axis_size(a) for a in ("x", "z", "y"))
    x_size, z_size, y_size = sizes
    plane = x_size * y_size
    tok_count, model_width = tokens.shape
    capacity = 2 * tok_count * routes.shape[1] // (plane * z_size)
    rows_here = plane * z_size * capacity
    my_z = lax.axis_index("z")

    def in_plane(rows):
        width = rows.shape[-1]
        rows = rows.reshape(plane, z_size * capacity, width)
        rows = lax.all_to_all(rows, ("x", "y"), split_axis=0, concat_axis=0, tiled=True)
        return rows.reshape(plane, z_size, capacity, width)

    into, back = cuts(ARRIVE), cuts(LEAVE)
    table = slot_table(routes, gate_probs, sizes, capacity).reshape(z_size, -1)
    table = jnp.pad(table, ((0, 0), (0, ARRIVE[0] - table.shape[1])))
    sent = [jnp.concatenate([tokens[:, into[0]], table], axis=0), tokens[:, into[1]]]
    gathered = [lax.all_gather(part, "z", axis=0, tiled=False) for part in sent]

    swap = [(0, 1), (1, 0)]

    def whole(w, axis):
        return jnp.concatenate([w, lax.ppermute(w, "dp", swap)], axis=axis)

    w_gate, w_up, w_down = whole(gate_w[0], 1), whole(up_w[0], 1), whole(down_w[0], 0)

    first, second = gathered
    w_gate, w_up, w_down, first = lax.optimization_barrier((w_gate, w_up, w_down, first))
    table = lax.dynamic_index_in_dim(first, tok_count + my_z, 1, keepdims=False)
    table = table[:, : 3 * plane * capacity].reshape(z_size, 3, plane * capacity)
    arrived, after = [], jnp.zeros((8, 128), tokens.dtype)
    for block in (first, second):
        rows = in_plane(pack(table, block, after, tok_count, plane, capacity))
        arrived.append(rows.reshape(rows_here, -1))
        after = arrived[-1][:8, :128] + 1
    hidden = hidden_of(*arrived, w_gate, w_up)

    outs = []
    for part in back:
        answers = dot(hidden, w_down[:, part]).astype(jnp.bfloat16)
        rows = in_plane(answers.reshape(plane, z_size, capacity, -1))
        partial = mix(table, rows, tok_count)
        partial, hidden = lax.optimization_barrier((partial, hidden))
        outs.append(lax.psum_scatter(partial, "z", scatter_dimension=0, tiled=True)[0])
    return jnp.concatenate(outs, axis=1)


def solution(mesh):
    experts, dp = mesh.shape["expert"], mesh.shape["dp"]
    x_size = y_size = 4
    z_size = experts // (x_size * y_size)
    grid = Mesh(mesh.devices.reshape(x_size, z_size, y_size, dp), ("x", "z", "y", "dp"))
    every, owner = ("x", "z", "y", "dp"), ("x", "z", "y")
    return jax.shard_map(
        body,
        mesh=grid,
        in_specs=(
            P(every, None),
            P(every, None),
            P(every, None),
            P(owner, None, "dp"),
            P(owner, None, "dp"),
            P(owner, "dp", None),
        ),
        out_specs=P(every, None),
        check_vma=False,
    )
```

time: 380 us -> 351 us (0.924)
  matrix products: 36 us -> 10.6 us
  blocking collectives: 189 us -> 200 us
  waiting for transfers between devices: 75.2 us -> 65.3 us
  starting transfers between devices: 9.88 us -> 0.83 us
    ppermute x7 -> x0, waiting for transfers between devices: 28.8 us -> none  [body(): lax.ppermute(mine, 'z', [(i, (i + d) % z_size) for i in range(z_size)])]
    all_gather x2, waiting for transfers between devices: 0.01 us -> 25.5 us  [body(): gathered = [lax.all_gather(part, 'z', axis=0, tiled=False) for part in sent]]
    dot_general x6 -> x2, matrix products: 36 us -> 10.6 us  [dot(): return jnp.dot(a, b, preferred_element_type=jnp.float32)]
    all_to_all x4, blocking collectives: 189 us -> 200 us  [in_plane(): lax.all_to_all(rows, ('x', 'y'), split_axis=0, concat_axis=0, tiled=True)]
    ppermute x7 -> x0, starting transfers between devices: 9.07 us -> none  [body(): lax.ppermute(mine, 'z', [(i, (i + d) % z_size) for i in range(z_size)])]
    reduce_scatter x2, waiting for transfers between devices: 46.4 us -> 39.7 us  [body(): lax.psum_scatter(partial, 'z', scatter_dimension=0, tiled=True)[0]]
    pallas_call x4 -> x5, Pallas kernels: 31.5 us -> 35 us  [the longest x1 18.2 us: hidden_of(): pl.pallas_call(functools.partial(hidden_kernel, split=split), grid=(depth...]
  transfers between devices with their start and end apart: 14 -> 7, of which waited for: 7 -> 2; matrix products, arithmetic and copies ran while one was open for 10% -> 9% of each run, Pallas kernels for 4% -> 2%
where the time goes in v4:
time: 351 us
  blocking collectives  200 us (57%)
  waiting for transfers between devices  65.3 us (19%)
  Pallas kernels  35 us (10%)
  other arithmetic  19.9 us (6%)
  between operations  13.3 us (4%)
  matrix products  10.6 us (3%)
  local copies, waits for them, and re-layouts  6.39 us (2%)
    all_to_all x4, blocking collectives, in_plane(): lax.all_to_all(rows, ('x', 'y'), split_axis=0, concat_axis=0, tiled=True)  200 us
    reduce_scatter x2, waiting for transfers between devices, body(): lax.psum_scatter(partial, 'z', scatter_dimension=0, tiled=True)[0]  39.7 us
    all_gather x2, waiting for transfers between devices, body(): gathered = [lax.all_gather(part, 'z', axis=0, tiled=False) for part in sent]  25.5 us
    pallas_call x1, Pallas kernels, hidden_of(): pl.pallas_call(functools.partial(hidden_kernel, split=split), grid=(depth...  18.2 us
    concatenate x3, other arithmetic, whole(): return jnp.concatenate([w, lax.ppermute(w, 'dp', swap)], axis=axis)  15.7 us
    dot_general x2, matrix products, dot(): return jnp.dot(a, b, preferred_element_type=jnp.float32)  10.6 us
    pallas_call x2, Pallas kernels, pack(): pl.pallas_call(pack_kernel, grid=(sources // GROUP,), in_specs=[pl.BlockS...  8.65 us
    pallas_call x2, Pallas kernels, mix(): pl.pallas_call(mix_kernel, grid=(sources // GROUP,), in_specs=[pl.BlockSp...  8.13 us
  transfers between devices with their start and end apart: 7, of which 2 were waited for; matrix products, arithmetic and copies ran while one was open for 9% of the time, Pallas kernels for 2%

profile of v4, /device:TPU:2, one launch (start us, length us, event | category | flops | bytes accessed | tf_op | source)
XLA Modules:
  0.0 350.9 jit_solution(10145556842875408130)
XLA Ops:
  6.5 0.0 all-gather.5.cloned.1.call-start
  6.5 0.0 collective-permute-start
  6.5 0.8 reshape.154
  7.3 0.8 broadcast_in_dim.30
  8.1 0.3 convert_reduce_fusion
  8.4 0.6 select_reduce_fusion.1
  9.1 0.9 slice.18
  10.1 0.7 fusion.3
  10.8 0.0 all-gather.5.cloned.1.call-update
  10.8 0.0 all-gather.7.cloned.1.call-start
  10.8 0.6 collective-permute-start.1
  11.4 0.1 collective-permute-start.2
  11.5 1.7 slice.20
  13.3 0.0 all-gather.7.cloned.1.call-update
  13.3 0.0 reduce-scatter.3.cloned.1.call-start
  13.3 0.0 copy-start.1
  13.4 0.0 collective-permute-done
  13.4 5.2 %pad_maximum_fusion.gate_ref = bf16[4096,768]{1,0:T(8,128)(2,1)} fusion(bf16[4096,384]{1,0:T(8,128)(2,1)S(1)} %collective-permute-done, bf16[4096,384]{1,0:T(8,128)(2,1)} %bitcast.46), kind=kLoop, calls=%fused_computation | loop fusion | flops 12582912 | bytes 12582912 | tf_op jit(solution)/shard_map/concatenate | solution.py:181
  18.6 0.0 collective-permute-done.1
  18.6 0.0 copy-done.1
  18.6 5.1 %pad_maximum_fusion.1.up_ref = bf16[4096,768]{1,0:T(8,128)(2,1)} fusion(bf16[4096,384]{1,0:T(8,128)(2,1)} %collective-permute-done.1, bf16[4096,384]{1,0:T(8,128)(2,1)S(1)} %bitcast.48), kind=kLoop, calls=%fused_computation.1 | loop fusion | flops 12582912 | bytes 12582912 | tf_op jit(solution)/shard_map/concatenate | solution.py:181
  23.7 0.0 collective-permute-done.2
  23.7 0.0 copy-done.2
  23.7 5.4 %pad_maximum_fusion.2 = bf16[768,4096]{1,0:T(8,128)(2,1)} fusion(bf16[384,4096]{1,0:T(8,128)(2,1)} %collective-permute-done.2, bf16[384,4096]{1,0:T(8,128)(2,1)S(1)} %bitcast.50), kind=kLoop, calls=%fused_computation.2 | loop fusion | flops 12582912 | bytes 12582912 | tf_op jit(solution)/shard_map/concatenate | solution.py:181
  29.1 25.5 %all-gather.5.cloned.1.call-done = bf16[576,1536]{1,0:T(8,128)(2,1)} async-done(((bf16[72,1536]{1,0:T(8,128)(2,1)}), bf16[576,1536]{1,0:T(8,128)(2,1)}) %all-gather.5.cloned.1.call-update) | async-done | bytes 1769488 | tf_op jit(solution)/shard_map/all_gather | solution.py:176
  54.6 1.0 constant_dynamic-slice_fusion
  55.6 0.6 copy.13.table_ref
  56.2 0.6 broadcast_in_dim.32._
  56.8 3.5 %pack.2 = bf16[16,8,8,1536]{3,2,1,0:T(8,128)(2,1)} custom-call(bf16[8,3,128]{2,1,0:T(4,128)(2,1)} %copy.13.table_ref, bf16[8,72,1536]{2,1,0:T(8,128)(2,1)} %bitcast.53, bf16[8,128]{1,0:T(8,128)(2,1)} %broadcast_in_dim.32._), custom_call_target="tpu_custom_call" | custom-call | tf_op jit(solution)/shard_map/pack/pallas_call | solution.py:55
  60.3 40.9 %all_to_all.20 = bf16[16,64,1536]{2,1,0:T(8,128)(2,1)S(1)} all-to-all(bf16[16,64,1536]{2,1,0:T(8,128)(2,1)} %bitcast.40), channel_id=1, replica_groups=mesh['x'=4,'z'=8,'y'=4,'dp'=2] {'x','y'}, dimensions={0} | all-to-all | bytes 6291456 | tf_op jit(solution)/shard_map/all_to_all | solution.py:169
  101.2 0.7 slice_add_fusion._
  101.9 5.1 %pack.3 = bf16[16,8,8,2560]{3,2,1,0:T(8,128)(2,1)} custom-call(bf16[8,3,128]{2,1,0:T(4,128)(2,1)} %copy.13.table_ref, bf16[8,64,2560]{2,1,0:T(8,128)(2,1)} %bitcast.51, bf16[8,128]{1,0:T(8,128)(2,1)} %slice_add_fusion._), custom_call_target="tpu_custom_call" | custom-call | tf_op jit(solution)/shard_map/pack/pallas_call | solution.py:55
  107.0 0.0 copy-done
  107.0 61.7 %all_to_all.21 = bf16[16,64,2560]{2,1,0:T(8,128)(2,1)} all-to-all(bf16[16,64,2560]{2,1,0:T(8,128)(2,1)} %bitcast.34), channel_id=1, replica_groups=mesh['x'=4,'z'=8,'y'=4,'dp'=2] {'x','y'}, dimensions={0} | all-to-all | bytes 10485760 | tf_op jit(solution)/shard_map/all_to_all | solution.py:169
  168.7 18.2 %hidden.1 = bf16[1024,768]{1,0:T(8,128)(2,1)} custom-call(bf16[1024,1536]{1,0:T(8,128)(2,1)} %bitcast.39, bf16[1024,2560]{1,0:T(8,128)(2,1)} %bitcast.35, bf16[4096,768]{1,0:T(8,128)(2,1)} %pad_maximum_fusion.gate_ref, bf16[4096,768]{1,0:T(8,128)(2,1)} %pad_maximum_fusion.1.up_ref), custom_call_target="tpu_custom_call" | custom-call | tf_op jit(solution)/shard_map/hidden/pallas_call | solution.py:131
  186.9 0.0 slice-done
  186.9 5.0 %convolution_convert_fusion.1 = bf16[1024,2048]{1,0:T(8,128)(2,1)S(1)} fusion(bf16[1024,768]{1,0:T(8,128)(2,1)} %hidden.1, bf16[768,4096]{1,0:T(8,128)(2,1)S(1)} %bitcast.42), kind=kOutput, calls=%fused_computation.4 | convolution fusion | flops 3223322624 | bytes 8912896 | tf_op jit(solution)/shard_map/dot_general | solution.py:154
  192.0 48.1 %all_to_all.22 = bf16[16,64,2048]{2,1,0:T(8,128)(2,1)} all-to-all(bf16[16,64,2048]{2,1,0:T(8,128)(2,1)S(1)} %bitcast.44), channel_id=1, replica_groups=mesh['x'=4,'z'=8,'y'=4,'dp'=2] {'x','y'}, dimensions={0} | all-to-all | bytes 8388608 | tf_op jit(solution)/shard_map/all_to_all | solution.py:169
  240.1 4.1 %mix.2 = bf16[8,64,2048]{2,1,0:T(8,128)(2,1)} custom-call(bf16[8,3,128]{2,1,0:T(4,128)(2,1)} %copy.13.table_ref, bf16[16,8,8,2048]{3,2,1,0:T(8,128)(2,1)} %bitcast.37), custom_call_target="tpu_custom_call" | custom-call | tf_op jit(solution)/shard_map/mix/pallas_call | solution.py:85
  244.2 0.0 reduce-scatter.3.cloned.1.call-update
  244.2 0.0 reduce-scatter.5.cloned.1.call-start
  244.3 5.5 %convolution_convert_fusion = bf16[1024,2048]{1,0:T(8,128)(2,1)S(1)} fusion(bf16[1024,768]{1,0:T(8,128)(2,1)S(1)} %copy-done.3, bf16[768,4096]{1,0:T(8,128)(2,1)} %pad_maximum_fusion.2), kind=kOutput, calls=%fused_computation.3 | convolution fusion | flops 3223322624 | bytes 8912896 | tf_op jit(solution)/shard_map/dot_general | solution.py:154
  249.8 49.0 %all_to_all.23 = bf16[16,64,2048]{2,1,0:T(8,128)(2,1)} all-to-all(bf16[16,64,2048]{2,1,0:T(8,128)(2,1)S(1)} %bitcast.43), channel_id=1, replica_groups=mesh['x'=4,'z'=8,'y'=4,'dp'=2] {'x','y'}, dimensions={0} | all-to-all | bytes 8388608 | tf_op jit(solution)/shard_map/all_to_all | solution.py:169
  298.8 4.0 %mix.3 = bf16[8,64,2048]{2,1,0:T(8,128)(2,1)} custom-call(bf16[8,3,128]{2,1,0:T(4,128)(2,1)} %copy.13.table_ref, bf16[16,8,8,2048]{3,2,1,0:T(8,128)(2,1)} %bitcast.36), custom_call_target="tpu_custom_call" | custom-call | tf_op jit(solution)/shard_map/mix/pallas_call | solution.py:85
  302.8 0.0 reduce-scatter.5.cloned.1.call-update
  302.8 0.0 reduce-scatter.3.cloned.1.call-done
  302.9 39.7 %reduce-scatter.5.cloned.1.call-done = bf16[1,64,2048]{2,1,0:T(8,128)(2,1)} async-done(((bf16[8,64,2048]{2,1,0:T(8,128)(2,1)}), bf16[1,64,2048]{2,1,0:T(8,128)(2,1)}) %reduce-scatter.5.cloned.1.call-update) | async-done | bytes 262160 | tf_op jit(solution)/shard_map/reduce_scatter | solution.py:202
  342.5 1.9 pad_maximum_fusion.3
  (15 shorter events, 0.1 us)
Async XLA Ops:
  6.5 48.0 %all-gather.5.cloned.1.call-start = ((), (), s32[]{:S(2)}) async-start(), calls=%async_computation.8 | async-start | bytes 1990656 | tf_op jit(solution)/shard_map/all_gather | solution.py:176
  6.5 6.8 %collective-permute-start = (bf16[4096,384]{1,0:T(8,128)(2,1)}, bf16[4096,384]{1,0:T(8,128)(2,1)S(1)}, u32[]{:S(2)}, u32[]{:S(2)}) collective-permute-start(bf16[4096,384]{1,0:T(8,128)(2,1)} %bitcast.45), channel_id=1, source_target_pairs={{0,1},{1,0},{2,3},{3,2},{4,5},{5,4},{6,7},{7,6},{8,9},{9,8},{10,11... | collective-permute-start | bytes 9437192 | tf_op jit(solution)/shard_map/ppermute | solution.py:181
  10.8 91.1 %all-gather.7.cloned.1.call-start = ((), (), s32[]{:S(2)}) async-start(), calls=%async_computation.9 | async-start | bytes 2949120 | tf_op jit(solution)/shard_map/all_gather | solution.py:176
  10.8 7.7 %collective-permute-start.1 = (bf16[4096,384]{1,0:T(8,128)(2,1)}, bf16[4096,384]{1,0:T(8,128)(2,1)}, u32[]{:S(2)}, u32[]{:S(2)}) collective-permute-start(bf16[4096,384]{1,0:T(8,128)(2,1)} %bitcast.47), channel_id=1, source_target_pairs={{0,1},{1,0},{2,3},{3,2},{4,5},{5,4},{6,7},{7,6},{8,9},{9,8},{10,11... | collective-permute-start | bytes 9437192 | tf_op jit(solution)/shard_map/ppermute | solution.py:181
  11.4 12.3 %collective-permute-start.2 = (bf16[384,4096]{1,0:T(8,128)(2,1)}, bf16[384,4096]{1,0:T(8,128)(2,1)}, u32[]{:S(2)}, u32[]{:S(2)}) collective-permute-start(bf16[384,4096]{1,0:T(8,128)(2,1)} %bitcast.49), channel_id=1, source_target_pairs={{0,1},{1,0},{2,3},{3,2},{4,5},{5,4},{6,7},{7,6},{8,9},{9,8},{10,11... | collective-permute-start | bytes 9437192 | tf_op jit(solution)/shard_map/ppermute | solution.py:181
  13.3 289.6 %reduce-scatter.3.cloned.1.call-start = ((), (), s32[]{:S(2)}) async-start(), calls=%async_computation.6 | async-start | bytes 2359296 | tf_op jit(solution)/shard_map/reduce_scatter | solution.py:202
  13.3 5.2 %copy-start.1 = (bf16[1,4096,384]{2,1,0:T(8,128)(2,1)S(1)}, bf16[1,4096,384]{2,1,0:T(8,128)(2,1)}, u32[]{:S(2)}) copy-start(bf16[1,4096,384]{2,1,0:T(8,128)(2,1)} %param.10) | copy-start | bytes 9437188
  18.6 5.1 %copy-start.2 = (bf16[1,384,4096]{2,1,0:T(8,128)(2,1)S(1)}, bf16[1,384,4096]{2,1,0:T(8,128)(2,1)}, u32[]{:S(2)}) copy-start(bf16[1,384,4096]{2,1,0:T(8,128)(2,1)} %param.11) | copy-start | bytes 9437188
  101.2 5.8 %copy-start = (bf16[16,64,1536]{2,1,0:T(8,128)(2,1)}, bf16[16,64,1536]{2,1,0:T(8,128)(2,1)S(1)}, u32[]{:S(2)}) copy-start(bf16[16,64,1536]{2,1,0:T(8,128)(2,1)S(1)} %all_to_all.20) | copy-start | bytes 9437188
  107.0 79.9 %slice-start = ((s8[6291456]{0:T(1024)(128)(4,1)}), s8[4194304]{0:T(1024)(128)(4,1)S(1)}, s32[]{:S(2)}) async-start(s8[6291456]{0:T(1024)(128)(4,1)} %bitcast.41), calls=%async_computation.10 | async-start | bytes 8388608
  168.7 18.2 %slice-start.1 = ((s8[6291456]{0:T(1024)(128)(4,1)}), s8[2097152]{0:T(1024)(128)(4,1)S(1)}, s32[]{:S(2)}) async-start(s8[6291456]{0:T(1024)(128)(4,1)} %bitcast.41), calls=%async_computation.11 | async-start | bytes 4194304
  240.1 4.2 %copy-start.3 = (bf16[1024,768]{1,0:T(8,128)(2,1)S(1)}, bf16[1024,768]{1,0:T(8,128)(2,1)}, u32[]{:S(2)}) copy-start(bf16[1024,768]{1,0:T(8,128)(2,1)} %hidden.1) | copy-start | bytes 4718596
  244.2 98.3 %reduce-scatter.5.cloned.1.call-start = ((), (), s32[]{:S(2)}) async-start(), calls=%async_computation.7 | async-start | bytes 2359296 | tf_op jit(solution)/shard_map/reduce_scatter | solution.py:202
Sparse Core Ops, SparseCore 0:
  10.9 43.5 all-gather.4
  56.3 40.8 all-gather.6
  244.4 40.6 reduce-scatter.2
  302.9 39.5 reduce-scatter.4

commit v5 on v4

v5 whole, which is shorter than its diff:
```python
import functools

import jax
import jax.numpy as jnp
import numpy as np
from jax import lax
from jax.experimental import pallas as pl
from jax.experimental.pallas import tpu as pltpu
from jax.sharding import Mesh
from jax.sharding import PartitionSpec as P

DEPTH = 1024
ARRIVE = (1024, 3072)
LEAVE = (3328, 768)


def slot_table(routes, gate_probs, sizes, capacity):
    x_size, z_size, y_size = sizes
    tok_count, top_count = routes.shape
    flat = routes.T.reshape(-1)
    token = jnp.arange(tok_count * top_count, dtype=jnp.int32) % tok_count
    earlier = (flat[:, None] == flat[None, :]) & (token[None, :] < token[:, None])
    slot = jnp.sum(earlier.astype(jnp.int32), axis=1)
    ex, ez, ey = flat // (z_size * y_size), flat // y_size % z_size, flat % y_size
    target = ((ez * x_size + ex) * y_size + ey) * capacity + slot
    slots = jnp.arange(x_size * z_size * y_size * capacity, dtype=jnp.int32)
    here = target[None, :] == slots[:, None]
    held = jnp.sum(jnp.where(here, (token + 1).astype(jnp.float32)[None, :], 0.0), axis=1)
    prob = jnp.sum(jnp.where(here, gate_probs.T.reshape(-1)[None, :], 0.0), axis=1)
    high = lax.reduce_precision(prob, 8, 7)
    table = jnp.stack([held, high, prob - high]).reshape(3, z_size, -1)
    return table.transpose(1, 0, 2).astype(jnp.bfloat16)


def hits(row_token, tok_count):
    tokens = lax.broadcasted_iota(jnp.int32, (tok_count, row_token.shape[1]), 0)
    return tokens == row_token.astype(jnp.int32) - 1


def place_rows(here, block):
    place = jnp.where(here, 1.0, 0.0).astype(jnp.bfloat16)
    rows = lax.dot_general(
        place, block, (((0,), (0,)), ((), ())), preferred_element_type=jnp.float32
    )
    return rows.astype(jnp.bfloat16)


def pack_ring_kernel(me_ref, *refs):
    *blocks, far_first, far_second, out_ref, table_ref = refs
    plane, sources, capacity, width = out_ref.shape
    lanes = plane * capacity
    tok_count = far_second.shape[0]
    for i in range(sources):
        ref = blocks[i] if i < len(blocks) else far_first
        lists = ref[tok_count:, : 3 * lanes].astype(jnp.float32)
        mine = lax.broadcasted_iota(jnp.int32, lists.shape, 0) == me_ref[0]
        lists = jnp.sum(jnp.where(mine, lists, 0.0), axis=0, keepdims=True)
        for r in range(3):
            table_ref[i, r : r + 1, :] = lists[:, r * lanes : (r + 1) * lanes]
        here = hits(lists[:, :lanes], tok_count)
        if i < len(blocks):
            rows = place_rows(here, ref[:tok_count, :])
            out_ref[:, i] = rows.reshape(plane, capacity, width)
        else:
            half = width // 2
            rows = place_rows(here, far_first[:tok_count, :])
            out_ref[:, i, :, :half] = rows.reshape(plane, capacity, half)
            rows = place_rows(here, far_second[...])
            out_ref[:, i, :, half:] = rows.reshape(plane, capacity, half)


def pack_ring(me, blocks, tok_count, plane, capacity):
    sources, width = len(blocks) - 1, blocks[0].shape[1]
    whole = [pl.BlockSpec(b.shape, lambda i, me: (0, 0)) for b in blocks]
    shapes = [(plane, sources, capacity, width), (sources, 3, plane * capacity)]
    return pl.pallas_call(
        pack_ring_kernel,
        grid_spec=pltpu.PrefetchScalarGridSpec(
            num_scalar_prefetch=1,
            grid=(1,),
            in_specs=whole,
            out_specs=[
                pl.BlockSpec(shapes[0], lambda i, me: (0, 0, 0, 0)),
                pl.BlockSpec(shapes[1], lambda i, me: (0, 0, 0)),
            ],
        ),
        out_shape=[
            jax.ShapeDtypeStruct(shapes[0], jnp.bfloat16),
            jax.ShapeDtypeStruct(shapes[1], jnp.float32),
        ],
        name="pack_ring",
    )(me, *blocks)


def pack_kernel(order_ref, table_ref, tok_ref, _, out_ref):
    plane, sources, capacity, width = out_ref.shape
    for i in range(sources):
        here = hits(table_ref[i, 0:1, :], tok_ref.shape[1])
        rows = place_rows(here, tok_ref[order_ref[i]])
        out_ref[:, i] = rows.reshape(plane, capacity, width)


def pack(order, table, tok, after, plane, capacity, step):
    sources, tok_count, width = tok.shape
    return pl.pallas_call(
        pack_kernel,
        grid_spec=pltpu.PrefetchScalarGridSpec(
            num_scalar_prefetch=1,
            grid=(width // step,),
            in_specs=[
                pl.BlockSpec(table.shape, lambda i, order: (0, 0, 0)),
                pl.BlockSpec((sources, tok_count, step), lambda i, order: (0, 0, i)),
                pl.BlockSpec(after.shape, lambda i, order: (0, 0)),
            ],
            out_specs=pl.BlockSpec((plane, sources, capacity, step), lambda i, order: (0, 0, 0, i)),
        ),
        out_shape=jax.ShapeDtypeStruct((plane, sources, capacity, width), tok.dtype),
        name="pack",
    )(order, table, tok, after)


def mix_kernel(order_ref, table_ref, rows_ref, out_ref):
    plane, sources, capacity, width = rows_ref.shape
    tok_count = out_ref.shape[1]
    for i in range(sources):
        here = hits(table_ref[i, 0:1, :], tok_count)
        both = [jnp.where(here, table_ref[i, r : r + 1, :], 0.0) for r in (1, 2)]
        both = jnp.concatenate(both, axis=0).astype(jnp.bfloat16)
        rows = rows_ref[:, i].reshape(plane * capacity, width)
        sums = jnp.dot(both, rows, preferred_element_type=jnp.float32)
        out_ref[order_ref[i]] = (sums[:tok_count] + sums[tok_count:]).astype(out_ref.dtype)


def mix(order, table, rows, tok_count, step):
    plane, sources, capacity, width = rows.shape
    return pl.pallas_call(
        mix_kernel,
        grid_spec=pltpu.PrefetchScalarGridSpec(
            num_scalar_prefetch=1,
            grid=(width // step,),
            in_specs=[
                pl.BlockSpec(table.shape, lambda i, order: (0, 0, 0)),
                pl.BlockSpec((plane, sources, capacity, step), lambda i, order: (0, 0, 0, i)),
            ],
            out_specs=pl.BlockSpec((sources, tok_count, step), lambda i, order: (0, 0, i)),
        ),
        out_shape=jax.ShapeDtypeStruct((sources, tok_count, width), jnp.bfloat16),
        name="mix",
    )(order, table, rows)


def hidden_kernel(first_ref, second_ref, *refs, split):
    *weights, out_ref, gate_acc, up_acc = refs
    step, steps = pl.program_id(0), pl.num_programs(0)

    def products(rows_ref):
        gate, gate_other, up, up_other = (ref[...] for ref in weights)
        gate = jnp.concatenate([gate, gate_other], axis=1)
        up = jnp.concatenate([up, up_other], axis=1)
        return dot(rows_ref[...], gate), dot(rows_ref[...], up)

    @pl.when(step == 0)
    def _():
        gate_acc[...], up_acc[...] = products(first_ref)

    if split > 1:

        @pl.when((step > 0) & (step < split))
        def _():
            gate, up = products(first_ref)
            gate_acc[...] += gate
            up_acc[...] += up

    @pl.when((step >= split) & (step < steps - 1))
    def _():
        gate, up = products(second_ref)
        gate_acc[...] += gate
        up_acc[...] += up

    @pl.when(step == steps - 1)
    def _():
        gate, up = products(second_ref)
        out_ref[...] = (jax.nn.silu(gate_acc[...] + gate) * (up_acc[...] + up)).astype(out_ref.dtype)


def hidden_of(first, second, weights):
    count = first.shape[0]
    depth, units = weights[0].shape
    split = first.shape[1] // DEPTH
    weight = pl.BlockSpec((DEPTH, units), lambda i: (i, 0))
    return pl.pallas_call(
        functools.partial(hidden_kernel, split=split),
        grid=(depth // DEPTH,),
        in_specs=[
            pl.BlockSpec((count, DEPTH), lambda i: (0, jnp.minimum(i, split - 1))),
            pl.BlockSpec((count, DEPTH), lambda i: (0, jnp.maximum(i - split, 0))),
            *[weight] * 4,
        ],
        out_specs=pl.BlockSpec((count, 2 * units), lambda i: (0, 0)),
        out_shape=jax.ShapeDtypeStruct((count, 2 * units), jnp.bfloat16),
        scratch_shapes=[pltpu.VMEM((count, 2 * units), jnp.float32)] * 2,
        compiler_params=pltpu.CompilerParams(vmem_limit_bytes=56 << 20),
        name="hidden",
    )(first, second, *weights)


def cuts(widths):
    ends = np.cumsum(widths)
    return [slice(int(end) - width, int(end)) for width, end in zip(widths, ends, strict=True)]


def dot(a, b):
    return jnp.dot(a, b, preferred_element_type=jnp.float32)


def body(tokens, routes, gate_probs, gate_w, up_w, down_w):
    sizes = tuple(lax.axis_size(a) for a in ("x", "z", "y"))
    x_size, z_size, y_size = sizes
    plane = x_size * y_size
    tok_count, model_width = tokens.shape
    capacity = 2 * tok_count * routes.shape[1] // (plane * z_size)
    rows_here = plane * z_size * capacity
    my_z = lax.axis_index("z")

    def in_plane(rows):
        width = rows.shape[-1]
        rows = rows.reshape(plane, z_size * capacity, width)
        rows = lax.all_to_all(rows, ("x", "y"), split_axis=0, concat_axis=0, tiled=True)
        return rows.reshape(plane, z_size, capacity, width)

    into, back = cuts(ARRIVE), cuts(LEAVE)
    up_ring = [(i, (i + 1) % z_size) for i in range(z_size)]
    down_ring = [(i, (i - 1) % z_size) for i in range(z_size)]

    second = lax.all_gather(tokens[:, into[1]], "z", axis=0, tiled=False)

    table = slot_table(routes, gate_probs, sizes, capacity).reshape(z_size, -1)
    table = jnp.pad(table, ((0, 0), (0, ARRIVE[0] - table.shape[1])))
    above = below = jnp.concatenate([tokens[:, into[0]], table], axis=0)
    ring, order = [above], [my_z]
    for hop in range(1, z_size // 2):
        above, below = lax.ppermute(above, "z", up_ring), lax.ppermute(below, "z", down_ring)
        ring += [above, below]
        order += [my_z - hop, my_z + hop]
    half = ARRIVE[0] // 2
    ring.append(lax.ppermute(above[:, :half], "z", up_ring))
    ring.append(lax.ppermute(below[:tok_count, half:], "z", down_ring))
    order = jnp.stack([*order, my_z + z_size // 2]) % z_size

    swap = [(0, 1), (1, 0)]
    weights = [gate_w[0], up_w[0]]
    weights = [v for w in weights for v in (w, lax.ppermute(w, "dp", swap))]
    w_down = jnp.concatenate([down_w[0], lax.ppermute(down_w[0], "dp", swap)], axis=0)

    weights, w_down, ring, order = lax.optimization_barrier((weights, w_down, ring, order))
    rows, table = pack_ring(my_z[None], ring, tok_count, plane, capacity)
    rows = in_plane(rows)
    first = rows.reshape(rows_here, -1)
    after = first[:8, :128] + 1
    rows = in_plane(pack(order, table, second, after, plane, capacity, ARRIVE[1] // 3))
    hidden = hidden_of(first, rows.reshape(rows_here, -1), weights)

    def answered(hidden, part, step):
        answers = dot(hidden, w_down[:, part]).astype(jnp.bfloat16)
        rows = in_plane(answers.reshape(plane, z_size, capacity, -1))
        return mix(order, table, rows, tok_count, step)

    partial = answered(hidden, back[0], LEAVE[0] // 2)
    partial, hidden = lax.optimization_barrier((partial, hidden))
    out_first = lax.psum_scatter(partial, "z", scatter_dimension=0, tiled=True)[0]
    partial = answered(hidden, back[1], LEAVE[1])
    parts = lax.all_to_all(partial, "z", split_axis=0, concat_axis=0, tiled=True)
    out_second = jnp.sum(parts.astype(jnp.float32), axis=0).astype(jnp.bfloat16)
    return jnp.concatenate([out_first, out_second], axis=1)


def solution(mesh):
    experts, dp = mesh.shape["expert"], mesh.shape["dp"]
    x_size = y_size = 4
    z_size = experts // (x_size * y_size)
    grid = Mesh(mesh.devices.reshape(x_size, z_size, y_size, dp), ("x", "z", "y", "dp"))
    every, owner = ("x", "z", "y", "dp"), ("x", "z", "y")
    return jax.shard_map(
        body,
        mesh=grid,
        in_specs=(
            P(every, None),
            P(every, None),
            P(every, None),
            P(owner, None, "dp"),
            P(owner, None, "dp"),
            P(owner, "dp", None),
        ),
        out_specs=P(every, None),
        check_vma=False,
    )
```

time: 351 us -> 353 us (level)
  waiting for transfers between devices: 65.3 us -> 18.6 us
  blocking collectives: 200 us -> 238 us
  starting transfers between devices: 0.83 us -> 17.9 us
  other arithmetic: 19.9 us -> 9.55 us
    reduce_scatter x2 -> x1, waiting for transfers between devices: 39.7 us -> 0.02 us  [body(): lax.psum_scatter(partial, 'z', scatter_dimension=0, tiled=True)[0]]
    all_to_all x0 -> x1, blocking collectives: none -> 35.3 us  [body(): lax.all_to_all(partial, 'z', split_axis=0, concat_axis=0, tiled=True)]
    all_gather x2 -> x1, waiting for transfers between devices: 25.5 us -> 0.01 us  [body(): second = lax.all_gather(tokens[:, into[1]], 'z', axis=0, tiled=False)]
    ppermute x3 -> x11, waiting for transfers between devices: 0.01 us -> 18.6 us  [the longest x3 15.6 us: body(): lax.ppermute(below, 'z', down_ring)]
    ppermute x3 -> x11, starting transfers between devices: 0.7 us -> 17.9 us  [the longest x3 13.4 us: body(): lax.ppermute(below, 'z', down_ring)]
    concatenate x5 -> x3, other arithmetic: 18.2 us -> 7.16 us  [the longest x1 5.31 us: body(): jnp.concatenate([down_w[0], lax.ppermute(down_w[0], 'dp', swap)], axis=0)]
  transfers between devices with their start and end apart: 7 -> 13, of which waited for: 2 -> 6; matrix products, arithmetic and copies ran while one was open for 9% -> 4% of each run, Pallas kernels for 2% -> 2%
where the time goes in v5:
time: 353 us; the launch traced here: 352 us
  blocking collectives  238 us (67%)
  Pallas kernels  38 us (11%)
  waiting for transfers between devices  18.6 us (5%)
  starting transfers between devices  17.9 us (5%)
  between operations  13.6 us (4%)
  matrix products  10.2 us (3%)
  other arithmetic  9.55 us (3%)
  local copies, waits for them, and re-layouts  6.32 us (2%)
    all_to_all x4, blocking collectives, in_plane(): lax.all_to_all(rows, ('x', 'y'), split_axis=0, concat_axis=0, tiled=True)  202 us
    all_to_all x1, blocking collectives, body(): lax.all_to_all(partial, 'z', split_axis=0, concat_axis=0, tiled=True)  35.3 us
    pallas_call x1, Pallas kernels, hidden_of(): pl.pallas_call(functools.partial(hidden_kernel, split=split), grid=(depth...  18.3 us
    ppermute x3, waiting for transfers between devices, body(): lax.ppermute(below, 'z', down_ring)  15.6 us
    ppermute x3, starting transfers between devices, body(): lax.ppermute(below, 'z', down_ring)  13.4 us
    dot_general x2, matrix products, dot(): return jnp.dot(a, b, preferred_element_type=jnp.float32)  10.2 us
    pallas_call x2, Pallas kernels, mix(): pl.pallas_call(mix_kernel, grid_spec=pltpu.PrefetchScalarGridSpec(num_sca...  9.49 us
  transfers between devices with their start and end apart: 13, of which 6 were waited for; matrix products, arithmetic and copies ran while one was open for 4% of the time, Pallas kernels for 2%

profile of v5, /device:TPU:2, one launch (start us, length us, event | category | flops | bytes accessed | tf_op | source)
XLA Modules:
  0.0 351.8 jit_solution(11460464462097149976)
XLA Ops:
  6.5 0.0 collective-permute-start.2
  6.5 1.8 slice.24
  8.3 0.0 all-gather.3.cloned.1.call-update
  8.3 0.0 reduce-scatter.2.cloned.1.call-start
  8.4 0.6 collective-permute-start
  9.0 0.1 collective-permute-start.1
  9.1 0.9 slice.21
  10.0 0.8 reshape.151
  10.8 0.8 broadcast_in_dim.28
  11.5 0.3 convert_reduce_fusion
  11.9 0.6 select_reduce_fusion.1
  12.6 5.9 %collective-permute-start.4 = (bf16[72,1024]{1,0:T(8,128)(2,1)S(1)}, bf16[72,1024]{1,0:T(8,128)(2,1)S(1)}, u32[]{:S(2)}, u32[]{:S(2)}) collective-permute-start(bf16[72,1024]{1,0:T(8,128)(2,1)S(1)} %fusion.3.refs_0_), channel_id=1, source_target_pairs={{0,56},{8,0},{16,8},{24,16},{32,24},{40,32},{48,40},{56,48},{1,57}... | collective-permute-start | bytes 442376 | tf_op jit(solution)/shard_map/ppermute | solution.py:242
  18.5 0.0 collective-permute-start.3
  18.5 3.7 %collective-permute-done.4.refs_2_ = bf16[72,1024]{1,0:T(8,128)(2,1)S(1)} collective-permute-done((bf16[72,1024]{1,0:T(8,128)(2,1)S(1)}, bf16[72,1024]{1,0:T(8,128)(2,1)S(1)}, u32[]{:S(2)}, u32[]{:S(2)}) %collective-permute-start.4) | collective-permute-done | bytes 147488 | tf_op jit(solution)/shard_map/ppermute | solution.py:242
  22.2 3.7 %collective-permute-start.6 = (bf16[72,1024]{1,0:T(8,128)(2,1)S(1)}, bf16[72,1024]{1,0:T(8,128)(2,1)}, u32[]{:S(2)}, u32[]{:S(2)}) collective-permute-start(bf16[72,1024]{1,0:T(8,128)(2,1)S(1)} %collective-permute-done.4.refs_2_), channel_id=1, source_target_pairs={{0,56},{8,0},{16,8},{24,16},{32,24},{40,32},{48,40},{56,48},{1,57}... | collective-permute-start | bytes 442376 | tf_op jit(solution)/shard_map/ppermute | solution.py:242
  25.9 0.1 stack.45
  26.0 6.6 %collective-permute-done.6.refs_4_ = bf16[72,1024]{1,0:T(8,128)(2,1)} collective-permute-done((bf16[72,1024]{1,0:T(8,128)(2,1)S(1)}, bf16[72,1024]{1,0:T(8,128)(2,1)}, u32[]{:S(2)}, u32[]{:S(2)}) %collective-permute-start.6) | collective-permute-done | bytes 147488 | tf_op jit(solution)/shard_map/ppermute | solution.py:242
  32.7 3.8 %collective-permute-start.8 = (bf16[72,1024]{1,0:T(8,128)(2,1)}, bf16[72,1024]{1,0:T(8,128)(2,1)S(1)}, u32[]{:S(2)}, u32[]{:S(2)}) collective-permute-start(bf16[72,1024]{1,0:T(8,128)(2,1)} %collective-permute-done.6.refs_4_), channel_id=1, source_target_pairs={{0,56},{8,0},{16,8},{24,16},{32,24},{40,32},{48,40},{56,48},{1,57}... | collective-permute-start | bytes 442376 | tf_op jit(solution)/shard_map/ppermute | solution.py:242
  36.5 0.3 collective-permute-done.5.refs_3_
  36.8 0.0 collective-permute-start.7
  36.8 0.6 and_select_fusion.order_ref
  37.4 5.2 %collective-permute-done.8.refs_6_ = bf16[72,1024]{1,0:T(8,128)(2,1)S(1)} collective-permute-done((bf16[72,1024]{1,0:T(8,128)(2,1)}, bf16[72,1024]{1,0:T(8,128)(2,1)S(1)}, u32[]{:S(2)}, u32[]{:S(2)}) %collective-permute-start.8) | collective-permute-done | bytes 147488 | tf_op jit(solution)/shard_map/ppermute | solution.py:242
  42.6 3.7 %collective-permute-start.10 = (bf16[64,512]{1,0:T(8,128)(2,1)S(1)}, bf16[64,512]{1,0:T(8,128)(2,1)S(1)}, u32[]{:S(2)}, u32[]{:S(2)}) collective-permute-start(bf16[64,512]{1,0:T(8,128)(2,1)S(1)} %slice.29), channel_id=1, source_target_pairs={{0,56},{8,0},{16,8},{24,16},{32,24},{40,32},{48,40},{56,48},{1,57}... | collective-permute-start | bytes 196616 | tf_op jit(solution)/shard_map/ppermute | solution.py:247
  46.3 0.9 collective-permute-done.7.refs_5_
  47.2 0.1 collective-permute-start.9
  47.3 0.0 collective-permute-done.2
  47.3 5.3 %pad_maximum_fusion = bf16[768,4096]{1,0:T(8,128)(2,1)} fusion(bf16[384,4096]{1,0:T(8,128)(2,1)S(1)} %collective-permute-done.2, bf16[384,4096]{1,0:T(8,128)(2,1)} %bitcast.45), kind=kLoop, calls=%fused_computation.1 | loop fusion | flops 12582912 | bytes 12582912 | tf_op jit(solution)/shard_map/concatenate | solution.py:253
  52.7 1.8 collective-permute-done.9.refs_7_
  54.4 0.0 collective-permute-done.1.refs_3_
  54.4 0.6 copy-done.6
  55.1 3.4 pack_ring.1
  58.5 31.1 %all_to_all.25 = bf16[16,64,1024]{2,1,0:T(8,128)(2,1)S(1)} all-to-all(bf16[16,64,1024]{2,1,0:T(8,128)(2,1)} %bitcast.51), channel_id=1, replica_groups=mesh['x'=4,'z'=8,'y'=4,'dp'=2] {'x','y'}, dimensions={0} | all-to-all | bytes 4194304 | tf_op jit(solution)/shard_map/all_to_all | solution.py:228
  89.6 0.6 slice_add_fusion._
  90.2 6.8 %pack.1 = bf16[16,8,8,3072]{3,2,1,0:T(8,128)(2,1)} custom-call(s32[8]{0:T(128)} %and_select_fusion.order_ref, f32[8,3,128]{2,1,0:T(4,128)} %get-tuple-element.34.table_ref, bf16[8,64,3072]{2,1,0:T(8,128)(2,1)} %bitcast.46, bf16[8,128]{1,0:T(8,128)(2,1)} %slice_add_fusion._), custom_call_target="tpu_custom_call" | custom-call | tf_op jit(solution)/shard_map/pack/pallas_call | solution.py:105
  97.0 73.9 %all_to_all.26 = bf16[16,64,3072]{2,1,0:T(8,128)(2,1)} all-to-all(bf16[16,64,3072]{2,1,0:T(8,128)(2,1)} %bitcast.37), channel_id=1, replica_groups=mesh['x'=4,'z'=8,'y'=4,'dp'=2] {'x','y'}, dimensions={0} | all-to-all | bytes 12582912 | tf_op jit(solution)/shard_map/all_to_all | solution.py:228
  171.0 18.3 %hidden.1 = bf16[1024,768]{1,0:T(8,128)(2,1)} custom-call(bf16[1024,1024]{1,0:T(8,128)(2,1)} %bitcast.39, bf16[1024,3072]{1,0:T(8,128)(2,1)} %bitcast.36, bf16[4096,384]{1,0:T(8,128)(2,1)} %bitcast.48, bf16[4096,384]{1,0:T(8,128)(2,1)} %collective-permute-done.refs_1_, bf16[4096,384]{1,0:T(8,128)(2,1)} %bitcast.50, ...), custom_call_target="tpu_custom_call" | custom-call | tf_op jit(solution)/shard_map/hidden/pallas_call | solution.py:191
  189.2 7.5 %convolution_convert_fusion = bf16[1024,3328]{1,0:T(8,128)(2,1)S(1)} fusion(bf16[1024,768]{1,0:T(8,128)(2,1)} %hidden.1, bf16[768,4096]{1,0:T(8,128)(2,1)S(1)} %bitcast.42), kind=kOutput, calls=%fused_computation | convolution fusion | flops 5237899264 | bytes 13500416 | tf_op jit(solution)/shard_map/dot_general | solution.py:213
  196.8 77.3 %all_to_all.27 = bf16[16,64,3328]{2,1,0:T(8,128)(2,1)} all-to-all(bf16[16,64,3328]{2,1,0:T(8,128)(2,1)S(1)} %bitcast.40), channel_id=1, replica_groups=mesh['x'=4,'z'=8,'y'=4,'dp'=2] {'x','y'}, dimensions={0} | all-to-all | bytes 13631488 | tf_op jit(solution)/shard_map/all_to_all | solution.py:228
  274.1 5.9 %mix.2 = bf16[8,64,3328]{2,1,0:T(8,128)(2,1)} custom-call(s32[8]{0:T(128)} %and_select_fusion.order_ref, f32[8,3,128]{2,1,0:T(4,128)} %get-tuple-element.34.table_ref, bf16[16,8,8,3328]{3,2,1,0:T(8,128)(2,1)} %bitcast.35), custom_call_target="tpu_custom_call" | custom-call | tf_op jit(solution)/shard_map/mix/pallas_call | solution.py:136
  280.0 0.0 reduce-scatter.2.cloned.1.call-update
  280.0 1.4 copy-done.1
  281.4 2.7 convolution_convert_fusion.1
  284.1 20.0 %all_to_all.28 = bf16[16,64,768]{2,1,0:T(8,128)(2,1)} all-to-all(bf16[16,64,768]{2,1,0:T(8,128)(2,1)S(1)} %bitcast.52), channel_id=1, replica_groups=mesh['x'=4,'z'=8,'y'=4,'dp'=2] {'x','y'}, dimensions={0} | all-to-all | bytes 3145728 | tf_op jit(solution)/shard_map/all_to_all | solution.py:228
  304.1 3.5 %mix.3 = bf16[8,64,768]{2,1,0:T(8,128)(2,1)} custom-call(s32[8]{0:T(128)} %and_select_fusion.order_ref, f32[8,3,128]{2,1,0:T(4,128)} %get-tuple-element.34.table_ref, bf16[16,8,8,768]{3,2,1,0:T(8,128)(2,1)} %bitcast.43), custom_call_target="tpu_custom_call" | custom-call | tf_op jit(solution)/shard_map/mix/pallas_call | solution.py:136
  307.7 35.3 %all_to_all.29 = bf16[8,64,768]{2,1,0:T(8,128)(2,1)S(1)} all-to-all(bf16[8,64,768]{2,1,0:T(8,128)(2,1)} %mix.3), channel_id=1, replica_groups=mesh['x'=4,'z'=8,'y'=4,'dp'=2] {'z'}, dimensions={0} | all-to-all | bytes 1572864 | tf_op jit(solution)/shard_map/all_to_all | solution.py:272
  343.0 0.1 reduce_sum.45
  343.1 0.0 reduce-scatter.2.cloned.1.call-done
  343.1 1.8 pad_maximum_fusion.1
  (32 shorter events, 0.1 us)
Async XLA Ops:
  6.5 83.7 %all-gather.3.cloned.1.call-start = ((), (), s32[]{:S(2)}) async-start(), calls=%async_computation.7 | async-start | bytes 3538944 | tf_op jit(solution)/shard_map/all_gather | solution.py:235
  6.5 40.8 %collective-permute-start.2 = (bf16[384,4096]{1,0:T(8,128)(2,1)}, bf16[384,4096]{1,0:T(8,128)(2,1)S(1)}, u32[]{:S(2)}, u32[]{:S(2)}) collective-permute-start(bf16[384,4096]{1,0:T(8,128)(2,1)} %bitcast.44), channel_id=1, source_target_pairs={{0,1},{1,0},{2,3},{3,2},{4,5},{5,4},{6,7},{7,6},{8,9},{9,8},{10,11... | collective-permute-start | bytes 9437192 | tf_op jit(solution)/shard_map/ppermute | solution.py:253
  8.3 334.8 %reduce-scatter.2.cloned.1.call-start = ((), (), s32[]{:S(2)}) async-start(), calls=%async_computation.6 | async-start | bytes 3833856 | tf_op jit(solution)/shard_map/reduce_scatter | solution.py:270
  8.4 46.1 %collective-permute-start = (bf16[4096,384]{1,0:T(8,128)(2,1)}, bf16[4096,384]{1,0:T(8,128)(2,1)}, u32[]{:S(2)}, u32[]{:S(2)}) collective-permute-start(bf16[4096,384]{1,0:T(8,128)(2,1)} %bitcast.47), channel_id=1, source_target_pairs={{0,1},{1,0},{2,3},{3,2},{4,5},{5,4},{6,7},{7,6},{8,9},{9,8},{10,11... | collective-permute-start | bytes 9437192 | tf_op jit(solution)/shard_map/ppermute | solution.py:252
  9.0 45.5 %collective-permute-start.1 = (bf16[4096,384]{1,0:T(8,128)(2,1)}, bf16[4096,384]{1,0:T(8,128)(2,1)}, u32[]{:S(2)}, u32[]{:S(2)}) collective-permute-start(bf16[4096,384]{1,0:T(8,128)(2,1)} %bitcast.49), channel_id=1, source_target_pairs={{0,1},{1,0},{2,3},{3,2},{4,5},{5,4},{6,7},{7,6},{8,9},{9,8},{10,11... | collective-permute-start | bytes 9437192 | tf_op jit(solution)/shard_map/ppermute | solution.py:252
  12.6 40.1 %copy-start.2 = (bf16[72,1024]{1,0:T(8,128)(2,1)}, bf16[72,1024]{1,0:T(8,128)(2,1)S(1)}, u32[]{:S(2)}) copy-start(bf16[72,1024]{1,0:T(8,128)(2,1)S(1)} %fusion.3.refs_0_) | copy-start | bytes 442372
  12.6 9.6 %collective-permute-start.4 = (bf16[72,1024]{1,0:T(8,128)(2,1)S(1)}, bf16[72,1024]{1,0:T(8,128)(2,1)S(1)}, u32[]{:S(2)}, u32[]{:S(2)}) collective-permute-start(bf16[72,1024]{1,0:T(8,128)(2,1)S(1)} %fusion.3.refs_0_), channel_id=1, source_target_pairs={{0,56},{8,0},{16,8},{24,16},{32,24},{40,32},{48,40},{56,48},{1,57}... | collective-permute-start | bytes 442376 | tf_op jit(solution)/shard_map/ppermute | solution.py:242
  18.5 7.4 %collective-permute-start.3 = (bf16[72,1024]{1,0:T(8,128)(2,1)S(1)}, bf16[72,1024]{1,0:T(8,128)(2,1)}, u32[]{:S(2)}, u32[]{:S(2)}) collective-permute-start(bf16[72,1024]{1,0:T(8,128)(2,1)S(1)} %fusion.3.refs_0_), channel_id=1, source_target_pairs={{0,8},{8,16},{16,24},{24,32},{32,40},{40,48},{48,56},{56,0},{1,9},... | collective-permute-start | bytes 442376 | tf_op jit(solution)/shard_map/ppermute | solution.py:242
  22.2 14.2 %copy-start.5 = (bf16[72,1024]{1,0:T(8,128)(2,1)}, bf16[72,1024]{1,0:T(8,128)(2,1)S(1)}, u32[]{:S(2)}) copy-start(bf16[72,1024]{1,0:T(8,128)(2,1)S(1)} %collective-permute-done.4.refs_2_) | copy-start | bytes 442372
  22.2 10.4 %collective-permute-start.6 = (bf16[72,1024]{1,0:T(8,128)(2,1)S(1)}, bf16[72,1024]{1,0:T(8,128)(2,1)}, u32[]{:S(2)}, u32[]{:S(2)}) collective-permute-start(bf16[72,1024]{1,0:T(8,128)(2,1)S(1)} %collective-permute-done.4.refs_2_), channel_id=1, source_target_pairs={{0,56},{8,0},{16,8},{24,16},{32,24},{40,32},{48,40},{56,48},{1,57}... | collective-permute-start | bytes 442376 | tf_op jit(solution)/shard_map/ppermute | solution.py:242
  25.9 10.8 %collective-permute-start.5 = (bf16[72,1024]{1,0:T(8,128)(2,1)}, bf16[72,1024]{1,0:T(8,128)(2,1)}, u32[]{:S(2)}, u32[]{:S(2)}) collective-permute-start(bf16[72,1024]{1,0:T(8,128)(2,1)} %collective-permute-done.3.refs_1_), channel_id=1, source_target_pairs={{0,8},{8,16},{16,24},{24,32},{32,40},{40,48},{48,56},{56,0},{1,9},... | collective-permute-start | bytes 442376 | tf_op jit(solution)/shard_map/ppermute | solution.py:242
  32.7 9.9 %collective-permute-start.8 = (bf16[72,1024]{1,0:T(8,128)(2,1)}, bf16[72,1024]{1,0:T(8,128)(2,1)S(1)}, u32[]{:S(2)}, u32[]{:S(2)}) collective-permute-start(bf16[72,1024]{1,0:T(8,128)(2,1)} %collective-permute-done.6.refs_4_), channel_id=1, source_target_pairs={{0,56},{8,0},{16,8},{24,16},{32,24},{40,32},{48,40},{56,48},{1,57}... | collective-permute-start | bytes 442376 | tf_op jit(solution)/shard_map/ppermute | solution.py:242
  36.8 10.4 %collective-permute-start.7 = (bf16[72,1024]{1,0:T(8,128)(2,1)}, bf16[72,1024]{1,0:T(8,128)(2,1)S(1)}, u32[]{:S(2)}, u32[]{:S(2)}) collective-permute-start(bf16[72,1024]{1,0:T(8,128)(2,1)} %collective-permute-done.5.refs_3_), channel_id=1, source_target_pairs={{0,8},{8,16},{16,24},{24,32},{32,40},{40,48},{48,56},{56,0},{1,9},... | collective-permute-start | bytes 442376 | tf_op jit(solution)/shard_map/ppermute | solution.py:242
  42.6 4.6 %copy-start.4 = (bf16[72,1024]{1,0:T(8,128)(2,1)}, bf16[72,1024]{1,0:T(8,128)(2,1)S(1)}, u32[]{:S(2)}) copy-start(bf16[72,1024]{1,0:T(8,128)(2,1)S(1)} %collective-permute-done.8.refs_6_) | copy-start | bytes 442372
  42.6 10.0 %collective-permute-start.10 = (bf16[64,512]{1,0:T(8,128)(2,1)S(1)}, bf16[64,512]{1,0:T(8,128)(2,1)S(1)}, u32[]{:S(2)}, u32[]{:S(2)}) collective-permute-start(bf16[64,512]{1,0:T(8,128)(2,1)S(1)} %slice.29), channel_id=1, source_target_pairs={{0,56},{8,0},{16,8},{24,16},{32,24},{40,32},{48,40},{56,48},{1,57}... | collective-permute-start | bytes 196616 | tf_op jit(solution)/shard_map/ppermute | solution.py:247
  47.2 5.4 %copy-start.3 = (bf16[72,1024]{1,0:T(8,128)(2,1)}, bf16[72,1024]{1,0:T(8,128)(2,1)S(1)}, u32[]{:S(2)}) copy-start(bf16[72,1024]{1,0:T(8,128)(2,1)S(1)} %collective-permute-done.7.refs_5_) | copy-start | bytes 442372
  47.2 7.2 %collective-permute-start.9 = (bf16[72,512]{1,0:T(8,128)(2,1)S(1)}, bf16[72,512]{1,0:T(8,128)(2,1)S(1)}, u32[]{:S(2)}, u32[]{:S(2)}) collective-permute-start(bf16[72,512]{1,0:T(8,128)(2,1)S(1)} %slice.28), channel_id=1, source_target_pairs={{0,8},{8,16},{16,24},{24,32},{32,40},{40,48},{48,56},{56,0},{1,9},... | collective-permute-start | bytes 221192 | tf_op jit(solution)/shard_map/ppermute | solution.py:246
  52.7 1.8 copy-start.7
  54.4 0.6 copy-start.6
  89.6 7.4 %copy-start = (bf16[16,64,1024]{2,1,0:T(8,128)(2,1)}, bf16[16,64,1024]{2,1,0:T(8,128)(2,1)S(1)}, u32[]{:S(2)}) copy-start(bf16[16,64,1024]{2,1,0:T(8,128)(2,1)S(1)} %all_to_all.25) | copy-start | bytes 6291460
  97.0 92.2 %slice-start = ((s8[6291456]{0:T(1024)(128)(4,1)}), s8[4194304]{0:T(1024)(128)(4,1)S(1)}, s32[]{:S(2)}) async-start(s8[6291456]{0:T(1024)(128)(4,1)} %bitcast.41), calls=%async_computation.8 | async-start | bytes 8388608
  171.0 18.3 %slice-start.1 = ((s8[6291456]{0:T(1024)(128)(4,1)}), s8[2097152]{0:T(1024)(128)(4,1)S(1)}, s32[]{:S(2)}) async-start(s8[6291456]{0:T(1024)(128)(4,1)} %bitcast.41), calls=%async_computation.9 | async-start | bytes 4194304
  280.0 1.4 copy-start.1
Sparse Core Ops, SparseCore 0:
  9.1 55.8 all-gather.2
  280.2 60.6 reduce-scatter.1

commit v6 on v5

--- a/solution.py
+++ b/solution.py
@@ -9,8 +9,8 @@
 from jax.sharding import Mesh
 from jax.sharding import PartitionSpec as P
 
-DEPTH = 1024
-ARRIVE = (1024, 3072)
+DEPTH = 512
+ARRIVE = (512, 3584)
 LEAVE = (3328, 768)
 
 
@@ -49,24 +49,21 @@
     *blocks, far_first, far_second, out_ref, table_ref = refs
     plane, sources, capacity, width = out_ref.shape
     lanes = plane * capacity
-    tok_count = far_second.shape[0]
+    tok_count = blocks[0].shape[0] - sources
     for i in range(sources):
-        ref = blocks[i] if i < len(blocks) else far_first
-        lists = ref[tok_count:, : 3 * lanes].astype(jnp.float32)
+        if i < len(blocks):
+            block, lists = blocks[i][:tok_count, :], blocks[i][tok_count:, : 3 * lanes]
+        else:
+            half = tok_count - far_first.shape[0]
+            block = jnp.concatenate([far_first[...], far_second[:half, :]], axis=0)
+            lists = far_second[half:, : 3 * lanes]
+        lists = lists.astype(jnp.float32)
         mine = lax.broadcasted_iota(jnp.int32, lists.shape, 0) == me_ref[0]
         lists = jnp.sum(jnp.where(mine, lists, 0.0), axis=0, keepdims=True)
         for r in range(3):
             table_ref[i, r : r + 1, :] = lists[:, r * lanes : (r + 1) * lanes]
-        here = hits(lists[:, :lanes], tok_count)
-        if i < len(blocks):
-            rows = place_rows(here, ref[:tok_count, :])
-            out_ref[:, i] = rows.reshape(plane, capacity, width)
-        else:
-            half = width // 2
-            rows = place_rows(here, far_first[:tok_count, :])
-            out_ref[:, i, :, :half] = rows.reshape(plane, capacity, half)
-            rows = place_rows(here, far_second[...])
-            out_ref[:, i, :, half:] = rows.reshape(plane, capacity, half)
+        rows = place_rows(hits(lists[:, :lanes], tok_count), block)
+        out_ref[:, i] = rows.reshape(plane, capacity, width)
 
 
 def pack_ring(me, blocks, tok_count, plane, capacity):
@@ -242,22 +239,24 @@
         above, below = lax.ppermute(above, "z", up_ring), lax.ppermute(below, "z", down_ring)
         ring += [above, below]
         order += [my_z - hop, my_z + hop]
-    half = ARRIVE[0] // 2
-    ring.append(lax.ppermute(above[:, :half], "z", up_ring))
-    ring.append(lax.ppermute(below[:tok_count, half:], "z", down_ring))
+    half = tok_count // 2
+    ring.append(lax.ppermute(below[:half], "z", down_ring))
+    ring.append(lax.ppermute(above[half:], "z", up_ring))
     order = jnp.stack([*order, my_z + z_size // 2]) % z_size
 
     swap = [(0, 1), (1, 0)]
     weights = [gate_w[0], up_w[0]]
     weights = [v for w in weights for v in (w, lax.ppermute(w, "dp", swap))]
-    w_down = jnp.concatenate([down_w[0], lax.ppermute(down_w[0], "dp", swap)], axis=0)
-
-    weights, w_down, ring, order = lax.optimization_barrier((weights, w_down, ring, order))
+    down_other = lax.ppermute(down_w[0], "dp", swap)
+
+    weights, down_other, ring, order = lax.optimization_barrier((weights, down_other, ring, order))
     rows, table = pack_ring(my_z[None], ring, tok_count, plane, capacity)
     rows = in_plane(rows)
     first = rows.reshape(rows_here, -1)
-    after = first[:8, :128] + 1
-    rows = in_plane(pack(order, table, second, after, plane, capacity, ARRIVE[1] // 3))
+    after, down_other = lax.optimization_barrier((first[:8, :128] + 1, down_other))
+    w_down = jnp.concatenate([down_w[0], down_other], axis=0)
+    after, w_down = lax.optimization_barrier((after, w_down))
+    rows = in_plane(pack(order, table, second, after, plane, capacity, ARRIVE[1] // 4))
     hidden = hidden_of(first, rows.reshape(rows_here, -1), weights)
 
     def answered(hidden, part, step):

time: 353 us -> 352 us (level)
  waiting for transfers between devices: 18.6 us -> 13.9 us
    ppermute x3, waiting for transfers between devices: 15.6 us -> 8.69 us  [body(): lax.ppermute(below, 'z', down_ring)]
where the time goes in v6:
time: 352 us
  blocking collectives  240 us (68%)
  Pallas kernels  38.2 us (11%)
  starting transfers between devices  17.8 us (5%)
  waiting for transfers between devices  13.9 us (4%)
  between operations  13.6 us (4%)
  other arithmetic  10.9 us (3%)
  matrix products  10.2 us (3%)
  local copies, waits for them, and re-layouts  6.75 us (2%)
    all_to_all x4, blocking collectives, in_plane(): lax.all_to_all(rows, ('x', 'y'), split_axis=0, concat_axis=0, tiled=True)  202 us
    all_to_all x1, blocking collectives, body(): lax.all_to_all(partial, 'z', split_axis=0, concat_axis=0, tiled=True)  38.5 us
    pallas_call x1, Pallas kernels, hidden_of(): pl.pallas_call(functools.partial(hidden_kernel, split=split), grid=(depth...  18.1 us
    ppermute x3, starting transfers between devices, body(): lax.ppermute(below, 'z', down_ring)  13.4 us
    dot_general x2, matrix products, dot(): return jnp.dot(a, b, preferred_element_type=jnp.float32)  10.2 us
    pallas_call x2, Pallas kernels, mix(): pl.pallas_call(mix_kernel, grid_spec=pltpu.PrefetchScalarGridSpec(num_sca...  9.59 us
    ppermute x3, waiting for transfers between devices, body(): lax.ppermute(below, 'z', down_ring)  8.69 us
    pallas_call x1, Pallas kernels, pack(): pl.pallas_call(pack_kernel, grid_spec=pltpu.PrefetchScalarGridSpec(num_sc...  7.39 us
  transfers between devices with their start and end apart: 13, of which 6 were waited for; matrix products, arithmetic and copies ran while one was open for 4% of the time, Pallas kernels for 2%

profile of v6, /device:TPU:2, one launch (start us, length us, event | category | flops | bytes accessed | tf_op | source)
XLA Modules:
  0.0 351.5 jit_solution(11022853823398353703)
XLA Ops:
  6.5 1.8 slice.24
  8.4 0.0 all-gather.3.cloned.1.call-update
  8.4 0.0 reduce-scatter.2.cloned.1.call-start
  8.4 0.1 collective-permute-start
  8.5 0.5 collective-permute-start.1
  9.0 0.1 collective-permute-start.2
  9.1 0.8 slice.21
  10.0 0.8 reshape.151
  10.7 0.8 broadcast_in_dim.28
  11.5 0.3 convert_reduce_fusion
  11.9 0.6 select_reduce_fusion.1
  12.6 5.9 %collective-permute-start.4 = (bf16[72,512]{1,0:T(8,128)(2,1)S(1)}, bf16[72,512]{1,0:T(8,128)(2,1)S(1)}, u32[]{:S(2)}, u32[]{:S(2)}) collective-permute-start(bf16[72,512]{1,0:T(8,128)(2,1)S(1)} %fusion.3.refs_0_), channel_id=1, source_target_pairs={{0,56},{8,0},{16,8},{24,16},{32,24},{40,32},{48,40},{56,48},{1,57}... | collective-permute-start | bytes 221192 | tf_op jit(solution)/shard_map/ppermute | solution.py:239
  18.5 2.1 collective-permute-done.4.refs_2_
  20.6 3.7 %collective-permute-start.6 = (bf16[72,512]{1,0:T(8,128)(2,1)S(1)}, bf16[72,512]{1,0:T(8,128)(2,1)}, u32[]{:S(2)}, u32[]{:S(2)}) collective-permute-start(bf16[72,512]{1,0:T(8,128)(2,1)S(1)} %collective-permute-done.4.refs_2_), channel_id=1, source_target_pairs={{0,56},{8,0},{16,8},{24,16},{32,24},{40,32},{48,40},{56,48},{1,57}... | collective-permute-start | bytes 221192 | tf_op jit(solution)/shard_map/ppermute | solution.py:239
  24.3 0.0 collective-permute-start.5
  24.3 3.6 %collective-permute-done.6.refs_4_ = bf16[72,512]{1,0:T(8,128)(2,1)} collective-permute-done((bf16[72,512]{1,0:T(8,128)(2,1)S(1)}, bf16[72,512]{1,0:T(8,128)(2,1)}, u32[]{:S(2)}, u32[]{:S(2)}) %collective-permute-start.6) | collective-permute-done | bytes 73760 | tf_op jit(solution)/shard_map/ppermute | solution.py:239
  28.0 3.8 %collective-permute-start.8 = (bf16[72,512]{1,0:T(8,128)(2,1)}, bf16[72,512]{1,0:T(8,128)(2,1)S(1)}, u32[]{:S(2)}, u32[]{:S(2)}) collective-permute-start(bf16[72,512]{1,0:T(8,128)(2,1)} %collective-permute-done.6.refs_4_), channel_id=1, source_target_pairs={{0,56},{8,0},{16,8},{24,16},{32,24},{40,32},{48,40},{56,48},{1,57}... | collective-permute-start | bytes 221192 | tf_op jit(solution)/shard_map/ppermute | solution.py:239
  31.8 0.6 stack.45
  32.4 2.9 collective-permute-done.8.refs_6_
  35.3 3.6 %collective-permute-start.9 = (bf16[32,512]{1,0:T(8,128)(2,1)S(1)}, bf16[32,512]{1,0:T(8,128)(2,1)S(1)}, u32[]{:S(2)}, u32[]{:S(2)}) collective-permute-start(bf16[32,512]{1,0:T(8,128)(2,1)S(1)} %slice.28), channel_id=1, source_target_pairs={{0,56},{8,0},{16,8},{24,16},{32,24},{40,32},{48,40},{56,48},{1,57}... | collective-permute-start | bytes 98312 | tf_op jit(solution)/shard_map/ppermute | solution.py:243
  38.9 0.2 collective-permute-done.7.refs_5_
  39.1 0.0 collective-permute-start.10
  39.1 1.1 and_select_fusion.order_ref
  40.2 0.3 collective-permute-done.9.refs_7_
  40.5 4.6 %collective-permute-done.10.refs_8_ = bf16[40,512]{1,0:T(8,128)(2,1)S(1)} collective-permute-done((bf16[40,512]{1,0:T(8,128)(2,1)S(1)}, bf16[40,512]{1,0:T(8,128)(2,1)S(1)}, u32[]{:S(2)}, u32[]{:S(2)}) %collective-permute-start.10) | collective-permute-done | bytes 40992 | tf_op jit(solution)/shard_map/ppermute | solution.py:244
  45.2 0.0 collective-permute-done.refs_1_
  45.2 0.0 collective-permute-done.1.refs_3_
  45.2 0.0 collective-permute-done.2
  45.2 0.5 copy-done.8
  45.8 3.2 pack_ring.1
  49.0 19.3 %all_to_all.25 = bf16[16,64,512]{2,1,0:T(8,128)(2,1)S(1)} all-to-all(bf16[16,64,512]{2,1,0:T(8,128)(2,1)} %bitcast.52), channel_id=1, replica_groups=mesh['x'=4,'z'=8,'y'=4,'dp'=2] {'x','y'}, dimensions={0} | all-to-all | bytes 2097152 | tf_op jit(solution)/shard_map/all_to_all | solution.py:225
  68.3 0.6 slice_add_fusion._
  68.9 6.2 %pad_maximum_fusion = bf16[768,4096]{1,0:T(8,128)(2,1)} fusion(bf16[384,4096]{1,0:T(8,128)(2,1)} %copy-done.1, bf16[384,4096]{1,0:T(8,128)(2,1)} %bitcast.46), kind=kLoop, calls=%fused_computation.1 | loop fusion | flops 12582912 | bytes 12582912 | tf_op jit(solution)/shard_map/concatenate | solution.py:257
  75.1 7.4 %pack.1 = bf16[16,8,8,3584]{3,2,1,0:T(8,128)(2,1)} custom-call(s32[8]{0:T(128)} %and_select_fusion.order_ref, f32[8,3,128]{2,1,0:T(4,128)} %get-tuple-element.38.table_ref, bf16[8,64,3584]{2,1,0:T(8,128)(2,1)} %bitcast.44, bf16[8,128]{1,0:T(8,128)(2,1)} %slice_add_fusion._), custom_call_target="tpu_custom_call" | custom-call | tf_op jit(solution)/shard_map/pack/pallas_call | solution.py:102
  82.5 85.0 %all_to_all.26 = bf16[16,64,3584]{2,1,0:T(8,128)(2,1)} all-to-all(bf16[16,64,3584]{2,1,0:T(8,128)(2,1)} %bitcast.36), channel_id=1, replica_groups=mesh['x'=4,'z'=8,'y'=4,'dp'=2] {'x','y'}, dimensions={0} | all-to-all | bytes 14680064 | tf_op jit(solution)/shard_map/all_to_all | solution.py:225
  167.5 18.1 %hidden.1 = bf16[1024,768]{1,0:T(8,128)(2,1)} custom-call(bf16[1024,512]{1,0:T(8,128)(2,1)} %bitcast.43, bf16[1024,3584]{1,0:T(8,128)(2,1)} %bitcast.35, bf16[4096,384]{1,0:T(8,128)(2,1)} %bitcast.48, bf16[4096,384]{1,0:T(8,128)(2,1)} %collective-permute-done.refs_1_, bf16[4096,384]{1,0:T(8,128)(2,1)} %bitcast.50, ...), custom_call_target="tpu_custom_call" | custom-call | tf_op jit(solution)/shard_map/hidden/pallas_call | solution.py:188
  185.6 7.5 %convolution_convert_fusion = bf16[1024,3328]{1,0:T(8,128)(2,1)S(1)} fusion(bf16[1024,768]{1,0:T(8,128)(2,1)} %hidden.1, bf16[768,4096]{1,0:T(8,128)(2,1)S(1)} %bitcast.40), kind=kOutput, calls=%fused_computation | convolution fusion | flops 5237899264 | bytes 13500416 | tf_op jit(solution)/shard_map/dot_general | solution.py:210
  193.1 77.8 %all_to_all.27 = bf16[16,64,3328]{2,1,0:T(8,128)(2,1)} all-to-all(bf16[16,64,3328]{2,1,0:T(8,128)(2,1)S(1)} %bitcast.38), channel_id=1, replica_groups=mesh['x'=4,'z'=8,'y'=4,'dp'=2] {'x','y'}, dimensions={0} | all-to-all | bytes 13631488 | tf_op jit(solution)/shard_map/all_to_all | solution.py:225
  270.9 6.0 %mix.2 = bf16[8,64,3328]{2,1,0:T(8,128)(2,1)} custom-call(s32[8]{0:T(128)} %and_select_fusion.order_ref, f32[8,3,128]{2,1,0:T(4,128)} %get-tuple-element.38.table_ref, bf16[16,8,8,3328]{3,2,1,0:T(8,128)(2,1)} %bitcast.37), custom_call_target="tpu_custom_call" | custom-call | tf_op jit(solution)/shard_map/mix/pallas_call | solution.py:133
  277.0 0.0 reduce-scatter.2.cloned.1.call-update
  277.0 1.4 copy-done.2
  278.4 2.7 convolution_convert_fusion.1
  281.1 19.6 %all_to_all.28 = bf16[16,64,768]{2,1,0:T(8,128)(2,1)} all-to-all(bf16[16,64,768]{2,1,0:T(8,128)(2,1)S(1)} %bitcast.51), channel_id=1, replica_groups=mesh['x'=4,'z'=8,'y'=4,'dp'=2] {'x','y'}, dimensions={0} | all-to-all | bytes 3145728 | tf_op jit(solution)/shard_map/all_to_all | solution.py:225
  300.6 3.5 %mix.3 = bf16[8,64,768]{2,1,0:T(8,128)(2,1)} custom-call(s32[8]{0:T(128)} %and_select_fusion.order_ref, f32[8,3,128]{2,1,0:T(4,128)} %get-tuple-element.38.table_ref, bf16[16,8,8,768]{3,2,1,0:T(8,128)(2,1)} %bitcast.41), custom_call_target="tpu_custom_call" | custom-call | tf_op jit(solution)/shard_map/mix/pallas_call | solution.py:133
  304.2 38.5 %all_to_all.29 = bf16[8,64,768]{2,1,0:T(8,128)(2,1)S(1)} all-to-all(bf16[8,64,768]{2,1,0:T(8,128)(2,1)} %mix.3), channel_id=1, replica_groups=mesh['x'=4,'z'=8,'y'=4,'dp'=2] {'z'}, dimensions={0} | all-to-all | bytes 1572864 | tf_op jit(solution)/shard_map/all_to_all | solution.py:271
  342.7 0.1 reduce_sum.45
  342.8 0.0 reduce-scatter.2.cloned.1.call-done
  342.8 1.8 pad_maximum_fusion.1
  (36 shorter events, 0.1 us)
Async XLA Ops:
  6.5 68.6 %all-gather.3.cloned.1.call-start = ((), (), s32[]{:S(2)}) async-start(), calls=%async_computation.7 | async-start | bytes 4128768 | tf_op jit(solution)/shard_map/all_gather | solution.py:232
  8.4 334.5 %reduce-scatter.2.cloned.1.call-start = ((), (), s32[]{:S(2)}) async-start(), calls=%async_computation.6 | async-start | bytes 3833856 | tf_op jit(solution)/shard_map/reduce_scatter | solution.py:269
  8.4 36.7 %collective-permute-start = (bf16[4096,384]{1,0:T(8,128)(2,1)}, bf16[4096,384]{1,0:T(8,128)(2,1)}, u32[]{:S(2)}, u32[]{:S(2)}) collective-permute-start(bf16[4096,384]{1,0:T(8,128)(2,1)} %bitcast.47), channel_id=1, source_target_pairs={{0,1},{1,0},{2,3},{3,2},{4,5},{5,4},{6,7},{7,6},{8,9},{9,8},{10,11... | collective-permute-start | bytes 9437192 | tf_op jit(solution)/shard_map/ppermute | solution.py:249
  8.5 36.6 %collective-permute-start.1 = (bf16[4096,384]{1,0:T(8,128)(2,1)}, bf16[4096,384]{1,0:T(8,128)(2,1)}, u32[]{:S(2)}, u32[]{:S(2)}) collective-permute-start(bf16[4096,384]{1,0:T(8,128)(2,1)} %bitcast.49), channel_id=1, source_target_pairs={{0,1},{1,0},{2,3},{3,2},{4,5},{5,4},{6,7},{7,6},{8,9},{9,8},{10,11... | collective-permute-start | bytes 9437192 | tf_op jit(solution)/shard_map/ppermute | solution.py:249
  9.0 36.2 %collective-permute-start.2 = (bf16[384,4096]{1,0:T(8,128)(2,1)}, bf16[384,4096]{1,0:T(8,128)(2,1)S(1)}, u32[]{:S(2)}, u32[]{:S(2)}) collective-permute-start(bf16[384,4096]{1,0:T(8,128)(2,1)} %bitcast.45), channel_id=1, source_target_pairs={{0,1},{1,0},{2,3},{3,2},{4,5},{5,4},{6,7},{7,6},{8,9},{9,8},{10,11... | collective-permute-start | bytes 9437192 | tf_op jit(solution)/shard_map/ppermute | solution.py:250
  12.6 32.6 %copy-start.3 = (bf16[72,512]{1,0:T(8,128)(2,1)}, bf16[72,512]{1,0:T(8,128)(2,1)S(1)}, u32[]{:S(2)}) copy-start(bf16[72,512]{1,0:T(8,128)(2,1)S(1)} %fusion.3.refs_0_) | copy-start | bytes 221188
  12.6 8.1 %collective-permute-start.4 = (bf16[72,512]{1,0:T(8,128)(2,1)S(1)}, bf16[72,512]{1,0:T(8,128)(2,1)S(1)}, u32[]{:S(2)}, u32[]{:S(2)}) collective-permute-start(bf16[72,512]{1,0:T(8,128)(2,1)S(1)} %fusion.3.refs_0_), channel_id=1, source_target_pairs={{0,56},{8,0},{16,8},{24,16},{32,24},{40,32},{48,40},{56,48},{1,57}... | collective-permute-start | bytes 221192 | tf_op jit(solution)/shard_map/ppermute | solution.py:239
  18.5 5.8 %collective-permute-start.3 = (bf16[72,512]{1,0:T(8,128)(2,1)S(1)}, bf16[72,512]{1,0:T(8,128)(2,1)S(1)}, u32[]{:S(2)}, u32[]{:S(2)}) collective-permute-start(bf16[72,512]{1,0:T(8,128)(2,1)S(1)} %fusion.3.refs_0_), channel_id=1, source_target_pairs={{0,8},{8,16},{16,24},{24,32},{32,40},{40,48},{48,56},{56,0},{1,9},... | collective-permute-start | bytes 221192 | tf_op jit(solution)/shard_map/ppermute | solution.py:239
  20.6 24.6 %copy-start.6 = (bf16[72,512]{1,0:T(8,128)(2,1)}, bf16[72,512]{1,0:T(8,128)(2,1)S(1)}, u32[]{:S(2)}) copy-start(bf16[72,512]{1,0:T(8,128)(2,1)S(1)} %collective-permute-done.4.refs_2_) | copy-start | bytes 221188
  20.6 7.3 %collective-permute-start.6 = (bf16[72,512]{1,0:T(8,128)(2,1)S(1)}, bf16[72,512]{1,0:T(8,128)(2,1)}, u32[]{:S(2)}, u32[]{:S(2)}) collective-permute-start(bf16[72,512]{1,0:T(8,128)(2,1)S(1)} %collective-permute-done.4.refs_2_), channel_id=1, source_target_pairs={{0,56},{8,0},{16,8},{24,16},{32,24},{40,32},{48,40},{56,48},{1,57}... | collective-permute-start | bytes 221192 | tf_op jit(solution)/shard_map/ppermute | solution.py:239
  24.3 20.9 %copy-start.7 = (bf16[72,512]{1,0:T(8,128)(2,1)}, bf16[72,512]{1,0:T(8,128)(2,1)S(1)}, u32[]{:S(2)}) copy-start(bf16[72,512]{1,0:T(8,128)(2,1)S(1)} %collective-permute-done.3.refs_1_) | copy-start | bytes 221188
  24.3 7.4 %collective-permute-start.5 = (bf16[72,512]{1,0:T(8,128)(2,1)S(1)}, bf16[72,512]{1,0:T(8,128)(2,1)}, u32[]{:S(2)}, u32[]{:S(2)}) collective-permute-start(bf16[72,512]{1,0:T(8,128)(2,1)S(1)} %collective-permute-done.3.refs_1_), channel_id=1, source_target_pairs={{0,8},{8,16},{16,24},{24,32},{32,40},{40,48},{48,56},{56,0},{1,9},... | collective-permute-start | bytes 221192 | tf_op jit(solution)/shard_map/ppermute | solution.py:239
  28.0 7.4 %collective-permute-start.8 = (bf16[72,512]{1,0:T(8,128)(2,1)}, bf16[72,512]{1,0:T(8,128)(2,1)S(1)}, u32[]{:S(2)}, u32[]{:S(2)}) collective-permute-start(bf16[72,512]{1,0:T(8,128)(2,1)} %collective-permute-done.6.refs_4_), channel_id=1, source_target_pairs={{0,56},{8,0},{16,8},{24,16},{32,24},{40,32},{48,40},{56,48},{1,57}... | collective-permute-start | bytes 221192 | tf_op jit(solution)/shard_map/ppermute | solution.py:239
  31.8 7.3 %collective-permute-start.7 = (bf16[72,512]{1,0:T(8,128)(2,1)}, bf16[72,512]{1,0:T(8,128)(2,1)S(1)}, u32[]{:S(2)}, u32[]{:S(2)}) collective-permute-start(bf16[72,512]{1,0:T(8,128)(2,1)} %collective-permute-done.5.refs_3_), channel_id=1, source_target_pairs={{0,8},{8,16},{16,24},{24,32},{32,40},{40,48},{48,56},{56,0},{1,9},... | collective-permute-start | bytes 221192 | tf_op jit(solution)/shard_map/ppermute | solution.py:239
  35.3 9.9 %copy-start.5 = (bf16[72,512]{1,0:T(8,128)(2,1)}, bf16[72,512]{1,0:T(8,128)(2,1)S(1)}, u32[]{:S(2)}) copy-start(bf16[72,512]{1,0:T(8,128)(2,1)S(1)} %collective-permute-done.8.refs_6_) | copy-start | bytes 221188
  35.3 5.2 %collective-permute-start.9 = (bf16[32,512]{1,0:T(8,128)(2,1)S(1)}, bf16[32,512]{1,0:T(8,128)(2,1)S(1)}, u32[]{:S(2)}, u32[]{:S(2)}) collective-permute-start(bf16[32,512]{1,0:T(8,128)(2,1)S(1)} %slice.28), channel_id=1, source_target_pairs={{0,56},{8,0},{16,8},{24,16},{32,24},{40,32},{48,40},{56,48},{1,57}... | collective-permute-start | bytes 98312 | tf_op jit(solution)/shard_map/ppermute | solution.py:243
  39.1 6.1 %copy-start.4 = (bf16[72,512]{1,0:T(8,128)(2,1)}, bf16[72,512]{1,0:T(8,128)(2,1)S(1)}, u32[]{:S(2)}) copy-start(bf16[72,512]{1,0:T(8,128)(2,1)S(1)} %collective-permute-done.7.refs_5_) | copy-start | bytes 221188
  39.1 6.1 %collective-permute-start.10 = (bf16[40,512]{1,0:T(8,128)(2,1)S(1)}, bf16[40,512]{1,0:T(8,128)(2,1)S(1)}, u32[]{:S(2)}, u32[]{:S(2)}) collective-permute-start(bf16[40,512]{1,0:T(8,128)(2,1)S(1)} %slice.29), channel_id=1, source_target_pairs={{0,8},{8,16},{16,24},{24,32},{32,40},{40,48},{48,56},{56,0},{1,9},... | collective-permute-start | bytes 122888 | tf_op jit(solution)/shard_map/ppermute | solution.py:244
  40.5 4.7 %copy-start.9 = (bf16[32,512]{1,0:T(8,128)(2,1)}, bf16[32,512]{1,0:T(8,128)(2,1)S(1)}, u32[]{:S(2)}) copy-start(bf16[32,512]{1,0:T(8,128)(2,1)S(1)} %collective-permute-done.9.refs_7_) | copy-start | bytes 98308
  45.2 0.6 copy-start.8
  45.8 3.2 copy-start.1
  68.3 6.8 %copy-start = (bf16[16,64,512]{2,1,0:T(8,128)(2,1)}, bf16[16,64,512]{2,1,0:T(8,128)(2,1)S(1)}, u32[]{:S(2)}) copy-start(bf16[16,64,512]{2,1,0:T(8,128)(2,1)S(1)} %all_to_all.25) | copy-start | bytes 3145732
  82.5 103.1 %slice-start = ((s8[6291456]{0:T(1024)(128)(4,1)}), s8[4194304]{0:T(1024)(128)(4,1)S(1)}, s32[]{:S(2)}) async-start(s8[6291456]{0:T(1024)(128)(4,1)} %bitcast.39), calls=%async_computation.8 | async-start | bytes 8388608
  167.5 18.1 %slice-start.1 = ((s8[6291456]{0:T(1024)(128)(4,1)}), s8[2097152]{0:T(1024)(128)(4,1)S(1)}, s32[]{:S(2)}) async-start(s8[6291456]{0:T(1024)(128)(4,1)} %bitcast.39), calls=%async_computation.9 | async-start | bytes 4194304
  277.0 1.4 copy-start.2
Sparse Core Ops, SparseCore 0:
  9.1 56.8 all-gather.2
  277.1 62.8 reduce-scatter.1

commit v7 on v1

v7 whole, which is shorter than its diff:
```python
import functools

import jax
import jax.numpy as jnp
import numpy as np
from jax import lax
from jax.experimental import pallas as pl
from jax.experimental.pallas import tpu as pltpu
from jax.sharding import Mesh
from jax.sharding import PartitionSpec as P

DEPTH = 512
STEP = 1024
LISTS = 512
NEAR = (0, -1, 1)


def slot_table(routes, gate_probs, sizes, capacity):
    x_size, z_size, y_size = sizes
    tok_count, top_count = routes.shape
    flat = routes.T.reshape(-1)
    token = jnp.arange(tok_count * top_count, dtype=jnp.int32) % tok_count
    earlier = (flat[:, None] == flat[None, :]) & (token[None, :] < token[:, None])
    slot = jnp.sum(earlier.astype(jnp.int32), axis=1)
    ex, ez, ey = flat // (z_size * y_size), flat // y_size % z_size, flat % y_size
    target = ((ez * x_size + ex) * y_size + ey) * capacity + slot
    slots = jnp.arange(x_size * z_size * y_size * capacity, dtype=jnp.int32)
    here = target[None, :] == slots[:, None]
    held = jnp.sum(jnp.where(here, (token + 1).astype(jnp.float32)[None, :], 0.0), axis=1)
    prob = jnp.sum(jnp.where(here, gate_probs.T.reshape(-1)[None, :], 0.0), axis=1)
    high = lax.reduce_precision(prob, 8, 7)
    table = jnp.stack([held, high, prob - high]).reshape(3, z_size, -1)
    return table.transpose(1, 0, 2).astype(jnp.bfloat16)


def hits(row_token, tok_count):
    tokens = lax.broadcasted_iota(jnp.int32, (tok_count, row_token.shape[1]), 0)
    return tokens == row_token.astype(jnp.int32) - 1


def place_rows(here, block):
    place = jnp.where(here, 1.0, 0.0).astype(jnp.bfloat16)
    rows = lax.dot_general(
        place, block, (((0,), (0,)), ((), ())), preferred_element_type=jnp.float32
    )
    return rows.astype(jnp.bfloat16)


def lists_of(rows, me, lanes):
    rows = rows[:, : 3 * lanes].astype(jnp.float32)
    mine = lax.broadcasted_iota(jnp.int32, rows.shape, 0) == me
    rows = jnp.sum(jnp.where(mine, rows, 0.0), axis=0, keepdims=True)
    return [rows[:, r * lanes : (r + 1) * lanes] for r in range(3)]


def mixed(lists, rows, tok_count):
    here = hits(lists[0], tok_count)
    both = jnp.concatenate([jnp.where(here, part, 0.0) for part in lists[1:]], axis=0)
    sums = jnp.dot(both.astype(jnp.bfloat16), rows, preferred_element_type=jnp.float32)
    return sums[:tok_count] + sums[tok_count:]


def pack_near_kernel(order_ref, *refs):
    *list_refs, out_ref = refs
    count = len(list_refs) // 2
    plane, _, capacity, width = out_ref.shape
    for i in range(count):
        token_ref = list_refs[count + i]
        lists = lists_of(list_refs[i][...], order_ref[0], plane * capacity)
        rows = place_rows(hits(lists[0], token_ref.shape[0]), token_ref[...])
        out_ref[:, i] = rows.reshape(plane, capacity, width)


def pack_near(order, blocks, tok_count, plane, capacity):
    count, width = len(blocks), blocks[0].shape[1]
    z_size = blocks[0].shape[0] - tok_count
    below = pl.BlockSpec((z_size, LISTS), lambda i, order: (tok_count // z_size, 0))
    return pl.pallas_call(
        pack_near_kernel,
        grid_spec=pltpu.PrefetchScalarGridSpec(
            num_scalar_prefetch=1,
            grid=(width // STEP,),
            in_specs=[below] * count
            + [pl.BlockSpec((tok_count, STEP), lambda i, order: (0, i))] * count,
            out_specs=pl.BlockSpec((plane, count, capacity, STEP), lambda i, order: (0, 0, 0, i)),
        ),
        out_shape=jax.ShapeDtypeStruct((plane, count, capacity, width), jnp.bfloat16),
        name="pack_near",
    )(order, *blocks, *blocks)


def pack_far_kernel(order_ref, lists_ref, tok_ref, _, out_ref):
    plane, count, capacity, width = out_ref.shape
    for i in range(count):
        src = order_ref[len(NEAR) + i]
        lists = lists_of(lists_ref[src], order_ref[0], plane * capacity)
        rows = place_rows(hits(lists[0], tok_ref.shape[1]), tok_ref[src])
        out_ref[:, i] = rows.reshape(plane, capacity, width)


def pack_far(order, blocks, after, tok_count, plane, capacity):
    z_size, _, width = blocks.shape
    count = z_size - len(NEAR)
    return pl.pallas_call(
        pack_far_kernel,
        grid_spec=pltpu.PrefetchScalarGridSpec(
            num_scalar_prefetch=1,
            grid=(width // STEP,),
            in_specs=[
                pl.BlockSpec((z_size, z_size, LISTS), lambda i, order: (0, tok_count // z_size, 0)),
                pl.BlockSpec((z_size, tok_count, STEP), lambda i, order: (0, 0, i)),
                pl.BlockSpec(after.shape, lambda i, order: (0, 0)),
            ],
            out_specs=pl.BlockSpec((plane, count, capacity, STEP), lambda i, order: (0, 0, 0, i)),
        ),
        out_shape=jax.ShapeDtypeStruct((plane, count, capacity, width), jnp.bfloat16),
        name="pack_far",
    )(order, blocks, blocks, after)


def mix_far_kernel(order_ref, lists_ref, rows_ref, out_ref):
    plane, count, capacity, width = rows_ref.shape
    for i in range(len(NEAR)):
        out_ref[order_ref[i]] = jnp.zeros(out_ref.shape[1:], out_ref.dtype)
    for i in range(count):
        src = order_ref[len(NEAR) + i]
        lists = lists_of(lists_ref[src], order_ref[0], plane * capacity)
        rows = rows_ref[:, i].reshape(plane * capacity, width)
        out_ref[src] = mixed(lists, rows, out_ref.shape[1]).astype(out_ref.dtype)


def mix_far(order, blocks, rows, tok_count):
    plane, count, capacity, width = rows.shape
    z_size = blocks.shape[0]
    return pl.pallas_call(
        mix_far_kernel,
        grid_spec=pltpu.PrefetchScalarGridSpec(
            num_scalar_prefetch=1,
            grid=(width // STEP,),
            in_specs=[
                pl.BlockSpec((z_size, z_size, LISTS), lambda i, order: (0, tok_count // z_size, 0)),
                pl.BlockSpec((plane, count, capacity, STEP), lambda i, order: (0, 0, 0, i)),
            ],
            out_specs=pl.BlockSpec((z_size, tok_count, STEP), lambda i, order: (0, 0, i)),
        ),
        out_shape=jax.ShapeDtypeStruct((z_size, tok_count, width), jnp.bfloat16),
        name="mix_far",
    )(order, blocks, rows)


def mix_near_kernel(order_ref, *refs):
    count = len(NEAR)
    rows_ref, outs = refs[count], refs[count + 1 :]
    plane, _, capacity, width = rows_ref.shape
    for i in range(count):
        lists = lists_of(refs[i][...], order_ref[0], plane * capacity)
        rows = rows_ref[:, i].reshape(plane * capacity, width)
        outs[i][...] = mixed(lists, rows, outs[i].shape[0]).astype(outs[i].dtype)


def mix_near(order, blocks, rows, tok_count):
    plane, count, capacity, width = rows.shape
    z_size = blocks[0].shape[0] - tok_count
    kinds = [jnp.bfloat16 if offset else jnp.float32 for offset in NEAR]
    return pl.pallas_call(
        mix_near_kernel,
        grid_spec=pltpu.PrefetchScalarGridSpec(
            num_scalar_prefetch=1,
            grid=(width // STEP,),
            in_specs=[pl.BlockSpec((z_size, LISTS), lambda i, order: (tok_count // z_size, 0))]
            * count
            + [pl.BlockSpec((plane, count, capacity, STEP), lambda i, order: (0, 0, 0, i))],
            out_specs=[pl.BlockSpec((tok_count, STEP), lambda i, order: (0, i))] * count,
        ),
        out_shape=[jax.ShapeDtypeStruct((tok_count, width), kind) for kind in kinds],
        name="mix_near",
    )(order, *blocks, rows)


def hidden_kernel(near_ref, far_ref, *refs):
    *weights, out_near, out_far, gate_near, up_near, gate_far, up_far = refs
    step, steps = pl.program_id(0), pl.num_programs(0)
    gate, gate_other, up, up_other = (ref[...] for ref in weights)
    gate = jnp.concatenate([gate, gate_other], axis=1)
    up = jnp.concatenate([up, up_other], axis=1)
    parts = [(near_ref, out_near, gate_near, up_near), (far_ref, out_far, gate_far, up_far)]
    for rows_ref, out_ref, gate_acc, up_acc in parts:
        rows = rows_ref[...]

        @pl.when(step == 0)
        def _():
            gate_acc[...] = dot(rows, gate)
            up_acc[...] = dot(rows, up)

        @pl.when((step > 0) & (step < steps - 1))
        def _():
            gate_acc[...] += dot(rows, gate)
            up_acc[...] += dot(rows, up)

        @pl.when(step == steps - 1)
        def _():
            gate_act = gate_acc[...] + dot(rows, gate)
            up_act = up_acc[...] + dot(rows, up)
            out_ref[...] = (jax.nn.silu(gate_act) * up_act).astype(out_ref.dtype)


def hidden_of(near, far, weights):
    depth, units = weights[0].shape
    counts = [near.shape[0], far.shape[0]]
    return pl.pallas_call(
        hidden_kernel,
        grid=(depth // DEPTH,),
        in_specs=[pl.BlockSpec((c, DEPTH), lambda i: (0, i)) for c in counts]
        + [pl.BlockSpec((DEPTH, units), lambda i: (i, 0))] * 4,
        out_specs=[pl.BlockSpec((c, 2 * units), lambda i: (0, 0)) for c in counts],
        out_shape=[jax.ShapeDtypeStruct((c, 2 * units), jnp.bfloat16) for c in counts],
        scratch_shapes=[pltpu.VMEM((c, 2 * units), jnp.float32) for c in counts for _ in range(2)],
        compiler_params=pltpu.CompilerParams(vmem_limit_bytes=56 << 20),
        name="hidden",
    )(near, far, *weights)


def dot(a, b):
    return jnp.dot(a, b, preferred_element_type=jnp.float32)


def body(tokens, routes, gate_probs, gate_w, up_w, down_w):
    sizes = tuple(lax.axis_size(a) for a in ("x", "z", "y"))
    x_size, z_size, y_size = sizes
    plane = x_size * y_size
    tok_count, model_width = tokens.shape
    capacity = 2 * tok_count * routes.shape[1] // (plane * z_size)
    my_z = lax.axis_index("z")
    up_ring = [(i, (i + 1) % z_size) for i in range(z_size)]
    down_ring = [(i, (i - 1) % z_size) for i in range(z_size)]

    def in_plane(rows, count):
        rows = rows.reshape(plane, count * capacity, model_width)
        rows = lax.all_to_all(rows, ("x", "y"), split_axis=0, concat_axis=0, tiled=True)
        return rows.reshape(plane, count, capacity, model_width)

    def flat(rows):
        return rows.reshape(-1, model_width)

    offsets = [*NEAR, *(d for d in range(2, z_size - 1))]
    near_count, far_count = len(NEAR), z_size - len(NEAR)
    order = jnp.stack([my_z + d for d in offsets]) % z_size

    table = slot_table(routes, gate_probs, sizes, capacity).reshape(z_size, -1)
    table = jnp.pad(table, ((0, 0), (0, model_width - table.shape[1])))
    block = jnp.concatenate([tokens, table], axis=0)
    blocks = lax.all_gather(block, "z", axis=0, tiled=False)
    near_blocks = [block, lax.ppermute(block, "z", up_ring), lax.ppermute(block, "z", down_ring)]

    swap = [(0, 1), (1, 0)]
    weights = [gate_w[0], up_w[0]]
    weights = [v for w in weights for v in (w, lax.ppermute(w, "dp", swap))]
    w_down = jnp.concatenate([down_w[0], lax.ppermute(down_w[0], "dp", swap)], axis=0)

    weights, w_down, near_blocks, order = lax.optimization_barrier(
        (weights, w_down, near_blocks, order)
    )
    near = flat(in_plane(pack_near(order, near_blocks, tok_count, plane, capacity), near_count))
    after = near[:8, :128] + 1
    far = pack_far(order, blocks, after, tok_count, plane, capacity)
    far = flat(in_plane(far, far_count))
    hidden_near, hidden_far = hidden_of(near, far, weights)

    answers = dot(hidden_far, w_down).astype(jnp.bfloat16)
    answers = in_plane(answers, far_count)
    partial = mix_far(order, blocks, answers, tok_count)
    partial, hidden_near = lax.optimization_barrier((partial, hidden_near))
    total = lax.psum_scatter(partial, "z", scatter_dimension=0, tiled=True)[0]

    answers = dot(hidden_near, w_down).astype(jnp.bfloat16)
    answers = in_plane(answers, near_count)
    own, under, over = mix_near(order, near_blocks, answers, tok_count)
    under, over = lax.ppermute(under, "z", down_ring), lax.ppermute(over, "z", up_ring)
    total = total.astype(jnp.float32) + own + under.astype(jnp.float32) + over.astype(jnp.float32)
    return total.astype(jnp.bfloat16)


def solution(mesh):
    experts, dp = mesh.shape["expert"], mesh.shape["dp"]
    x_size = y_size = 4
    z_size = experts // (x_size * y_size)
    grid = Mesh(mesh.devices.reshape(x_size, z_size, y_size, dp), ("x", "z", "y", "dp"))
    every, owner = ("x", "z", "y", "dp"), ("x", "z", "y")
    return jax.shard_map(
        body,
        mesh=grid,
        in_specs=(
            P(every, None),
            P(every, None),
            P(every, None),
            P(owner, None, "dp"),
            P(owner, None, "dp"),
            P(owner, "dp", None),
        ),
        out_specs=P(every, None),
        check_vma=False,
    )
```

time: 482 us -> 335 us (0.70)
  waiting for transfers between devices: 329 us -> 27.8 us
  blocking collectives: 0 us -> 203 us
  starting transfers between devices: 77.5 us -> 17.1 us
  Pallas kernels: 13.4 us -> 44.5 us
  matrix products: 40.3 us -> 11.3 us
  other arithmetic: 3.15 us -> 12.8 us
    all_to_all x0 -> x4, blocking collectives: none -> 203 us  [in_plane(): lax.all_to_all(rows, ('x', 'y'), split_axis=0, concat_axis=0, tiled=True)]
    all_to_all x2 -> x0, waiting for transfers between devices: 198 us -> none  [the longest x1 103 us: body(): lax.all_to_all(answers, PLANE, split_axis=0, concat_axis=0, tiled=True)]
    reduce_scatter x1, waiting for transfers between devices: 85 us -> 0.01 us  [body(): total = lax.psum_scatter(partial, 'z', scatter_dimension=0, tiled=True)[0]]
    all_to_all x2 -> x0, starting transfers between devices: 58.3 us -> none  [the longest x1 50.7 us: body(): lax.all_to_all(answers, PLANE, split_axis=0, concat_axis=0, tiled=True)]
    all_gather x1, waiting for transfers between devices: 35.1 us -> 0.01 us  [body(): blocks = lax.all_gather(block, 'z', axis=0, tiled=False)]
    pallas_call x1 -> x5, Pallas kernels: 13.4 us -> 44.5 us  [the longest x1 20.5 us: hidden_of(): pl.pallas_call(hidden_kernel, grid=(depth // DEPTH,), in_specs=[pl.BlockS...]
    dot_general x4 -> x2, matrix products: 40.3 us -> 11.3 us  [dot(): return jnp.dot(a, b, preferred_element_type=jnp.float32)]
    ppermute x9 -> x6, waiting for transfers between devices: 10.3 us -> 27.8 us  [the longest x1 12.6 us: body(): lax.ppermute(block, 'z', down_ring)]
  transfers between devices with their start and end apart: 14 -> 9, of which waited for: 6 -> 4; matrix products, arithmetic and copies ran while one was open for 6% -> 4% of each run, Pallas kernels for 0% -> 3%
where the time goes in v7:
time: 335 us; the launch traced here: 334 us
  blocking collectives  203 us (61%)
  Pallas kernels  44.5 us (13%)
  waiting for transfers between devices  27.8 us (8%)
  starting transfers between devices  17.1 us (5%)
  between operations  13.5 us (4%)
  other arithmetic  12.8 us (4%)
  matrix products  11.3 us (3%)
  local copies, waits for them, and re-layouts  3.46 us (1%)
    all_to_all x4, blocking collectives, in_plane(): lax.all_to_all(rows, ('x', 'y'), split_axis=0, concat_axis=0, tiled=True)  203 us
    pallas_call x1, Pallas kernels, hidden_of(): pl.pallas_call(hidden_kernel, grid=(depth // DEPTH,), in_specs=[pl.BlockS...  20.5 us
    ppermute x1, waiting for transfers between devices, body(): lax.ppermute(block, 'z', down_ring)  12.6 us
    dot_general x2, matrix products, dot(): return jnp.dot(a, b, preferred_element_type=jnp.float32)  11.3 us
    ppermute x1, starting transfers between devices, body(): lax.ppermute(under, 'z', down_ring)  10.5 us
    ppermute x1, waiting for transfers between devices, body(): lax.ppermute(under, 'z', down_ring)  8.54 us
    pallas_call x1, Pallas kernels, pack_far(): pl.pallas_call(pack_far_kernel, grid_spec=pltpu.PrefetchScalarGridSpec(nu...  6.71 us
  transfers between devices with their start and end apart: 9, of which 4 were waited for; matrix products, arithmetic and copies ran while one was open for 4% of the time, Pallas kernels for 3%

profile of v7, /device:TPU:2, one launch (start us, length us, event | category | flops | bytes accessed | tf_op | source)
XLA Modules:
  0.0 333.7 jit_solution(18395833867123458208)
XLA Ops:
  6.5 0.0 all-gather.3.cloned.1.call-start
  6.5 0.8 reshape.159
  7.3 0.8 broadcast_in_dim.27
  8.1 0.3 convert_reduce_fusion
  8.4 0.6 select_reduce_fusion.1
  9.1 1.9 fusion.4.refs_0_.refs_3_
  11.0 0.0 all-gather.3.cloned.1.call-update
  11.0 0.0 reduce-scatter.2.cloned.1.call-start
  11.1 0.1 collective-permute-start.2
  11.2 0.5 collective-permute-start
  11.7 0.1 collective-permute-start.1
  11.8 5.9 %collective-permute-start.4 = (bf16[72,4096]{1,0:T(8,128)(2,1)}, bf16[72,4096]{1,0:T(8,128)(2,1)S(1)}, u32[]{:S(2)}, u32[]{:S(2)}) collective-permute-start(bf16[72,4096]{1,0:T(8,128)(2,1)} %fusion.4.refs_0_.refs_3_), channel_id=1, source_target_pairs={{0,56},{8,0},{16,8},{24,16},{32,24},{40,32},{48,40},{56,48},{1,57}... | collective-permute-start | bytes 1769480 | tf_op jit(solution)/shard_map/ppermute | solution.py:253
  17.6 0.0 collective-permute-start.3
  17.6 0.1 stack.45
  17.7 0.6 and_select_fusion.order_ref
  18.3 0.0 collective-permute-done.2
  18.3 6.3 %pad_maximum_fusion = bf16[768,4096]{1,0:T(8,128)(2,1)} fusion(bf16[384,4096]{1,0:T(8,128)(2,1)} %collective-permute-done.2, bf16[384,4096]{1,0:T(8,128)(2,1)} %bitcast.58), kind=kLoop, calls=%fused_computation.1 | loop fusion | flops 12582912 | bytes 12582912 | tf_op jit(solution)/shard_map/concatenate | solution.py:258
  24.6 12.6 %collective-permute-done.4.refs_2_.refs_5_ = bf16[72,4096]{1,0:T(8,128)(2,1)S(1)} collective-permute-done((bf16[72,4096]{1,0:T(8,128)(2,1)}, bf16[72,4096]{1,0:T(8,128)(2,1)S(1)}, u32[]{:S(2)}, u32[]{:S(2)}) %collective-permute-start.4) | collective-permute-done | bytes 589856 | tf_op jit(solution)/shard_map/ppermute | solution.py:253
  37.3 0.0 copy-start.1
  37.3 3.3 collective-permute-done.3.refs_1_.refs_4_
  40.5 0.0 copy-start.2
  40.5 0.0 collective-permute-done.refs_1_
  40.6 0.0 collective-permute-done.1.refs_3_
  40.6 0.0 copy-done.1
  40.6 0.8 copy-done.2
  41.4 5.6 %pack_near.1 = bf16[16,3,8,4096]{3,2,1,0:T(8,128)(2,1)} custom-call(s32[8]{0:T(128)} %and_select_fusion.order_ref, bf16[72,4096]{1,0:T(8,128)(2,1)} %fusion.4.refs_0_.refs_3_, bf16[72,4096]{1,0:T(8,128)(2,1)} %copy-done.2, bf16[72,4096]{1,0:T(8,128)(2,1)} %copy-done.1, bf16[72,4096]{1,0:T(8,128)(2,1)} %fusion.4.refs_0_.refs_3_, bf16[72,4096]{1,0:T(8,128)(2,1)} %copy-done.2, ...), custom_call_target="tpu_custom_call" | custom-call | tf_op jit(solution)/shard_map/pack_near/pallas_call | solution.py:78
  46.9 43.0 %all_to_all.20 = bf16[16,24,4096]{2,1,0:T(8,128)(2,1)S(1)} all-to-all(bf16[16,24,4096]{2,1,0:T(8,128)(2,1)} %bitcast.48), channel_id=1, replica_groups=mesh['x'=4,'z'=8,'y'=4,'dp'=2] {'x','y'}, dimensions={0} | all-to-all | bytes 6291456 | tf_op jit(solution)/shard_map/all_to_all | solution.py:239
  90.0 0.0 copy-start
  90.0 0.6 slice_add_fusion._
  90.6 6.7 %pack_far.1 = bf16[16,5,8,4096]{3,2,1,0:T(8,128)(2,1)} custom-call(s32[8]{0:T(128)} %and_select_fusion.order_ref, bf16[8,72,4096]{2,1,0:T(8,128)(2,1)} %bitcast.39, bf16[8,72,4096]{2,1,0:T(8,128)(2,1)} %bitcast.40, bf16[8,128]{1,0:T(8,128)(2,1)} %slice_add_fusion._), custom_call_target="tpu_custom_call" | custom-call | tf_op jit(solution)/shard_map/pack_far/pallas_call | solution.py:104
  97.3 0.0 copy-done
  97.3 63.7 %all_to_all.21 = bf16[16,40,4096]{2,1,0:T(8,128)(2,1)} all-to-all(bf16[16,40,4096]{2,1,0:T(8,128)(2,1)} %bitcast.43), channel_id=1, replica_groups=mesh['x'=4,'z'=8,'y'=4,'dp'=2] {'x','y'}, dimensions={0} | all-to-all | bytes 10485760 | tf_op jit(solution)/shard_map/all_to_all | solution.py:239
  161.0 20.5 %hidden.1 = (bf16[384,768]{1,0:T(8,128)(2,1)}, bf16[640,768]{1,0:T(8,128)(2,1)}) custom-call(bf16[384,4096]{1,0:T(8,128)(2,1)} %bitcast.46, bf16[640,4096]{1,0:T(8,128)(2,1)} %bitcast.42, bf16[4096,384]{1,0:T(8,128)(2,1)} %bitcast.53, bf16[4096,384]{1,0:T(8,128)(2,1)} %collective-permute-done.refs_1_, bf16[4096,384]{1,0:T(8,128)(2,1)} %bitcast.55, ...), custom_call_target="tpu_custom_call" | custom-call | tf_op jit(solution)/shard_map/hidden/pallas_call | solution.py:210
  181.5 0.0 slice-done
  181.5 0.0 slice-done.1
  181.5 5.6 %convolution_convert_fusion = bf16[640,4096]{1,0:T(8,128)(2,1)S(1)} fusion(bf16[640,768]{1,0:T(8,128)(2,1)} %get-tuple-element.29, bf16[768,4096]{1,0:T(8,128)(2,1)S(1)} %bitcast.50), kind=kOutput, calls=%fused_computation | convolution fusion | flops 4029153280 | bytes 12517376 | tf_op jit(solution)/shard_map/dot_general | solution.py:224
  187.2 60.0 %all_to_all.22 = bf16[16,40,4096]{2,1,0:T(8,128)(2,1)} all-to-all(bf16[16,40,4096]{2,1,0:T(8,128)(2,1)S(1)} %bitcast.51), channel_id=1, replica_groups=mesh['x'=4,'z'=8,'y'=4,'dp'=2] {'x','y'}, dimensions={0} | all-to-all | bytes 10485760 | tf_op jit(solution)/shard_map/all_to_all | solution.py:239
  247.2 6.5 %mix_far.1 = bf16[8,64,4096]{2,1,0:T(8,128)(2,1)} custom-call(s32[8]{0:T(128)} %and_select_fusion.order_ref, bf16[8,72,4096]{2,1,0:T(8,128)(2,1)} %bitcast.41, bf16[16,5,8,4096]{3,2,1,0:T(8,128)(2,1)} %bitcast.44), custom_call_target="tpu_custom_call" | custom-call | tf_op jit(solution)/shard_map/mix_far/pallas_call | solution.py:135
  253.7 0.0 reduce-scatter.2.cloned.1.call-update
  253.7 1.0 copy-done.3
  254.8 5.6 %convolution_convert_fusion.1 = bf16[384,4096]{1,0:T(8,128)(2,1)S(1)} fusion(bf16[384,768]{1,0:T(8,128)(2,1)S(1)} %copy-done.3, bf16[768,4096]{1,0:T(8,128)(2,1)} %pad_maximum_fusion), kind=kOutput, calls=%fused_computation.2 | convolution fusion | flops 2417491968 | bytes 10027008 | tf_op jit(solution)/shard_map/dot_general | solution.py:224
  260.4 36.5 %all_to_all.23 = bf16[16,24,4096]{2,1,0:T(8,128)(2,1)} all-to-all(bf16[16,24,4096]{2,1,0:T(8,128)(2,1)S(1)} %bitcast.56), channel_id=1, replica_groups=mesh['x'=4,'z'=8,'y'=4,'dp'=2] {'x','y'}, dimensions={0} | all-to-all | bytes 6291456 | tf_op jit(solution)/shard_map/all_to_all | solution.py:239
  296.9 5.2 %mix_near.1 = (f32[64,4096]{1,0:T(8,128)}, bf16[64,4096]{1,0:T(8,128)(2,1)}, bf16[64,4096]{1,0:T(8,128)(2,1)}) custom-call(s32[8]{0:T(128)} %and_select_fusion.order_ref, bf16[72,4096]{1,0:T(8,128)(2,1)} %fusion.4.refs_0_.refs_3_, bf16[72,4096]{1,0:T(8,128)(2,1)} %copy-done.2, bf16[72,4096]{1,0:T(8,128)(2,1)} %copy-done.1, bf16[16,3,8,4096]{3,2,1,0:T(8,128)(2,1)} %bitcast.47), custom_call_target="tpu_custom_call" | custom-call | tf_op jit(solution)/shard_map/mix_near/pallas_call | solution.py:165
  302.1 10.5 %collective-permute-start.5 = (bf16[64,4096]{1,0:T(8,128)(2,1)}, bf16[64,4096]{1,0:T(8,128)(2,1)S(1)}, u32[]{:S(2)}, u32[]{:S(2)}) collective-permute-start(bf16[64,4096]{1,0:T(8,128)(2,1)} %get-tuple-element.35), channel_id=1, source_target_pairs={{0,56},{8,0},{16,8},{24,16},{32,24},{40,32},{48,40},{56,48},{1,57}... | collective-permute-start | bytes 1572872 | tf_op jit(solution)/shard_map/ppermute | solution.py:278
  312.6 0.0 collective-permute-start.6
  312.6 8.5 %collective-permute-done.5 = bf16[64,4096]{1,0:T(8,128)(2,1)S(1)} collective-permute-done((bf16[64,4096]{1,0:T(8,128)(2,1)}, bf16[64,4096]{1,0:T(8,128)(2,1)S(1)}, u32[]{:S(2)}, u32[]{:S(2)}) %collective-permute-start.5) | collective-permute-done | bytes 524320 | tf_op jit(solution)/shard_map/ppermute | solution.py:278
  321.2 3.3 collective-permute-done.6
  324.5 2.4 fusion.3
  (10 shorter events, 0.1 us)
Async XLA Ops:
  6.5 84.1 %all-gather.3.cloned.1.call-start = ((), (), s32[]{:S(2)}) async-start(), calls=%async_computation.6 | async-start | bytes 5308416 | tf_op jit(solution)/shard_map/all_gather | solution.py:252
  11.0 313.4 %reduce-scatter.2.cloned.1.call-start = ((), (), s32[]{:S(2)}) async-start(), calls=%async_computation.5 | async-start | bytes 4718592 | tf_op jit(solution)/shard_map/reduce_scatter | solution.py:273
  11.1 7.3 %collective-permute-start.2 = (bf16[384,4096]{1,0:T(8,128)(2,1)}, bf16[384,4096]{1,0:T(8,128)(2,1)}, u32[]{:S(2)}, u32[]{:S(2)}) collective-permute-start(bf16[384,4096]{1,0:T(8,128)(2,1)} %bitcast.57), channel_id=1, source_target_pairs={{0,1},{1,0},{2,3},{3,2},{4,5},{5,4},{6,7},{7,6},{8,9},{9,8},{10,11... | collective-permute-start | bytes 9437192 | tf_op jit(solution)/shard_map/ppermute | solution.py:258
  11.2 29.4 %collective-permute-start = (bf16[4096,384]{1,0:T(8,128)(2,1)}, bf16[4096,384]{1,0:T(8,128)(2,1)}, u32[]{:S(2)}, u32[]{:S(2)}) collective-permute-start(bf16[4096,384]{1,0:T(8,128)(2,1)} %bitcast.52), channel_id=1, source_target_pairs={{0,1},{1,0},{2,3},{3,2},{4,5},{5,4},{6,7},{7,6},{8,9},{9,8},{10,11... | collective-permute-start | bytes 9437192 | tf_op jit(solution)/shard_map/ppermute | solution.py:257
  11.7 28.9 %collective-permute-start.1 = (bf16[4096,384]{1,0:T(8,128)(2,1)}, bf16[4096,384]{1,0:T(8,128)(2,1)}, u32[]{:S(2)}, u32[]{:S(2)}) collective-permute-start(bf16[4096,384]{1,0:T(8,128)(2,1)} %bitcast.54), channel_id=1, source_target_pairs={{0,1},{1,0},{2,3},{3,2},{4,5},{5,4},{6,7},{7,6},{8,9},{9,8},{10,11... | collective-permute-start | bytes 9437192 | tf_op jit(solution)/shard_map/ppermute | solution.py:257
  11.8 25.5 %collective-permute-start.4 = (bf16[72,4096]{1,0:T(8,128)(2,1)}, bf16[72,4096]{1,0:T(8,128)(2,1)S(1)}, u32[]{:S(2)}, u32[]{:S(2)}) collective-permute-start(bf16[72,4096]{1,0:T(8,128)(2,1)} %fusion.4.refs_0_.refs_3_), channel_id=1, source_target_pairs={{0,56},{8,0},{16,8},{24,16},{32,24},{40,32},{48,40},{56,48},{1,57}... | collective-permute-start | bytes 1769480 | tf_op jit(solution)/shard_map/ppermute | solution.py:253
  17.6 22.9 %collective-permute-start.3 = (bf16[72,4096]{1,0:T(8,128)(2,1)}, bf16[72,4096]{1,0:T(8,128)(2,1)S(1)}, u32[]{:S(2)}, u32[]{:S(2)}) collective-permute-start(bf16[72,4096]{1,0:T(8,128)(2,1)} %fusion.4.refs_0_.refs_3_), channel_id=1, source_target_pairs={{0,8},{8,16},{16,24},{24,32},{32,40},{40,48},{48,56},{56,0},{1,9},... | collective-permute-start | bytes 1769480 | tf_op jit(solution)/shard_map/ppermute | solution.py:253
  37.3 3.3 copy-start.1
  40.5 0.8 copy-start.2
  90.0 7.3 %copy-start = (bf16[16,24,4096]{2,1,0:T(8,128)(2,1)}, bf16[16,24,4096]{2,1,0:T(8,128)(2,1)S(1)}, u32[]{:S(2)}) copy-start(bf16[16,24,4096]{2,1,0:T(8,128)(2,1)S(1)} %all_to_all.20) | copy-start | bytes 9437188
  97.3 84.2 %slice-start = ((s8[6291456]{0:T(1024)(128)(4,1)}), s8[4194304]{0:T(1024)(128)(4,1)S(1)}, s32[]{:S(2)}) async-start(s8[6291456]{0:T(1024)(128)(4,1)} %bitcast.49), calls=%async_computation.7 | async-start | bytes 8388608
  161.0 20.5 %slice-start.1 = ((s8[6291456]{0:T(1024)(128)(4,1)}), s8[2097152]{0:T(1024)(128)(4,1)S(1)}, s32[]{:S(2)}) async-start(s8[6291456]{0:T(1024)(128)(4,1)} %bitcast.49), calls=%async_computation.8 | async-start | bytes 4194304
  253.7 1.1 copy-start.3
  302.1 19.0 %collective-permute-start.5 = (bf16[64,4096]{1,0:T(8,128)(2,1)}, bf16[64,4096]{1,0:T(8,128)(2,1)S(1)}, u32[]{:S(2)}, u32[]{:S(2)}) collective-permute-start(bf16[64,4096]{1,0:T(8,128)(2,1)} %get-tuple-element.35), channel_id=1, source_target_pairs={{0,56},{8,0},{16,8},{24,16},{32,24},{40,32},{48,40},{56,48},{1,57}... | collective-permute-start | bytes 1572872 | tf_op jit(solution)/shard_map/ppermute | solution.py:278
  312.6 11.9 %collective-permute-start.6 = (bf16[64,4096]{1,0:T(8,128)(2,1)}, bf16[64,4096]{1,0:T(8,128)(2,1)S(1)}, u32[]{:S(2)}, u32[]{:S(2)}) collective-permute-start(bf16[64,4096]{1,0:T(8,128)(2,1)} %get-tuple-element.36), channel_id=1, source_target_pairs={{0,8},{8,16},{16,24},{24,32},{32,40},{40,48},{48,56},{56,0},{1,9},... | collective-permute-start | bytes 1572872 | tf_op jit(solution)/shard_map/ppermute | solution.py:278
Sparse Core Ops, SparseCore 0:
  11.2 68.1 all-gather.2
  253.9 53.9 reduce-scatter.1

commit v8 on v7

--- a/solution.py
+++ b/solution.py
@@ -149,7 +149,7 @@
 
 
 def mix_near_kernel(order_ref, *refs):
-    count = len(NEAR)
+    count = len(refs) // 2
     rows_ref, outs = refs[count], refs[count + 1 :]
     plane, _, capacity, width = rows_ref.shape
     for i in range(count):
@@ -158,10 +158,9 @@
         outs[i][...] = mixed(lists, rows, outs[i].shape[0]).astype(outs[i].dtype)
 
 
-def mix_near(order, blocks, rows, tok_count):
+def mix_near(order, blocks, rows, tok_count, kind):
     plane, count, capacity, width = rows.shape
     z_size = blocks[0].shape[0] - tok_count
-    kinds = [jnp.bfloat16 if offset else jnp.float32 for offset in NEAR]
     return pl.pallas_call(
         mix_near_kernel,
         grid_spec=pltpu.PrefetchScalarGridSpec(
@@ -172,52 +171,54 @@
             + [pl.BlockSpec((plane, count, capacity, STEP), lambda i, order: (0, 0, 0, i))],
             out_specs=[pl.BlockSpec((tok_count, STEP), lambda i, order: (0, i))] * count,
         ),
-        out_shape=[jax.ShapeDtypeStruct((tok_count, width), kind) for kind in kinds],
+        out_shape=[jax.ShapeDtypeStruct((tok_count, width), kind)] * count,
         name="mix_near",
     )(order, *blocks, rows)
 
 
-def hidden_kernel(near_ref, far_ref, *refs):
-    *weights, out_near, out_far, gate_near, up_near, gate_far, up_far = refs
+def hidden_kernel(own_ref, next_ref, far_ref, *refs):
+    *weights, out_near, out_far, gate_acc, up_acc = refs
     step, steps = pl.program_id(0), pl.num_programs(0)
     gate, gate_other, up, up_other = (ref[...] for ref in weights)
     gate = jnp.concatenate([gate, gate_other], axis=1)
     up = jnp.concatenate([up, up_other], axis=1)
-    parts = [(near_ref, out_near, gate_near, up_near), (far_ref, out_far, gate_far, up_far)]
-    for rows_ref, out_ref, gate_acc, up_acc in parts:
-        rows = rows_ref[...]
-
-        @pl.when(step == 0)
-        def _():
-            gate_acc[...] = dot(rows, gate)
-            up_acc[...] = dot(rows, up)
-
-        @pl.when((step > 0) & (step < steps - 1))
-        def _():
-            gate_acc[...] += dot(rows, gate)
-            up_acc[...] += dot(rows, up)
-
-        @pl.when(step == steps - 1)
-        def _():
-            gate_act = gate_acc[...] + dot(rows, gate)
-            up_act = up_acc[...] + dot(rows, up)
-            out_ref[...] = (jax.nn.silu(gate_act) * up_act).astype(out_ref.dtype)
-
-
-def hidden_of(near, far, weights):
+    rows = jnp.concatenate([own_ref[...], next_ref[...], far_ref[...]], axis=0)
+
+    @pl.when(step == 0)
+    def _():
+        gate_acc[...] = dot(rows, gate)
+        up_acc[...] = dot(rows, up)
+
+    @pl.when((step > 0) & (step < steps - 1))
+    def _():
+        gate_acc[...] += dot(rows, gate)
+        up_acc[...] += dot(rows, up)
+
+    @pl.when(step == steps - 1)
+    def _():
+        gate_act = gate_acc[...] + dot(rows, gate)
+        up_act = up_acc[...] + dot(rows, up)
+        hidden = (jax.nn.silu(gate_act) * up_act).astype(out_far.dtype)
+        near = out_near.shape[0]
+        out_near[...] = hidden[:near]
+        out_far[...] = hidden[near:]
+
+
+def hidden_of(own, beside, far, weights):
     depth, units = weights[0].shape
-    counts = [near.shape[0], far.shape[0]]
+    groups = [r.shape[0] for r in (own, beside, far)]
+    counts = [groups[0] + groups[1], groups[2]]
     return pl.pallas_call(
         hidden_kernel,
         grid=(depth // DEPTH,),
-        in_specs=[pl.BlockSpec((c, DEPTH), lambda i: (0, i)) for c in counts]
+        in_specs=[pl.BlockSpec((c, DEPTH), lambda i: (0, i)) for c in groups]
         + [pl.BlockSpec((DEPTH, units), lambda i: (i, 0))] * 4,
         out_specs=[pl.BlockSpec((c, 2 * units), lambda i: (0, 0)) for c in counts],
         out_shape=[jax.ShapeDtypeStruct((c, 2 * units), jnp.bfloat16) for c in counts],
-        scratch_shapes=[pltpu.VMEM((c, 2 * units), jnp.float32) for c in counts for _ in range(2)],
+        scratch_shapes=[pltpu.VMEM((sum(counts), 2 * units), jnp.float32)] * 2,
         compiler_params=pltpu.CompilerParams(vmem_limit_bytes=56 << 20),
         name="hidden",
-    )(near, far, *weights)
+    )(own, beside, far, *weights)
 
 
 def dot(a, b):
@@ -243,28 +244,36 @@
         return rows.reshape(-1, model_width)
 
     offsets = [*NEAR, *(d for d in range(2, z_size - 1))]
-    near_count, far_count = len(NEAR), z_size - len(NEAR)
+    far_count = z_size - len(NEAR)
     order = jnp.stack([my_z + d for d in offsets]) % z_size
 
     table = slot_table(routes, gate_probs, sizes, capacity).reshape(z_size, -1)
     table = jnp.pad(table, ((0, 0), (0, model_width - table.shape[1])))
     block = jnp.concatenate([tokens, table], axis=0)
     blocks = lax.all_gather(block, "z", axis=0, tiled=False)
-    near_blocks = [block, lax.ppermute(block, "z", up_ring), lax.ppermute(block, "z", down_ring)]
+    own_blocks = [block]
+    next_blocks = [lax.ppermute(block, "z", up_ring), lax.ppermute(block, "z", down_ring)]
 
     swap = [(0, 1), (1, 0)]
     weights = [gate_w[0], up_w[0]]
     weights = [v for w in weights for v in (w, lax.ppermute(w, "dp", swap))]
-    w_down = jnp.concatenate([down_w[0], lax.ppermute(down_w[0], "dp", swap)], axis=0)
-
-    weights, w_down, near_blocks, order = lax.optimization_barrier(
-        (weights, w_down, near_blocks, order)
+    down_other = lax.ppermute(down_w[0], "dp", swap)
+
+    def packed(blocks):
+        return pack_near(order, blocks, tok_count, plane, capacity)
+
+    own = flat(in_plane(packed(own_blocks), len(own_blocks)))
+    after = own[:8, :128] + 1
+    next_blocks, weights, down_other, order, after = lax.optimization_barrier(
+        (next_blocks, weights, down_other, order, after)
     )
-    near = flat(in_plane(pack_near(order, near_blocks, tok_count, plane, capacity), near_count))
-    after = near[:8, :128] + 1
+    beside = flat(in_plane(packed(next_blocks), len(next_blocks)))
+    after, down_other = lax.optimization_barrier((after + beside[:8, :128], down_other))
+    w_down = jnp.concatenate([down_w[0], down_other], axis=0)
+    after, w_down = lax.optimization_barrier((after, w_down))
     far = pack_far(order, blocks, after, tok_count, plane, capacity)
     far = flat(in_plane(far, far_count))
-    hidden_near, hidden_far = hidden_of(near, far, weights)
+    hidden_near, hidden_far = hidden_of(own, beside, far, weights)
 
     answers = dot(hidden_far, w_down).astype(jnp.bfloat16)
     answers = in_plane(answers, far_count)
@@ -273,10 +282,16 @@
     total = lax.psum_scatter(partial, "z", scatter_dimension=0, tiled=True)[0]
 
     answers = dot(hidden_near, w_down).astype(jnp.bfloat16)
-    answers = in_plane(answers, near_count)
-    own, under, over = mix_near(order, near_blocks, answers, tok_count)
+    split = own.shape[0]
+    answers_own, answers = answers[:split], answers[split:]
+    answers, answers_own = lax.optimization_barrier((answers, answers_own))
+    answers = in_plane(answers, len(next_blocks))
+    under, over = mix_near(order, next_blocks, answers, tok_count, jnp.bfloat16)
+    under, over, answers_own = lax.optimization_barrier((under, over, answers_own))
     under, over = lax.ppermute(under, "z", down_ring), lax.ppermute(over, "z", up_ring)
-    total = total.astype(jnp.float32) + own + under.astype(jnp.float32) + over.astype(jnp.float32)
+    answers_own = in_plane(answers_own, len(own_blocks))
+    (mine,) = mix_near(order, own_blocks, answers_own, tok_count, jnp.float32)
+    total = total.astype(jnp.float32) + mine + under.astype(jnp.float32) + over.astype(jnp.float32)
     return total.astype(jnp.bfloat16)
 
 

time: 335 us -> 348 us (1.039)
  waiting for transfers between devices: 27.8 us -> 40.3 us
  blocking collectives: 203 us -> 191 us
  Pallas kernels: 44.5 us -> 51 us
  starting transfers between devices: 17.1 us -> 21.6 us
    all_to_all x0 -> x2, waiting for transfers between devices: none -> 20.5 us  [in_plane(): lax.all_to_all(rows, ('x', 'y'), split_axis=0, concat_axis=0, tiled=True)]
    all_to_all x0 -> x2, starting transfers between devices: none -> 12.9 us  [in_plane(): lax.all_to_all(rows, ('x', 'y'), split_axis=0, concat_axis=0, tiled=True)]
    all_to_all x4, blocking collectives: 203 us -> 191 us  [in_plane(): lax.all_to_all(rows, ('x', 'y'), split_axis=0, concat_axis=0, tiled=True)]
    ppermute x1, starting transfers between devices: 10.5 us -> 0.01 us  [body(): lax.ppermute(under, 'z', down_ring)]
    ppermute x1, waiting for transfers between devices: 8.54 us -> 0.01 us  [body(): lax.ppermute(under, 'z', down_ring)]
    pallas_call x1 -> x2, Pallas kernels: 5.2 us -> 9.17 us  [mix_near(): pl.pallas_call(mix_near_kernel, grid_spec=pltpu.PrefetchScalarGridSpec(nu...]
    pallas_call x1 -> x2, Pallas kernels: 5.56 us -> 9.46 us  [pack_near(): pl.pallas_call(pack_near_kernel, grid_spec=pltpu.PrefetchScalarGridSpec(n...]
  transfers between devices with their start and end apart: 9 -> 11, of which waited for: 4 -> 4; matrix products, arithmetic and copies ran while one was open for 4% -> 4% of each run, Pallas kernels for 3% -> 5%
where the time goes in v8:
time: 348 us; the launch traced here: 346 us
  blocking collectives  191 us (55%)
  Pallas kernels  51 us (15%)
  waiting for transfers between devices  40.3 us (12%)
  starting transfers between devices  21.6 us (6%)
  between operations  13.5 us (4%)
  other arithmetic  11.9 us (3%)
  matrix products  11.3 us (3%)
  local copies, waits for them, and re-layouts  5.66 us (2%)
    all_to_all x4, blocking collectives, in_plane(): lax.all_to_all(rows, ('x', 'y'), split_axis=0, concat_axis=0, tiled=True)  191 us
    all_to_all x2, waiting for transfers between devices, in_plane(): lax.all_to_all(rows, ('x', 'y'), split_axis=0, concat_axis=0, tiled=True)  20.5 us
    pallas_call x1, Pallas kernels, hidden_of(): pl.pallas_call(hidden_kernel, grid=(depth // DEPTH,), in_specs=[pl.BlockS...  19.1 us
    ppermute x1, waiting for transfers between devices, body(): lax.ppermute(block, 'z', down_ring)  16.1 us
    all_to_all x2, starting transfers between devices, in_plane(): lax.all_to_all(rows, ('x', 'y'), split_axis=0, concat_axis=0, tiled=True)  12.9 us
    dot_general x2, matrix products, dot(): return jnp.dot(a, b, preferred_element_type=jnp.float32)  11.3 us
    pallas_call x2, Pallas kernels, pack_near(): pl.pallas_call(pack_near_kernel, grid_spec=pltpu.PrefetchScalarGridSpec(n...  9.46 us
    pallas_call x2, Pallas kernels, mix_near(): pl.pallas_call(mix_near_kernel, grid_spec=pltpu.PrefetchScalarGridSpec(nu...  9.17 us
  transfers between devices with their start and end apart: 11, of which 4 were waited for; matrix products, arithmetic and copies ran while one was open for 4% of the time, Pallas kernels for 5%

profile of v8, /device:TPU:2, one launch (start us, length us, event | category | flops | bytes accessed | tf_op | source)
XLA Modules:
  0.0 345.7 jit_solution(4979621564836610134)
XLA Ops:
  6.5 0.8 reshape.168
  7.3 0.8 broadcast_in_dim.27
  8.1 0.3 convert_reduce_fusion
  8.4 0.6 select_reduce_fusion.1
  9.1 1.9 fusion.4.refs_0_.refs_1_
  11.0 0.0 all-gather.3.cloned.1.call-update
  11.0 0.1 collective-permute-start.2
  11.2 0.5 collective-permute-start.3
  11.6 0.1 collective-permute-start.4
  11.8 0.1 stack.45
  11.8 0.5 and_select_fusion.order_ref
  12.4 4.5 %pack_near.2 = bf16[16,1,8,4096]{3,2,1,0:T(8,128)(2,1)} custom-call(s32[8]{0:T(128)} %and_select_fusion.order_ref, bf16[72,4096]{1,0:T(8,128)(2,1)} %fusion.4.refs_0_.refs_1_, bf16[72,4096]{1,0:T(8,128)(2,1)} %fusion.4.refs_0_.refs_1_), custom_call_target="tpu_custom_call" | custom-call | tf_op jit(solution)/shard_map/pack_near/pallas_call | solution.py:78
  16.8 7.5 %all-to-all-start = ((bf16[16,8,4096]{2,1,0:T(8,128)(2,1)}), bf16[16,8,4096]{2,1,0:T(8,128)(2,1)S(1)}, u32[]{:S(2)}, u32[]{:S(2)}) async-start(bf16[16,8,4096]{2,1,0:T(8,128)(2,1)} %bitcast.59), calls=%async_computation | async-start | bytes 2097152 | tf_op jit(solution)/shard_map/all_to_all | solution.py:240
  24.3 0.0 reduce-scatter.2.cloned.1.call-start
  24.4 5.9 %collective-permute-start.1 = (bf16[72,4096]{1,0:T(8,128)(2,1)S(1)}, bf16[72,4096]{1,0:T(8,128)(2,1)S(1)}, u32[]{:S(2)}, u32[]{:S(2)}) collective-permute-start(bf16[72,4096]{1,0:T(8,128)(2,1)S(1)} %copy-done), channel_id=1, source_target_pairs={{0,56},{8,0},{16,8},{24,16},{32,24},{40,32},{48,40},{56,48},{1,57}... | collective-permute-start | bytes 1769480 | tf_op jit(solution)/shard_map/ppermute | solution.py:255
  30.3 0.0 collective-permute-start
  30.3 9.8 %all-to-all-done = bf16[16,8,4096]{2,1,0:T(8,128)(2,1)S(1)} async-done(((bf16[16,8,4096]{2,1,0:T(8,128)(2,1)}), bf16[16,8,4096]{2,1,0:T(8,128)(2,1)S(1)}, u32[]{:S(2)}, u32[]{:S(2)}) %all-to-all-start) | async-done | bytes 1048608 | tf_op jit(solution)/shard_map/all_to_all | solution.py:240
  40.1 16.1 %collective-permute-done.1.refs_1_.refs_3_ = bf16[72,4096]{1,0:T(8,128)(2,1)S(1)} collective-permute-done((bf16[72,4096]{1,0:T(8,128)(2,1)S(1)}, bf16[72,4096]{1,0:T(8,128)(2,1)S(1)}, u32[]{:S(2)}, u32[]{:S(2)}) %collective-permute-start.1) | collective-permute-done | bytes 589856 | tf_op jit(solution)/shard_map/ppermute | solution.py:255
  56.2 3.6 %collective-permute-done.refs_0_.refs_2_ = bf16[72,4096]{1,0:T(8,128)(2,1)S(1)} collective-permute-done((bf16[72,4096]{1,0:T(8,128)(2,1)S(1)}, bf16[72,4096]{1,0:T(8,128)(2,1)S(1)}, u32[]{:S(2)}, u32[]{:S(2)}) %collective-permute-start) | collective-permute-done | bytes 589856 | tf_op jit(solution)/shard_map/ppermute | solution.py:255
  59.8 0.0 collective-permute-done.2.refs_1_
  59.8 0.0 collective-permute-done.3.refs_3_
  59.8 0.0 collective-permute-done.4
  59.9 0.8 copy-done.3
  60.7 5.0 %pack_near.3 = bf16[16,2,8,4096]{3,2,1,0:T(8,128)(2,1)} custom-call(s32[8]{0:T(128)} %and_select_fusion.order_ref, bf16[72,4096]{1,0:T(8,128)(2,1)} %copy-done.3, bf16[72,4096]{1,0:T(8,128)(2,1)} %copy-done.2, bf16[72,4096]{1,0:T(8,128)(2,1)} %copy-done.3, bf16[72,4096]{1,0:T(8,128)(2,1)} %copy-done.2), custom_call_target="tpu_custom_call" | custom-call | tf_op jit(solution)/shard_map/pack_near/pallas_call | solution.py:78
  65.7 32.6 %all_to_all.30 = bf16[16,16,4096]{2,1,0:T(8,128)(2,1)S(1)} all-to-all(bf16[16,16,4096]{2,1,0:T(8,128)(2,1)} %bitcast.53), channel_id=1, replica_groups=mesh['x'=4,'z'=8,'y'=4,'dp'=2] {'x','y'}, dimensions={0} | all-to-all | bytes 4194304 | tf_op jit(solution)/shard_map/all_to_all | solution.py:240
  98.3 0.6 slice_add_fusion._
  99.0 5.4 %pad_maximum_fusion = bf16[768,4096]{1,0:T(8,128)(2,1)} fusion(bf16[384,4096]{1,0:T(8,128)(2,1)} %collective-permute-done.4, bf16[384,4096]{1,0:T(8,128)(2,1)S(1)} %bitcast.66), kind=kLoop, calls=%fused_computation.1 | loop fusion | flops 12582912 | bytes 12582912 | tf_op jit(solution)/shard_map/concatenate | solution.py:272
  104.4 6.7 %pack_far.1 = bf16[16,5,8,4096]{3,2,1,0:T(8,128)(2,1)} custom-call(s32[8]{0:T(128)} %and_select_fusion.order_ref, bf16[8,72,4096]{2,1,0:T(8,128)(2,1)} %bitcast.43, bf16[8,72,4096]{2,1,0:T(8,128)(2,1)} %bitcast.44, bf16[8,128]{1,0:T(8,128)(2,1)} %slice_add_fusion._), custom_call_target="tpu_custom_call" | custom-call | tf_op jit(solution)/shard_map/pack_far/pallas_call | solution.py:104
  111.1 64.6 %all_to_all.31 = bf16[16,40,4096]{2,1,0:T(8,128)(2,1)} all-to-all(bf16[16,40,4096]{2,1,0:T(8,128)(2,1)} %bitcast.47), channel_id=1, replica_groups=mesh['x'=4,'z'=8,'y'=4,'dp'=2] {'x','y'}, dimensions={0} | all-to-all | bytes 10485760 | tf_op jit(solution)/shard_map/all_to_all | solution.py:240
  175.7 19.1 %hidden.1 = (bf16[384,768]{1,0:T(8,128)(2,1)}, bf16[640,768]{1,0:T(8,128)(2,1)}) custom-call(bf16[128,4096]{1,0:T(8,128)(2,1)} %bitcast.58, bf16[256,4096]{1,0:T(8,128)(2,1)} %bitcast.50, bf16[640,4096]{1,0:T(8,128)(2,1)} %bitcast.46, bf16[4096,384]{1,0:T(8,128)(2,1)} %bitcast.62, bf16[4096,384]{1,0:T(8,128)(2,1)} %collective-permute-done.2.refs_1_, ...), custom_call_target="tpu_custom_call" | custom-call | tf_op jit(solution)/shard_map/hidden/pallas_call | solution.py:211
  194.8 5.6 %convolution_convert_fusion = bf16[640,4096]{1,0:T(8,128)(2,1)S(1)} fusion(bf16[640,768]{1,0:T(8,128)(2,1)} %get-tuple-element.41, bf16[768,4096]{1,0:T(8,128)(2,1)S(1)} %bitcast.55), kind=kOutput, calls=%fused_computation | convolution fusion | flops 4029153280 | bytes 12517376 | tf_op jit(solution)/shard_map/dot_general | solution.py:225
  200.5 62.3 %all_to_all.32 = bf16[16,40,4096]{2,1,0:T(8,128)(2,1)} all-to-all(bf16[16,40,4096]{2,1,0:T(8,128)(2,1)S(1)} %bitcast.56), channel_id=1, replica_groups=mesh['x'=4,'z'=8,'y'=4,'dp'=2] {'x','y'}, dimensions={0} | all-to-all | bytes 10485760 | tf_op jit(solution)/shard_map/all_to_all | solution.py:240
  262.8 6.5 %mix_far.1 = bf16[8,64,4096]{2,1,0:T(8,128)(2,1)} custom-call(s32[8]{0:T(128)} %and_select_fusion.order_ref, bf16[8,72,4096]{2,1,0:T(8,128)(2,1)} %bitcast.45, bf16[16,5,8,4096]{3,2,1,0:T(8,128)(2,1)} %bitcast.48), custom_call_target="tpu_custom_call" | custom-call | tf_op jit(solution)/shard_map/mix_far/pallas_call | solution.py:135
  269.3 0.0 reduce-scatter.2.cloned.1.call-update
  269.4 1.0 copy-done.7
  270.4 5.6 %convolution_convert_fusion.1 = bf16[384,4096]{1,0:T(8,128)(2,1)S(1)} fusion(bf16[384,768]{1,0:T(8,128)(2,1)S(1)} %copy-done.7, bf16[768,4096]{1,0:T(8,128)(2,1)} %pad_maximum_fusion), kind=kOutput, calls=%fused_computation.2 | convolution fusion | flops 2417491968 | bytes 10027008 | tf_op jit(solution)/shard_map/dot_general | solution.py:225
  276.0 1.1 slice.19
  277.1 0.1 slice.18
  277.2 31.0 %all_to_all.33 = bf16[16,16,4096]{2,1,0:T(8,128)(2,1)} all-to-all(bf16[16,16,4096]{2,1,0:T(8,128)(2,1)S(1)} %bitcast.52), channel_id=1, replica_groups=mesh['x'=4,'z'=8,'y'=4,'dp'=2] {'x','y'}, dimensions={0} | all-to-all | bytes 4194304 | tf_op jit(solution)/shard_map/all_to_all | solution.py:240
  308.2 4.7 %mix_near.2 = (bf16[64,4096]{1,0:T(8,128)(2,1)}, bf16[64,4096]{1,0:T(8,128)(2,1)}) custom-call(s32[8]{0:T(128)} %and_select_fusion.order_ref, bf16[72,4096]{1,0:T(8,128)(2,1)} %copy-done.3, bf16[72,4096]{1,0:T(8,128)(2,1)} %copy-done.2, bf16[16,2,8,4096]{3,2,1,0:T(8,128)(2,1)} %bitcast.51), custom_call_target="tpu_custom_call" | custom-call | tf_op jit(solution)/shard_map/mix_near/pallas_call | solution.py:164
  312.9 5.4 %all-to-all-start.5 = ((bf16[16,8,4096]{2,1,0:T(8,128)(2,1)}), bf16[16,8,4096]{2,1,0:T(8,128)(2,1)S(1)}, u32[]{:S(2)}, u32[]{:S(2)}) async-start(bf16[16,8,4096]{2,1,0:T(8,128)(2,1)} %bitcast.29), calls=%async_computation.6 | async-start | bytes 2097152 | tf_op jit(solution)/shard_map/all_to_all | solution.py:240
  318.3 2.0 collective-permute-start.6
  320.3 10.7 %all-to-all-done.5 = bf16[16,8,4096]{2,1,0:T(8,128)(2,1)S(1)} async-done(((bf16[16,8,4096]{2,1,0:T(8,128)(2,1)}), bf16[16,8,4096]{2,1,0:T(8,128)(2,1)S(1)}, u32[]{:S(2)}, u32[]{:S(2)}) %all-to-all-start.5) | async-done | bytes 1048608 | tf_op jit(solution)/shard_map/all_to_all | solution.py:240
  331.0 1.0 copy-done.5
  332.0 4.5 %mix_near.3 = f32[64,4096]{1,0:T(8,128)} custom-call(s32[8]{0:T(128)} %and_select_fusion.order_ref, bf16[72,4096]{1,0:T(8,128)(2,1)} %fusion.4.refs_0_.refs_1_, bf16[16,1,8,4096]{3,2,1,0:T(8,128)(2,1)} %bitcast.60), custom_call_target="tpu_custom_call" | custom-call | tf_op jit(solution)/shard_map/mix_near/pallas_call | solution.py:164
  336.5 0.0 collective-permute-done.5
  336.5 0.0 reduce-scatter.2.cloned.1.call-done
  336.5 2.4 fusion.3
  (27 shorter events, 0.1 us)
Async XLA Ops:
  6.5 97.9 %all-gather.3.cloned.1.call-start = ((), (), s32[]{:S(2)}) async-start(), calls=%async_computation.8 | async-start | bytes 5308416 | tf_op jit(solution)/shard_map/all_gather | solution.py:253
  11.0 13.3 %copy-start = (bf16[72,4096]{1,0:T(8,128)(2,1)S(1)}, bf16[72,4096]{1,0:T(8,128)(2,1)}, u32[]{:S(2)}) copy-start(bf16[72,4096]{1,0:T(8,128)(2,1)} %fusion.4.refs_0_.refs_1_) | copy-start | bytes 1769476
  11.0 48.8 %collective-permute-start.2 = (bf16[4096,384]{1,0:T(8,128)(2,1)}, bf16[4096,384]{1,0:T(8,128)(2,1)}, u32[]{:S(2)}, u32[]{:S(2)}) collective-permute-start(bf16[4096,384]{1,0:T(8,128)(2,1)} %bitcast.61), channel_id=1, source_target_pairs={{0,1},{1,0},{2,3},{3,2},{4,5},{5,4},{6,7},{7,6},{8,9},{9,8},{10,11... | collective-permute-start | bytes 9437192 | tf_op jit(solution)/shard_map/ppermute | solution.py:259
  11.2 48.7 %collective-permute-start.3 = (bf16[4096,384]{1,0:T(8,128)(2,1)}, bf16[4096,384]{1,0:T(8,128)(2,1)}, u32[]{:S(2)}, u32[]{:S(2)}) collective-permute-start(bf16[4096,384]{1,0:T(8,128)(2,1)} %bitcast.63), channel_id=1, source_target_pairs={{0,1},{1,0},{2,3},{3,2},{4,5},{5,4},{6,7},{7,6},{8,9},{9,8},{10,11... | collective-permute-start | bytes 9437192 | tf_op jit(solution)/shard_map/ppermute | solution.py:259
  11.6 48.2 %collective-permute-start.4 = (bf16[384,4096]{1,0:T(8,128)(2,1)}, bf16[384,4096]{1,0:T(8,128)(2,1)}, u32[]{:S(2)}, u32[]{:S(2)}) collective-permute-start(bf16[384,4096]{1,0:T(8,128)(2,1)} %bitcast.65), channel_id=1, source_target_pairs={{0,1},{1,0},{2,3},{3,2},{4,5},{5,4},{6,7},{7,6},{8,9},{9,8},{10,11... | collective-permute-start | bytes 9437192 | tf_op jit(solution)/shard_map/ppermute | solution.py:260
  16.8 23.3 %all-to-all-start = ((bf16[16,8,4096]{2,1,0:T(8,128)(2,1)}), bf16[16,8,4096]{2,1,0:T(8,128)(2,1)S(1)}, u32[]{:S(2)}, u32[]{:S(2)}) async-start(bf16[16,8,4096]{2,1,0:T(8,128)(2,1)} %bitcast.59), calls=%async_computation | async-start | bytes 2097152 | tf_op jit(solution)/shard_map/all_to_all | solution.py:240
  24.3 312.2 %reduce-scatter.2.cloned.1.call-start = ((), (), s32[]{:S(2)}) async-start(), calls=%async_computation.7 | async-start | bytes 4718592 | tf_op jit(solution)/shard_map/reduce_scatter | solution.py:282
  24.4 31.9 %collective-permute-start.1 = (bf16[72,4096]{1,0:T(8,128)(2,1)S(1)}, bf16[72,4096]{1,0:T(8,128)(2,1)S(1)}, u32[]{:S(2)}, u32[]{:S(2)}) collective-permute-start(bf16[72,4096]{1,0:T(8,128)(2,1)S(1)} %copy-done), channel_id=1, source_target_pairs={{0,56},{8,0},{16,8},{24,16},{32,24},{40,32},{48,40},{56,48},{1,57}... | collective-permute-start | bytes 1769480 | tf_op jit(solution)/shard_map/ppermute | solution.py:255
  30.3 29.6 %collective-permute-start = (bf16[72,4096]{1,0:T(8,128)(2,1)S(1)}, bf16[72,4096]{1,0:T(8,128)(2,1)S(1)}, u32[]{:S(2)}, u32[]{:S(2)}) collective-permute-start(bf16[72,4096]{1,0:T(8,128)(2,1)S(1)} %copy-done), channel_id=1, source_target_pairs={{0,8},{8,16},{16,24},{24,32},{32,40},{40,48},{48,56},{56,0},{1,9},... | collective-permute-start | bytes 1769480 | tf_op jit(solution)/shard_map/ppermute | solution.py:255
  40.1 25.6 %copy-start.4 = (bf16[16,8,4096]{2,1,0:T(8,128)(2,1)}, bf16[16,8,4096]{2,1,0:T(8,128)(2,1)S(1)}, u32[]{:S(2)}) copy-start(bf16[16,8,4096]{2,1,0:T(8,128)(2,1)S(1)} %all-to-all-done) | copy-start | bytes 3145732
  56.2 3.6 %copy-start.2 = (bf16[72,4096]{1,0:T(8,128)(2,1)}, bf16[72,4096]{1,0:T(8,128)(2,1)S(1)}, u32[]{:S(2)}) copy-start(bf16[72,4096]{1,0:T(8,128)(2,1)S(1)} %collective-permute-done.1.refs_1_.refs_3_) | copy-start | bytes 1769476
  59.8 0.8 copy-start.3
  65.7 33.3 %copy-start.6 = (bf16[1,384,4096]{2,1,0:T(8,128)(2,1)S(1)}, bf16[1,384,4096]{2,1,0:T(8,128)(2,1)}, u32[]{:S(2)}) copy-start(bf16[1,384,4096]{2,1,0:T(8,128)(2,1)} %param.11) | copy-start | bytes 9437188
  98.3 6.1 %copy-start.1 = (bf16[16,16,4096]{2,1,0:T(8,128)(2,1)}, bf16[16,16,4096]{2,1,0:T(8,128)(2,1)S(1)}, u32[]{:S(2)}) copy-start(bf16[16,16,4096]{2,1,0:T(8,128)(2,1)S(1)} %all_to_all.30) | copy-start | bytes 6291460
  111.1 83.7 %slice-start = ((s8[6291456]{0:T(1024)(128)(4,1)}), s8[4194304]{0:T(1024)(128)(4,1)S(1)}, s32[]{:S(2)}) async-start(s8[6291456]{0:T(1024)(128)(4,1)} %bitcast.54), calls=%async_computation.9 | async-start | bytes 8388608
  175.7 19.1 %slice-start.1 = ((s8[6291456]{0:T(1024)(128)(4,1)}), s8[2097152]{0:T(1024)(128)(4,1)S(1)}, s32[]{:S(2)}) async-start(s8[6291456]{0:T(1024)(128)(4,1)} %bitcast.54), calls=%async_computation.10 | async-start | bytes 4194304
  269.3 1.1 copy-start.7
  312.9 18.1 %all-to-all-start.5 = ((bf16[16,8,4096]{2,1,0:T(8,128)(2,1)}), bf16[16,8,4096]{2,1,0:T(8,128)(2,1)S(1)}, u32[]{:S(2)}, u32[]{:S(2)}) async-start(bf16[16,8,4096]{2,1,0:T(8,128)(2,1)} %bitcast.29), calls=%async_computation.6 | async-start | bytes 2097152 | tf_op jit(solution)/shard_map/all_to_all | solution.py:240
  318.3 18.2 %collective-permute-start.5 = (bf16[64,4096]{1,0:T(8,128)(2,1)}, bf16[64,4096]{1,0:T(8,128)(2,1)S(1)}, u32[]{:S(2)}, u32[]{:S(2)}) collective-permute-start(bf16[64,4096]{1,0:T(8,128)(2,1)} %get-tuple-element.51), channel_id=1, source_target_pairs={{0,56},{8,0},{16,8},{24,16},{32,24},{40,32},{48,40},{56,48},{1,57}... | collective-permute-start | bytes 1572872 | tf_op jit(solution)/shard_map/ppermute | solution.py:291
  318.3 18.2 %collective-permute-start.6 = (bf16[64,4096]{1,0:T(8,128)(2,1)}, bf16[64,4096]{1,0:T(8,128)(2,1)S(1)}, u32[]{:S(2)}, u32[]{:S(2)}) collective-permute-start(bf16[64,4096]{1,0:T(8,128)(2,1)} %get-tuple-element.52), channel_id=1, source_target_pairs={{0,8},{8,16},{16,24},{24,32},{32,40},{40,48},{48,56},{56,0},{1,9},... | collective-permute-start | bytes 1572872 | tf_op jit(solution)/shard_map/ppermute | solution.py:291
  331.0 1.0 copy-start.5
Sparse Core Ops, SparseCore 0:
  11.2 75.3 all-gather.2
  269.5 50.4 reduce-scatter.1

commit v9 on v7

--- a/solution.py
+++ b/solution.py
@@ -12,7 +12,9 @@
 DEPTH = 512
 STEP = 1024
 LISTS = 512
-NEAR = (0, -1, 1)
+NEAR = (0,)
+ARRIVE = (2048, 2048)
+LEAVE = (2048, 2048)
 
 
 def slot_table(routes, gate_probs, sizes, capacity):
@@ -98,7 +100,7 @@
         out_ref[:, i] = rows.reshape(plane, capacity, width)
 
 
-def pack_far(order, blocks, after, tok_count, plane, capacity):
+def pack_far(order, listed, blocks, after, tok_count, plane, capacity):
     z_size, _, width = blocks.shape
     count = z_size - len(NEAR)
     return pl.pallas_call(
@@ -115,7 +117,7 @@
         ),
         out_shape=jax.ShapeDtypeStruct((plane, count, capacity, width), jnp.bfloat16),
         name="pack_far",
-    )(order, blocks, blocks, after)
+    )(order, listed, blocks, after)
 
 
 def mix_far_kernel(order_ref, lists_ref, rows_ref, out_ref):
@@ -129,9 +131,9 @@
         out_ref[src] = mixed(lists, rows, out_ref.shape[1]).astype(out_ref.dtype)
 
 
-def mix_far(order, blocks, rows, tok_count):
+def mix_far(order, listed, rows, tok_count):
     plane, count, capacity, width = rows.shape
-    z_size = blocks.shape[0]
+    z_size = listed.shape[0]
     return pl.pallas_call(
         mix_far_kernel,
         grid_spec=pltpu.PrefetchScalarGridSpec(
@@ -145,7 +147,7 @@
         ),
         out_shape=jax.ShapeDtypeStruct((z_size, tok_count, width), jnp.bfloat16),
         name="mix_far",
-    )(order, blocks, rows)
+    )(order, listed, rows)
 
 
 def mix_near_kernel(order_ref, *refs):
@@ -177,47 +179,66 @@
     )(order, *blocks, rows)
 
 
-def hidden_kernel(near_ref, far_ref, *refs):
-    *weights, out_near, out_far, gate_near, up_near, gate_far, up_far = refs
+def hidden_kernel(own_ref, first_ref, second_ref, *refs, split):
+    *weights, out_own, out_far, gate_acc, up_acc = refs
     step, steps = pl.program_id(0), pl.num_programs(0)
-    gate, gate_other, up, up_other = (ref[...] for ref in weights)
-    gate = jnp.concatenate([gate, gate_other], axis=1)
-    up = jnp.concatenate([up, up_other], axis=1)
-    parts = [(near_ref, out_near, gate_near, up_near), (far_ref, out_far, gate_far, up_far)]
-    for rows_ref, out_ref, gate_acc, up_acc in parts:
-        rows = rows_ref[...]
-
-        @pl.when(step == 0)
-        def _():
-            gate_acc[...] = dot(rows, gate)
-            up_acc[...] = dot(rows, up)
-
-        @pl.when((step > 0) & (step < steps - 1))
-        def _():
-            gate_acc[...] += dot(rows, gate)
-            up_acc[...] += dot(rows, up)
-
-        @pl.when(step == steps - 1)
-        def _():
-            gate_act = gate_acc[...] + dot(rows, gate)
-            up_act = up_acc[...] + dot(rows, up)
-            out_ref[...] = (jax.nn.silu(gate_act) * up_act).astype(out_ref.dtype)
-
-
-def hidden_of(near, far, weights):
+
+    def products(far_ref):
+        gate, gate_other, up, up_other = (ref[...] for ref in weights)
+        gate = jnp.concatenate([gate, gate_other], axis=1)
+        up = jnp.concatenate([up, up_other], axis=1)
+        rows = jnp.concatenate([own_ref[...], far_ref[...]], axis=0)
+        return dot(rows, gate), dot(rows, up)
+
+    @pl.when(step == 0)
+    def _():
+        gate_acc[...], up_acc[...] = products(first_ref)
+
+    @pl.when((step > 0) & (step < split))
+    def _():
+        gate, up = products(first_ref)
+        gate_acc[...] += gate
+        up_acc[...] += up
+
+    @pl.when((step >= split) & (step < steps - 1))
+    def _():
+        gate, up = products(second_ref)
+        gate_acc[...] += gate
+        up_acc[...] += up
+
+    @pl.when(step == steps - 1)
+    def _():
+        gate, up = products(second_ref)
+        hidden = jax.nn.silu(gate_acc[...] + gate) * (up_acc[...] + up)
+        count = out_own.shape[0]
+        out_own[...] = hidden[:count].astype(out_own.dtype)
+        out_far[...] = hidden[count:].astype(out_far.dtype)
+
+
+def hidden_of(own, first, second, weights):
     depth, units = weights[0].shape
-    counts = [near.shape[0], far.shape[0]]
-    return pl.pallas_call(
-        hidden_kernel,
+    counts = [own.shape[0], first.shape[0]]
+    split = first.shape[1] // DEPTH
+    return pl.pallas_call(
+        functools.partial(hidden_kernel, split=split),
         grid=(depth // DEPTH,),
-        in_specs=[pl.BlockSpec((c, DEPTH), lambda i: (0, i)) for c in counts]
+        in_specs=[
+            pl.BlockSpec((counts[0], DEPTH), lambda i: (0, i)),
+            pl.BlockSpec((counts[1], DEPTH), lambda i: (0, jnp.minimum(i, split - 1))),
+            pl.BlockSpec((counts[1], DEPTH), lambda i: (0, jnp.maximum(i - split, 0))),
+        ]
         + [pl.BlockSpec((DEPTH, units), lambda i: (i, 0))] * 4,
         out_specs=[pl.BlockSpec((c, 2 * units), lambda i: (0, 0)) for c in counts],
         out_shape=[jax.ShapeDtypeStruct((c, 2 * units), jnp.bfloat16) for c in counts],
-        scratch_shapes=[pltpu.VMEM((c, 2 * units), jnp.float32) for c in counts for _ in range(2)],
+        scratch_shapes=[pltpu.VMEM((sum(counts), 2 * units), jnp.float32)] * 2,
         compiler_params=pltpu.CompilerParams(vmem_limit_bytes=56 << 20),
         name="hidden",
-    )(near, far, *weights)
+    )(own, first, second, *weights)
+
+
+def cuts(widths):
+    ends = np.cumsum(widths)
+    return [slice(int(end) - width, int(end)) for width, end in zip(widths, ends, strict=True)]
 
 
 def dot(a, b):
@@ -231,52 +252,58 @@
     tok_count, model_width = tokens.shape
     capacity = 2 * tok_count * routes.shape[1] // (plane * z_size)
     my_z = lax.axis_index("z")
-    up_ring = [(i, (i + 1) % z_size) for i in range(z_size)]
-    down_ring = [(i, (i - 1) % z_size) for i in range(z_size)]
 
     def in_plane(rows, count):
-        rows = rows.reshape(plane, count * capacity, model_width)
+        width = rows.shape[-1]
+        rows = rows.reshape(plane, count * capacity, width)
         rows = lax.all_to_all(rows, ("x", "y"), split_axis=0, concat_axis=0, tiled=True)
-        return rows.reshape(plane, count, capacity, model_width)
+        return rows.reshape(plane, count, capacity, width)
 
     def flat(rows):
-        return rows.reshape(-1, model_width)
-
-    offsets = [*NEAR, *(d for d in range(2, z_size - 1))]
-    near_count, far_count = len(NEAR), z_size - len(NEAR)
-    order = jnp.stack([my_z + d for d in offsets]) % z_size
+        return rows.reshape(-1, rows.shape[-1])
+
+    own_count, far_count = len(NEAR), z_size - len(NEAR)
+    order = jnp.stack([my_z + d for d in range(z_size)]) % z_size
+    into, back = cuts(ARRIVE), cuts(LEAVE)
 
     table = slot_table(routes, gate_probs, sizes, capacity).reshape(z_size, -1)
-    table = jnp.pad(table, ((0, 0), (0, model_width - table.shape[1])))
-    block = jnp.concatenate([tokens, table], axis=0)
-    blocks = lax.all_gather(block, "z", axis=0, tiled=False)
-    near_blocks = [block, lax.ppermute(block, "z", up_ring), lax.ppermute(block, "z", down_ring)]
+    table = jnp.pad(table, ((0, 0), (0, ARRIVE[0] - table.shape[1])))
+    top = jnp.concatenate([tokens[:, into[0]], table], axis=0)
+    first = lax.all_gather(top, "z", axis=0, tiled=False)
+    second = lax.all_gather(tokens[:, into[1]], "z", axis=0, tiled=False)
+    mine = jnp.pad(table, ((0, 0), (0, ARRIVE[1])))
+    mine = [jnp.concatenate([tokens, mine], axis=0)]
 
     swap = [(0, 1), (1, 0)]
     weights = [gate_w[0], up_w[0]]
     weights = [v for w in weights for v in (w, lax.ppermute(w, "dp", swap))]
-    w_down = jnp.concatenate([down_w[0], lax.ppermute(down_w[0], "dp", swap)], axis=0)
-
-    weights, w_down, near_blocks, order = lax.optimization_barrier(
-        (weights, w_down, near_blocks, order)
+    down_other = lax.ppermute(down_w[0], "dp", swap)
+
+    own = flat(in_plane(pack_near(order, mine, tok_count, plane, capacity), own_count))
+    after, weights, down_other = lax.optimization_barrier(
+        (own[:8, :128] + 1, weights, down_other)
     )
-    near = flat(in_plane(pack_near(order, near_blocks, tok_count, plane, capacity), near_count))
-    after = near[:8, :128] + 1
-    far = pack_far(order, blocks, after, tok_count, plane, capacity)
-    far = flat(in_plane(far, far_count))
-    hidden_near, hidden_far = hidden_of(near, far, weights)
-
-    answers = dot(hidden_far, w_down).astype(jnp.bfloat16)
-    answers = in_plane(answers, far_count)
-    partial = mix_far(order, blocks, answers, tok_count)
-    partial, hidden_near = lax.optimization_barrier((partial, hidden_near))
-    total = lax.psum_scatter(partial, "z", scatter_dimension=0, tiled=True)[0]
-
-    answers = dot(hidden_near, w_down).astype(jnp.bfloat16)
-    answers = in_plane(answers, near_count)
-    own, under, over = mix_near(order, near_blocks, answers, tok_count)
-    under, over = lax.ppermute(under, "z", down_ring), lax.ppermute(over, "z", up_ring)
-    total = total.astype(jnp.float32) + own + under.astype(jnp.float32) + over.astype(jnp.float32)
+    w_down = jnp.concatenate([down_w[0], down_other], axis=0)
+    after, w_down = lax.optimization_barrier((after, w_down))
+    far = []
+    for block in (first, second):
+        rows = pack_far(order, first, block, after, tok_count, plane, capacity)
+        far.append(flat(in_plane(rows, far_count)))
+        after = far[-1][:8, :128] + 1
+    hidden_own, hidden_far = hidden_of(own, *far, weights)
+
+    totals = []
+    for part in back:
+        answers = dot(hidden_far, w_down[:, part]).astype(jnp.bfloat16)
+        partial = mix_far(order, first, in_plane(answers, far_count), tok_count)
+        partial, hidden_far, hidden_own = lax.optimization_barrier(
+            (partial, hidden_far, hidden_own)
+        )
+        totals.append(lax.psum_scatter(partial, "z", scatter_dimension=0, tiled=True)[0])
+
+    answers = dot(hidden_own, w_down).astype(jnp.bfloat16)
+    (mine,) = mix_near(order, mine, in_plane(answers, own_count), tok_count)
+    total = jnp.concatenate(totals, axis=1).astype(jnp.float32) + mine
     return total.astype(jnp.bfloat16)
 
 

time: 335 us -> 338 us (level)
  waiting for transfers between devices: 27.8 us -> 41.6 us
  starting transfers between devices: 17.1 us -> 8.29 us
  blocking collectives: 203 us -> 196 us
    ppermute x5 -> x1, waiting for transfers between devices: 27.8 us -> 0.01 us  [body(): down_other = lax.ppermute(down_w[0], 'dp', swap)]
    reduce_scatter x1 -> x2, waiting for transfers between devices: 0.01 us -> 19.2 us  [body(): lax.psum_scatter(partial, 'z', scatter_dimension=0, tiled=True)[0]]
    ppermute x5 -> x1, starting transfers between devices: 16.5 us -> 0.1 us  [body(): down_other = lax.ppermute(down_w[0], 'dp', swap)]
    all_to_all x0 -> x1, waiting for transfers between devices: none -> 15 us  [in_plane(): lax.all_to_all(rows, ('x', 'y'), split_axis=0, concat_axis=0, tiled=True)]
    all_to_all x4 -> x5, blocking collectives: 203 us -> 196 us  [in_plane(): lax.all_to_all(rows, ('x', 'y'), split_axis=0, concat_axis=0, tiled=True)]
    all_to_all x0 -> x1, starting transfers between devices: none -> 7.48 us  [in_plane(): lax.all_to_all(rows, ('x', 'y'), split_axis=0, concat_axis=0, tiled=True)]
    all_gather x1 -> x2, waiting for transfers between devices: 0.01 us -> 6.66 us  [the longest x1 6.66 us: body(): first = lax.all_gather(top, 'z', axis=0, tiled=False)]
    pallas_call x1 -> x2, Pallas kernels: 6.55 us -> 9.16 us  [mix_far(): pl.pallas_call(mix_far_kernel, grid_spec=pltpu.PrefetchScalarGridSpec(num...]
  transfers between devices with their start and end apart: 9 -> 8, of which waited for: 4 -> 3; matrix products, arithmetic and copies ran while one was open for 4% -> 6% of each run, Pallas kernels for 3% -> 5%
where the time goes in v9:
time: 338 us; the launch traced here: 337 us
  blocking collectives  196 us (58%)
  Pallas kernels  45.3 us (13%)
  waiting for transfers between devices  41.6 us (12%)
  other arithmetic  14 us (4%)
  matrix products  13.5 us (4%)
  between operations  13.2 us (4%)
  starting transfers between devices  8.29 us (2%)
  local copies, waits for them, and re-layouts  5.27 us (2%)
    all_to_all x5, blocking collectives, in_plane(): lax.all_to_all(rows, ('x', 'y'), split_axis=0, concat_axis=0, tiled=True)  196 us
    reduce_scatter x2, waiting for transfers between devices, body(): lax.psum_scatter(partial, 'z', scatter_dimension=0, tiled=True)[0]  19.2 us
    pallas_call x1, Pallas kernels, hidden_of(): pl.pallas_call(functools.partial(hidden_kernel, split=split), grid=(depth...  18.1 us
    all_to_all x1, waiting for transfers between devices, in_plane(): lax.all_to_all(rows, ('x', 'y'), split_axis=0, concat_axis=0, tiled=True)  15 us
    dot_general x3, matrix products, dot(): return jnp.dot(a, b, preferred_element_type=jnp.float32)  13.5 us
    pallas_call x2, Pallas kernels, pack_far(): pl.pallas_call(pack_far_kernel, grid_spec=pltpu.PrefetchScalarGridSpec(nu...  9.16 us
    pallas_call x2, Pallas kernels, mix_far(): pl.pallas_call(mix_far_kernel, grid_spec=pltpu.PrefetchScalarGridSpec(num...  9.16 us
    all_to_all x1, starting transfers between devices, in_plane(): lax.all_to_all(rows, ('x', 'y'), split_axis=0, concat_axis=0, tiled=True)  7.48 us
  transfers between devices with their start and end apart: 8, of which 3 were waited for; matrix products, arithmetic and copies ran while one was open for 6% of the time, Pallas kernels for 5%

profile of v9, /device:TPU:2, one launch (start us, length us, event | category | flops | bytes accessed | tf_op | source)
XLA Modules:
  0.0 336.8 jit_solution(4840011367980356976)
XLA Ops:
  6.5 0.8 reshape.166
  7.3 0.8 broadcast_in_dim.27
  8.1 0.3 convert_reduce_fusion
  8.4 0.6 select_reduce_fusion.1
  9.1 1.8 fusion.19
  10.9 0.7 pad_maximum_fusion.1
  11.6 0.0 all-gather.5.cloned.1.call-update
  11.7 0.1 collective-permute-start
  11.8 0.5 collective-permute-start.1
  12.3 0.1 collective-permute-start.2
  12.4 0.1 stack.43
  12.4 0.5 and_select_fusion.order_ref
  13.0 1.9 fusion.4.refs_0_.refs_1_
  14.9 4.5 %pack_near.1 = bf16[16,1,8,4096]{3,2,1,0:T(8,128)(2,1)} custom-call(s32[8]{0:T(128)} %and_select_fusion.order_ref, bf16[72,4096]{1,0:T(8,128)(2,1)} %fusion.4.refs_0_.refs_1_, bf16[72,4096]{1,0:T(8,128)(2,1)} %fusion.4.refs_0_.refs_1_), custom_call_target="tpu_custom_call" | custom-call | tf_op jit(solution)/shard_map/pack_near/pallas_call | solution.py:80
  19.4 7.5 %all-to-all-start = ((bf16[16,8,4096]{2,1,0:T(8,128)(2,1)}), bf16[16,8,4096]{2,1,0:T(8,128)(2,1)S(1)}, u32[]{:S(2)}, u32[]{:S(2)}) async-start(bf16[16,8,4096]{2,1,0:T(8,128)(2,1)} %bitcast.60), calls=%async_computation | async-start | bytes 2097152 | tf_op jit(solution)/shard_map/all_to_all | solution.py:259
  26.9 0.0 all-gather.7.cloned.1.call-start
  26.9 0.7 all-gather.7.cloned.1.call-update
  27.6 0.0 reduce-scatter.3.cloned.1.call-start
  27.7 15.0 %all-to-all-done = bf16[16,8,4096]{2,1,0:T(8,128)(2,1)S(1)} async-done(((bf16[16,8,4096]{2,1,0:T(8,128)(2,1)}), bf16[16,8,4096]{2,1,0:T(8,128)(2,1)S(1)}, u32[]{:S(2)}, u32[]{:S(2)}) %all-to-all-start) | async-done | bytes 1048608 | tf_op jit(solution)/shard_map/all_to_all | solution.py:259
  42.7 0.6 slice_add_fusion.1._
  43.3 0.0 collective-permute-done.refs_1_
  43.3 0.0 collective-permute-done.1.refs_3_
  43.3 0.0 collective-permute-done.2
  43.3 6.4 %pad_maximum_fusion = bf16[768,4096]{1,0:T(8,128)(2,1)} fusion(bf16[384,4096]{1,0:T(8,128)(2,1)} %collective-permute-done.2, bf16[384,4096]{1,0:T(8,128)(2,1)} %bitcast.69), kind=kLoop, calls=%fused_computation | loop fusion | flops 12582912 | bytes 12582912 | tf_op jit(solution)/shard_map/concatenate | solution.py:286
  49.7 6.7 %all-gather.5.cloned.1.call-done = bf16[576,2048]{1,0:T(8,128)(2,1)} async-done(((bf16[72,2048]{1,0:T(8,128)(2,1)}), bf16[576,2048]{1,0:T(8,128)(2,1)}) %all-gather.5.cloned.1.call-update) | async-done | bytes 2359312 | tf_op jit(solution)/shard_map/all_gather | solution.py:272
  56.3 4.6 %pack_far.2 = bf16[16,7,8,2048]{3,2,1,0:T(8,128)(2,1)} custom-call(s32[8]{0:T(128)} %and_select_fusion.order_ref, bf16[8,72,2048]{2,1,0:T(8,128)(2,1)} %bitcast.44, bf16[8,72,2048]{2,1,0:T(8,128)(2,1)} %bitcast.45, bf16[8,128]{1,0:T(8,128)(2,1)} %slice_add_fusion.1._), custom_call_target="tpu_custom_call" | custom-call | tf_op jit(solution)/shard_map/pack_far/pallas_call | solution.py:106
  61.0 47.8 %all_to_all.30 = bf16[16,56,2048]{2,1,0:T(8,128)(2,1)S(1)} all-to-all(bf16[16,56,2048]{2,1,0:T(8,128)(2,1)} %bitcast.55), channel_id=1, replica_groups=mesh['x'=4,'z'=8,'y'=4,'dp'=2] {'x','y'}, dimensions={0} | all-to-all | bytes 7340032 | tf_op jit(solution)/shard_map/all_to_all | solution.py:259
  108.8 1.9 copy-done
  110.7 0.6 slice_add_fusion._
  111.2 4.6 %pack_far.3 = bf16[16,7,8,2048]{3,2,1,0:T(8,128)(2,1)} custom-call(s32[8]{0:T(128)} %and_select_fusion.order_ref, bf16[8,72,2048]{2,1,0:T(8,128)(2,1)} %bitcast.46, bf16[8,64,2048]{2,1,0:T(8,128)(2,1)} %bitcast.70, bf16[8,128]{1,0:T(8,128)(2,1)} %slice_add_fusion._), custom_call_target="tpu_custom_call" | custom-call | tf_op jit(solution)/shard_map/pack_far/pallas_call | solution.py:106
  115.8 46.0 %all_to_all.31 = bf16[16,56,2048]{2,1,0:T(8,128)(2,1)} all-to-all(bf16[16,56,2048]{2,1,0:T(8,128)(2,1)} %bitcast.54), channel_id=1, replica_groups=mesh['x'=4,'z'=8,'y'=4,'dp'=2] {'x','y'}, dimensions={0} | all-to-all | bytes 7340032 | tf_op jit(solution)/shard_map/all_to_all | solution.py:259
  161.8 18.1 %hidden.1 = (bf16[128,768]{1,0:T(8,128)(2,1)}, bf16[896,768]{1,0:T(8,128)(2,1)}) custom-call(bf16[128,4096]{1,0:T(8,128)(2,1)} %bitcast.59, bf16[896,2048]{1,0:T(8,128)(2,1)} %bitcast.52, bf16[896,2048]{1,0:T(8,128)(2,1)} %bitcast.53, bf16[4096,384]{1,0:T(8,128)(2,1)} %bitcast.65, bf16[4096,384]{1,0:T(8,128)(2,1)} %collective-permute-done.refs_1_, ...), custom_call_target="tpu_custom_call" | custom-call | tf_op jit(solution)/shard_map/hidden/pallas_call | solution.py:222
  180.0 4.6 %convolution_convert_fusion.2 = bf16[896,2048]{1,0:T(8,128)(2,1)S(1)} fusion(bf16[896,768]{1,0:T(8,128)(2,1)} %get-tuple-element.31, bf16[768,4096]{1,0:T(8,128)(2,1)S(1)} %bitcast.50), kind=kOutput, calls=%fused_computation.4 | convolution fusion | flops 2820407296 | bytes 8192000 | tf_op jit(solution)/shard_map/dot_general | solution.py:245
  184.5 43.2 %all_to_all.32 = bf16[16,56,2048]{2,1,0:T(8,128)(2,1)} all-to-all(bf16[16,56,2048]{2,1,0:T(8,128)(2,1)S(1)} %bitcast.63), channel_id=1, replica_groups=mesh['x'=4,'z'=8,'y'=4,'dp'=2] {'x','y'}, dimensions={0} | all-to-all | bytes 7340032 | tf_op jit(solution)/shard_map/all_to_all | solution.py:259
  227.8 4.6 %mix_far.2 = bf16[8,64,2048]{2,1,0:T(8,128)(2,1)} custom-call(s32[8]{0:T(128)} %and_select_fusion.order_ref, bf16[8,72,2048]{2,1,0:T(8,128)(2,1)} %bitcast.47, bf16[16,7,8,2048]{3,2,1,0:T(8,128)(2,1)} %bitcast.57), custom_call_target="tpu_custom_call" | custom-call | tf_op jit(solution)/shard_map/mix_far/pallas_call | solution.py:137
  232.4 0.0 reduce-scatter.3.cloned.1.call-update
  232.4 0.0 reduce-scatter.5.cloned.1.call-start
  232.5 0.0 copy-done.3
  232.5 5.1 %convolution_convert_fusion.1 = bf16[896,2048]{1,0:T(8,128)(2,1)S(1)} fusion(bf16[896,768]{1,0:T(8,128)(2,1)S(1)} %copy-done.3, bf16[768,4096]{1,0:T(8,128)(2,1)} %pad_maximum_fusion), kind=kOutput, calls=%fused_computation.3 | convolution fusion | flops 2820407296 | bytes 8192000 | tf_op jit(solution)/shard_map/dot_general | solution.py:245
  237.6 42.2 %all_to_all.33 = bf16[16,56,2048]{2,1,0:T(8,128)(2,1)} all-to-all(bf16[16,56,2048]{2,1,0:T(8,128)(2,1)S(1)} %bitcast.62), channel_id=1, replica_groups=mesh['x'=4,'z'=8,'y'=4,'dp'=2] {'x','y'}, dimensions={0} | all-to-all | bytes 7340032 | tf_op jit(solution)/shard_map/all_to_all | solution.py:259
  279.8 4.6 %mix_far.3 = bf16[8,64,2048]{2,1,0:T(8,128)(2,1)} custom-call(s32[8]{0:T(128)} %and_select_fusion.order_ref, bf16[8,72,2048]{2,1,0:T(8,128)(2,1)} %bitcast.48, bf16[16,7,8,2048]{3,2,1,0:T(8,128)(2,1)} %bitcast.56), custom_call_target="tpu_custom_call" | custom-call | tf_op jit(solution)/shard_map/mix_far/pallas_call | solution.py:137
  284.4 0.0 reduce-scatter.5.cloned.1.call-update
  284.4 0.0 copy-done.2
  284.4 3.8 %fusion = bf16[16,8,4096]{2,1,0:T(8,128)(2,1)S(1)} fusion(bf16[128,768]{1,0:T(8,128)(2,1)S(1)} %copy-done.2, bf16[768,4096]{1,0:T(8,128)(2,1)} %pad_maximum_fusion), kind=kOutput, calls=%fused_computation.2 | convolution fusion | flops 805830656 | bytes 7536640 | tf_op jit(solution)/shard_map/dot_general | solution.py:245
  288.2 16.3 %all_to_all.34 = bf16[16,8,4096]{2,1,0:T(8,128)(2,1)} all-to-all(bf16[16,8,4096]{2,1,0:T(8,128)(2,1)S(1)} %fusion), channel_id=1, replica_groups=mesh['x'=4,'z'=8,'y'=4,'dp'=2] {'x','y'}, dimensions={0} | all-to-all | bytes 2097152 | tf_op jit(solution)/shard_map/all_to_all | solution.py:259
  304.5 4.4 %mix_near.1 = f32[64,4096]{1,0:T(8,128)} custom-call(s32[8]{0:T(128)} %and_select_fusion.order_ref, bf16[72,4096]{1,0:T(8,128)(2,1)} %fusion.4.refs_0_.refs_1_, bf16[16,1,8,4096]{3,2,1,0:T(8,128)(2,1)} %bitcast.61), custom_call_target="tpu_custom_call" | custom-call | tf_op jit(solution)/shard_map/mix_near/pallas_call | solution.py:167
  308.9 19.2 %reduce-scatter.5.cloned.1.call-done = bf16[1,64,2048]{2,1,0:T(8,128)(2,1)} async-done(((bf16[8,64,2048]{2,1,0:T(8,128)(2,1)}), bf16[1,64,2048]{2,1,0:T(8,128)(2,1)}) %reduce-scatter.5.cloned.1.call-update) | async-done | bytes 262160 | tf_op jit(solution)/shard_map/reduce_scatter | solution.py:302
  328.1 2.2 add_convert_fusion
  (18 shorter events, 0.1 us)
Async XLA Ops:
  6.5 49.8 %all-gather.5.cloned.1.call-start = ((), (), s32[]{:S(2)}) async-start(), calls=%async_computation.10 | async-start | bytes 2654208 | tf_op jit(solution)/shard_map/all_gather | solution.py:272
  11.7 31.7 %collective-permute-start = (bf16[4096,384]{1,0:T(8,128)(2,1)}, bf16[4096,384]{1,0:T(8,128)(2,1)}, u32[]{:S(2)}, u32[]{:S(2)}) collective-permute-start(bf16[4096,384]{1,0:T(8,128)(2,1)} %bitcast.64), channel_id=1, source_target_pairs={{0,1},{1,0},{2,3},{3,2},{4,5},{5,4},{6,7},{7,6},{8,9},{9,8},{10,11... | collective-permute-start | bytes 9437192 | tf_op jit(solution)/shard_map/ppermute | solution.py:279
  11.8 31.6 %collective-permute-start.1 = (bf16[4096,384]{1,0:T(8,128)(2,1)}, bf16[4096,384]{1,0:T(8,128)(2,1)}, u32[]{:S(2)}, u32[]{:S(2)}) collective-permute-start(bf16[4096,384]{1,0:T(8,128)(2,1)} %bitcast.66), channel_id=1, source_target_pairs={{0,1},{1,0},{2,3},{3,2},{4,5},{5,4},{6,7},{7,6},{8,9},{9,8},{10,11... | collective-permute-start | bytes 9437192 | tf_op jit(solution)/shard_map/ppermute | solution.py:279
  12.3 31.1 %collective-permute-start.2 = (bf16[384,4096]{1,0:T(8,128)(2,1)}, bf16[384,4096]{1,0:T(8,128)(2,1)}, u32[]{:S(2)}, u32[]{:S(2)}) collective-permute-start(bf16[384,4096]{1,0:T(8,128)(2,1)} %bitcast.68), channel_id=1, source_target_pairs={{0,1},{1,0},{2,3},{3,2},{4,5},{5,4},{6,7},{7,6},{8,9},{9,8},{10,11... | collective-permute-start | bytes 9437192 | tf_op jit(solution)/shard_map/ppermute | solution.py:280
  19.4 23.3 %all-to-all-start = ((bf16[16,8,4096]{2,1,0:T(8,128)(2,1)}), bf16[16,8,4096]{2,1,0:T(8,128)(2,1)S(1)}, u32[]{:S(2)}, u32[]{:S(2)}) async-start(bf16[16,8,4096]{2,1,0:T(8,128)(2,1)} %bitcast.60), calls=%async_computation | async-start | bytes 2097152 | tf_op jit(solution)/shard_map/all_to_all | solution.py:259
  26.9 84.4 %all-gather.7.cloned.1.call-start = ((), (), s32[]{:S(2)}) async-start(), calls=%async_computation.11 | async-start | bytes 2359296 | tf_op jit(solution)/shard_map/all_gather | solution.py:273
  27.6 281.3 %reduce-scatter.3.cloned.1.call-start = ((), (), s32[]{:S(2)}) async-start(), calls=%async_computation.8 | async-start | bytes 2359296 | tf_op jit(solution)/shard_map/reduce_scatter | solution.py:302
  42.7 7.0 %copy-start.1 = (bf16[16,8,4096]{2,1,0:T(8,128)(2,1)}, bf16[16,8,4096]{2,1,0:T(8,128)(2,1)S(1)}, u32[]{:S(2)}) copy-start(bf16[16,8,4096]{2,1,0:T(8,128)(2,1)S(1)} %all-to-all-done) | copy-start | bytes 3145732
  108.8 1.9 copy-start
  115.8 64.2 %slice-start = ((s8[6291456]{0:T(1024)(128)(4,1)}), s8[4194304]{0:T(1024)(128)(4,1)S(1)}, s32[]{:S(2)}) async-start(s8[6291456]{0:T(1024)(128)(4,1)} %bitcast.49), calls=%async_computation.12 | async-start | bytes 8388608
  161.8 18.1 %slice-start.1 = ((s8[6291456]{0:T(1024)(128)(4,1)}), s8[2097152]{0:T(1024)(128)(4,1)S(1)}, s32[]{:S(2)}) async-start(s8[6291456]{0:T(1024)(128)(4,1)} %bitcast.49), calls=%async_computation.13 | async-start | bytes 4194304
  227.8 4.7 %copy-start.3 = (bf16[896,768]{1,0:T(8,128)(2,1)S(1)}, bf16[896,768]{1,0:T(8,128)(2,1)}, u32[]{:S(2)}) copy-start(bf16[896,768]{1,0:T(8,128)(2,1)} %get-tuple-element.31) | copy-start | bytes 4128772
  232.4 95.7 %reduce-scatter.5.cloned.1.call-start = ((), (), s32[]{:S(2)}) async-start(), calls=%async_computation.9 | async-start | bytes 2359296 | tf_op jit(solution)/shard_map/reduce_scatter | solution.py:302
  279.8 4.6 %copy-start.2 = (bf16[128,768]{1,0:T(8,128)(2,1)S(1)}, bf16[128,768]{1,0:T(8,128)(2,1)}, u32[]{:S(2)}) copy-start(bf16[128,768]{1,0:T(8,128)(2,1)} %get-tuple-element.34) | copy-start | bytes 589828
Sparse Core Ops, SparseCore 0:
  11.8 44.5 all-gather.4
  58.1 40.0 all-gather.6
  232.5 40.8 reduce-scatter.2
  284.6 43.4 reduce-scatter.4

commit v10 on v7

--- a/solution.py
+++ b/solution.py
@@ -12,7 +12,7 @@
 DEPTH = 512
 STEP = 1024
 LISTS = 512
-NEAR = (0, -1, 1)
+NEAR = (0, 1)
 
 
 def slot_table(routes, gate_probs, sizes, capacity):
@@ -178,30 +178,29 @@
 
 
 def hidden_kernel(near_ref, far_ref, *refs):
-    *weights, out_near, out_far, gate_near, up_near, gate_far, up_far = refs
+    *weights, out_near, out_far, gate_acc, up_acc = refs
     step, steps = pl.program_id(0), pl.num_programs(0)
     gate, gate_other, up, up_other = (ref[...] for ref in weights)
     gate = jnp.concatenate([gate, gate_other], axis=1)
     up = jnp.concatenate([up, up_other], axis=1)
-    parts = [(near_ref, out_near, gate_near, up_near), (far_ref, out_far, gate_far, up_far)]
-    for rows_ref, out_ref, gate_acc, up_acc in parts:
-        rows = rows_ref[...]
-
-        @pl.when(step == 0)
-        def _():
-            gate_acc[...] = dot(rows, gate)
-            up_acc[...] = dot(rows, up)
-
-        @pl.when((step > 0) & (step < steps - 1))
-        def _():
-            gate_acc[...] += dot(rows, gate)
-            up_acc[...] += dot(rows, up)
-
-        @pl.when(step == steps - 1)
-        def _():
-            gate_act = gate_acc[...] + dot(rows, gate)
-            up_act = up_acc[...] + dot(rows, up)
-            out_ref[...] = (jax.nn.silu(gate_act) * up_act).astype(out_ref.dtype)
+    rows = jnp.concatenate([near_ref[...], far_ref[...]], axis=0)
+
+    @pl.when(step == 0)
+    def _():
+        gate_acc[...] = dot(rows, gate)
+        up_acc[...] = dot(rows, up)
+
+    @pl.when((step > 0) & (step < steps - 1))
+    def _():
+        gate_acc[...] += dot(rows, gate)
+        up_acc[...] += dot(rows, up)
+
+    @pl.when(step == steps - 1)
+    def _():
+        hidden = jax.nn.silu(gate_acc[...] + dot(rows, gate)) * (up_acc[...] + dot(rows, up))
+        count = out_near.shape[0]
+        out_near[...] = hidden[:count].astype(out_near.dtype)
+        out_far[...] = hidden[count:].astype(out_far.dtype)
 
 
 def hidden_of(near, far, weights):
@@ -214,7 +213,7 @@
         + [pl.BlockSpec((DEPTH, units), lambda i: (i, 0))] * 4,
         out_specs=[pl.BlockSpec((c, 2 * units), lambda i: (0, 0)) for c in counts],
         out_shape=[jax.ShapeDtypeStruct((c, 2 * units), jnp.bfloat16) for c in counts],
-        scratch_shapes=[pltpu.VMEM((c, 2 * units), jnp.float32) for c in counts for _ in range(2)],
+        scratch_shapes=[pltpu.VMEM((sum(counts), 2 * units), jnp.float32)] * 2,
         compiler_params=pltpu.CompilerParams(vmem_limit_bytes=56 << 20),
         name="hidden",
     )(near, far, *weights)
@@ -242,7 +241,7 @@
     def flat(rows):
         return rows.reshape(-1, model_width)
 
-    offsets = [*NEAR, *(d for d in range(2, z_size - 1))]
+    offsets = [*NEAR, *range(len(NEAR), z_size)]
     near_count, far_count = len(NEAR), z_size - len(NEAR)
     order = jnp.stack([my_z + d for d in offsets]) % z_size
 
@@ -250,7 +249,7 @@
     table = jnp.pad(table, ((0, 0), (0, model_width - table.shape[1])))
     block = jnp.concatenate([tokens, table], axis=0)
     blocks = lax.all_gather(block, "z", axis=0, tiled=False)
-    near_blocks = [block, lax.ppermute(block, "z", up_ring), lax.ppermute(block, "z", down_ring)]
+    near_blocks = [block, lax.ppermute(block, "z", down_ring)]
 
     swap = [(0, 1), (1, 0)]
     weights = [gate_w[0], up_w[0]]
@@ -274,9 +273,9 @@
 
     answers = dot(hidden_near, w_down).astype(jnp.bfloat16)
     answers = in_plane(answers, near_count)
-    own, under, over = mix_near(order, near_blocks, answers, tok_count)
-    under, over = lax.ppermute(under, "z", down_ring), lax.ppermute(over, "z", up_ring)
-    total = total.astype(jnp.float32) + own + under.astype(jnp.float32) + over.astype(jnp.float32)
+    own, over = mix_near(order, near_blocks, answers, tok_count)
+    over = lax.ppermute(over, "z", up_ring)
+    total = total.astype(jnp.float32) + own + over.astype(jnp.float32)
     return total.astype(jnp.bfloat16)
 
 

time: 335 us -> 345 us (1.030)
  blocking collectives: 203 us -> 220 us
  starting transfers between devices: 17.1 us -> 6.59 us
  waiting for transfers between devices: 27.8 us -> 33.2 us
    all_to_all x4, blocking collectives: 203 us -> 220 us  [in_plane(): lax.all_to_all(rows, ('x', 'y'), split_axis=0, concat_axis=0, tiled=True)]
    ppermute x4 -> x2, starting transfers between devices: 16.4 us -> 5.86 us  [the longest x1 5.86 us: body(): near_blocks = [block, lax.ppermute(block, 'z', down_ring)]]
    ppermute x4 -> x2, waiting for transfers between devices: 27.8 us -> 33.2 us  [the longest x1 20.5 us: body(): over = lax.ppermute(over, 'z', up_ring)]
  transfers between devices with their start and end apart: 9 -> 7, of which waited for: 4 -> 2; matrix products, arithmetic and copies ran while one was open for 4% -> 4% of each run, Pallas kernels for 3% -> 3%
where the time goes in v10:
time: 345 us; the launch traced here: 344 us
  blocking collectives  220 us (64%)
  Pallas kernels  43.1 us (12%)
  waiting for transfers between devices  33.2 us (10%)
  between operations  13.5 us (4%)
  other arithmetic  12.7 us (4%)
  matrix products  11.1 us (3%)
  starting transfers between devices  6.59 us (2%)
    all_to_all x4, blocking collectives, in_plane(): lax.all_to_all(rows, ('x', 'y'), split_axis=0, concat_axis=0, tiled=True)  220 us
    ppermute x1, waiting for transfers between devices, body(): over = lax.ppermute(over, 'z', up_ring)  20.5 us
    pallas_call x1, Pallas kernels, hidden_of(): pl.pallas_call(hidden_kernel, grid=(depth // DEPTH,), in_specs=[pl.BlockS...  19.1 us
    ppermute x1, waiting for transfers between devices, body(): near_blocks = [block, lax.ppermute(block, 'z', down_ring)]  12.7 us
    dot_general x2, matrix products, dot(): return jnp.dot(a, b, preferred_element_type=jnp.float32)  11.1 us
    pallas_call x1, Pallas kernels, pack_far(): pl.pallas_call(pack_far_kernel, grid_spec=pltpu.PrefetchScalarGridSpec(nu...  7.16 us
    pallas_call x1, Pallas kernels, mix_far(): pl.pallas_call(mix_far_kernel, grid_spec=pltpu.PrefetchScalarGridSpec(num...  6.99 us
  transfers between devices with their start and end apart: 7, of which 2 were waited for; matrix products, arithmetic and copies ran while one was open for 4% of the time, Pallas kernels for 3%

profile of v10, /device:TPU:2, one launch (start us, length us, event | category | flops | bytes accessed | tf_op | source)
XLA Modules:
  0.0 344.0 jit_solution(11920349750842035496)
XLA Ops:
  6.5 0.0 all-gather.3.cloned.1.call-start
  6.5 0.8 reshape.159
  7.3 0.8 broadcast_in_dim.27
  8.1 0.3 convert_reduce_fusion
  8.4 0.6 select_reduce_fusion.1
  9.1 1.9 fusion.3.refs_0_.refs_2_
  11.0 0.0 all-gather.3.cloned.1.call-update
  11.1 0.0 reduce-scatter.2.cloned.1.call-start
  11.1 0.1 collective-permute-start.2
  11.2 0.5 collective-permute-start
  11.7 0.1 collective-permute-start.1
  11.8 5.9 %collective-permute-start.3 = (bf16[72,4096]{1,0:T(8,128)(2,1)}, bf16[72,4096]{1,0:T(8,128)(2,1)S(1)}, u32[]{:S(2)}, u32[]{:S(2)}) collective-permute-start(bf16[72,4096]{1,0:T(8,128)(2,1)} %fusion.3.refs_0_.refs_2_), channel_id=1, source_target_pairs={{0,56},{8,0},{16,8},{24,16},{32,24},{40,32},{48,40},{56,48},{1,57}... | collective-permute-start | bytes 1769480 | tf_op jit(solution)/shard_map/ppermute | solution.py:252
  17.7 0.1 stack.45
  17.8 0.6 and_select_fusion.order_ref
  18.3 0.0 collective-permute-done.2
  18.3 6.3 %pad_maximum_fusion = bf16[768,4096]{1,0:T(8,128)(2,1)} fusion(bf16[384,4096]{1,0:T(8,128)(2,1)} %collective-permute-done.2, bf16[384,4096]{1,0:T(8,128)(2,1)} %bitcast.57), kind=kLoop, calls=%fused_computation.1 | loop fusion | flops 12582912 | bytes 12582912 | tf_op jit(solution)/shard_map/concatenate | solution.py:257
  24.6 12.7 %collective-permute-done.3.refs_1_.refs_3_ = bf16[72,4096]{1,0:T(8,128)(2,1)S(1)} collective-permute-done((bf16[72,4096]{1,0:T(8,128)(2,1)}, bf16[72,4096]{1,0:T(8,128)(2,1)S(1)}, u32[]{:S(2)}, u32[]{:S(2)}) %collective-permute-start.3) | collective-permute-done | bytes 589856 | tf_op jit(solution)/shard_map/ppermute | solution.py:252
  37.3 0.0 copy-start.1
  37.3 0.0 collective-permute-done.refs_1_
  37.3 0.0 collective-permute-done.1.refs_3_
  37.3 0.8 copy-done.1
  38.1 5.1 %pack_near.1 = bf16[16,2,8,4096]{3,2,1,0:T(8,128)(2,1)} custom-call(s32[8]{0:T(128)} %and_select_fusion.order_ref, bf16[72,4096]{1,0:T(8,128)(2,1)} %fusion.3.refs_0_.refs_2_, bf16[72,4096]{1,0:T(8,128)(2,1)} %copy-done.1, bf16[72,4096]{1,0:T(8,128)(2,1)} %fusion.3.refs_0_.refs_2_, bf16[72,4096]{1,0:T(8,128)(2,1)} %copy-done.1), custom_call_target="tpu_custom_call" | custom-call | tf_op jit(solution)/shard_map/pack_near/pallas_call | solution.py:78
  43.3 33.0 %all_to_all.20 = bf16[16,16,4096]{2,1,0:T(8,128)(2,1)S(1)} all-to-all(bf16[16,16,4096]{2,1,0:T(8,128)(2,1)} %bitcast.48), channel_id=1, replica_groups=mesh['x'=4,'z'=8,'y'=4,'dp'=2] {'x','y'}, dimensions={0} | all-to-all | bytes 4194304 | tf_op jit(solution)/shard_map/all_to_all | solution.py:238
  76.3 0.0 copy-start
  76.3 0.6 slice_add_fusion._
  76.9 0.0 all-gather.3.cloned.1.call-done
  76.9 7.2 %pack_far.1 = bf16[16,6,8,4096]{3,2,1,0:T(8,128)(2,1)} custom-call(s32[8]{0:T(128)} %and_select_fusion.order_ref, bf16[8,72,4096]{2,1,0:T(8,128)(2,1)} %bitcast.39, bf16[8,72,4096]{2,1,0:T(8,128)(2,1)} %bitcast.40, bf16[8,128]{1,0:T(8,128)(2,1)} %slice_add_fusion._), custom_call_target="tpu_custom_call" | custom-call | tf_op jit(solution)/shard_map/pack_far/pallas_call | solution.py:104
  84.1 0.0 copy-done
  84.1 0.0 slice-start
  84.1 78.7 %all_to_all.21 = bf16[16,48,4096]{2,1,0:T(8,128)(2,1)} all-to-all(bf16[16,48,4096]{2,1,0:T(8,128)(2,1)} %bitcast.43), channel_id=1, replica_groups=mesh['x'=4,'z'=8,'y'=4,'dp'=2] {'x','y'}, dimensions={0} | all-to-all | bytes 12582912 | tf_op jit(solution)/shard_map/all_to_all | solution.py:238
  162.7 0.0 slice-start.1
  162.7 19.1 %hidden.1 = (bf16[256,768]{1,0:T(8,128)(2,1)}, bf16[768,768]{1,0:T(8,128)(2,1)}) custom-call(bf16[256,4096]{1,0:T(8,128)(2,1)} %bitcast.46, bf16[768,4096]{1,0:T(8,128)(2,1)} %bitcast.44, bf16[4096,384]{1,0:T(8,128)(2,1)} %bitcast.53, bf16[4096,384]{1,0:T(8,128)(2,1)} %collective-permute-done.refs_1_, bf16[4096,384]{1,0:T(8,128)(2,1)} %bitcast.55, ...), custom_call_target="tpu_custom_call" | custom-call | tf_op jit(solution)/shard_map/hidden/pallas_call | solution.py:209
  181.9 0.0 slice-done
  181.9 0.0 slice-done.1
  181.9 6.5 %convolution_convert_fusion = bf16[768,4096]{1,0:T(8,128)(2,1)S(1)} fusion(bf16[768,768]{1,0:T(8,128)(2,1)} %get-tuple-element.26, bf16[768,4096]{1,0:T(8,128)(2,1)S(1)} %bitcast.50), kind=kOutput, calls=%fused_computation | convolution fusion | flops 4834983936 | bytes 13762560 | tf_op jit(solution)/shard_map/dot_general | solution.py:223
  188.4 76.6 %all_to_all.22 = bf16[16,48,4096]{2,1,0:T(8,128)(2,1)} all-to-all(bf16[16,48,4096]{2,1,0:T(8,128)(2,1)S(1)} %bitcast.51), channel_id=1, replica_groups=mesh['x'=4,'z'=8,'y'=4,'dp'=2] {'x','y'}, dimensions={0} | all-to-all | bytes 12582912 | tf_op jit(solution)/shard_map/all_to_all | solution.py:238
  265.0 7.0 %mix_far.1 = bf16[8,64,4096]{2,1,0:T(8,128)(2,1)} custom-call(s32[8]{0:T(128)} %and_select_fusion.order_ref, bf16[8,72,4096]{2,1,0:T(8,128)(2,1)} %bitcast.41, bf16[16,6,8,4096]{3,2,1,0:T(8,128)(2,1)} %bitcast.42), custom_call_target="tpu_custom_call" | custom-call | tf_op jit(solution)/shard_map/mix_far/pallas_call | solution.py:135
  272.0 0.0 copy-start.2
  272.0 0.0 reduce-scatter.2.cloned.1.call-update
  272.0 1.0 copy-done.2
  273.0 4.6 %convolution_convert_fusion.1 = bf16[256,4096]{1,0:T(8,128)(2,1)S(1)} fusion(bf16[256,768]{1,0:T(8,128)(2,1)S(1)} %copy-done.2, bf16[768,4096]{1,0:T(8,128)(2,1)} %pad_maximum_fusion), kind=kOutput, calls=%fused_computation.2 | convolution fusion | flops 1611661312 | bytes 8781824 | tf_op jit(solution)/shard_map/dot_general | solution.py:223
  277.6 32.1 %all_to_all.23 = bf16[16,16,4096]{2,1,0:T(8,128)(2,1)} all-to-all(bf16[16,16,4096]{2,1,0:T(8,128)(2,1)S(1)} %bitcast.58), channel_id=1, replica_groups=mesh['x'=4,'z'=8,'y'=4,'dp'=2] {'x','y'}, dimensions={0} | all-to-all | bytes 4194304 | tf_op jit(solution)/shard_map/all_to_all | solution.py:238
  309.7 4.7 %mix_near.1 = (f32[64,4096]{1,0:T(8,128)}, bf16[64,4096]{1,0:T(8,128)(2,1)}) custom-call(s32[8]{0:T(128)} %and_select_fusion.order_ref, bf16[72,4096]{1,0:T(8,128)(2,1)} %fusion.3.refs_0_.refs_2_, bf16[72,4096]{1,0:T(8,128)(2,1)} %copy-done.1, bf16[16,2,8,4096]{3,2,1,0:T(8,128)(2,1)} %bitcast.47), custom_call_target="tpu_custom_call" | custom-call | tf_op jit(solution)/shard_map/mix_near/pallas_call | solution.py:165
  314.4 0.0 collective-permute-start.4
  314.4 20.5 %collective-permute-done.4 = bf16[64,4096]{1,0:T(8,128)(2,1)S(1)} collective-permute-done((bf16[64,4096]{1,0:T(8,128)(2,1)}, bf16[64,4096]{1,0:T(8,128)(2,1)S(1)}, u32[]{:S(2)}, u32[]{:S(2)}) %collective-permute-start.4) | collective-permute-done | bytes 524320 | tf_op jit(solution)/shard_map/ppermute | solution.py:277
  334.9 0.0 reduce-scatter.2.cloned.1.call-done
  334.9 2.3 fusion.2
  (5 shorter events, 0.0 us)
Async XLA Ops:
  6.5 70.4 %all-gather.3.cloned.1.call-start = ((), (), s32[]{:S(2)}) async-start(), calls=%async_computation.6 | async-start | bytes 5308416 | tf_op jit(solution)/shard_map/all_gather | solution.py:251
  11.1 323.8 %reduce-scatter.2.cloned.1.call-start = ((), (), s32[]{:S(2)}) async-start(), calls=%async_computation.5 | async-start | bytes 4718592 | tf_op jit(solution)/shard_map/reduce_scatter | solution.py:272
  11.1 7.2 %collective-permute-start.2 = (bf16[384,4096]{1,0:T(8,128)(2,1)}, bf16[384,4096]{1,0:T(8,128)(2,1)}, u32[]{:S(2)}, u32[]{:S(2)}) collective-permute-start(bf16[384,4096]{1,0:T(8,128)(2,1)} %bitcast.56), channel_id=1, source_target_pairs={{0,1},{1,0},{2,3},{3,2},{4,5},{5,4},{6,7},{7,6},{8,9},{9,8},{10,11... | collective-permute-start | bytes 9437192 | tf_op jit(solution)/shard_map/ppermute | solution.py:257
  11.2 26.1 %collective-permute-start = (bf16[4096,384]{1,0:T(8,128)(2,1)}, bf16[4096,384]{1,0:T(8,128)(2,1)}, u32[]{:S(2)}, u32[]{:S(2)}) collective-permute-start(bf16[4096,384]{1,0:T(8,128)(2,1)} %bitcast.52), channel_id=1, source_target_pairs={{0,1},{1,0},{2,3},{3,2},{4,5},{5,4},{6,7},{7,6},{8,9},{9,8},{10,11... | collective-permute-start | bytes 9437192 | tf_op jit(solution)/shard_map/ppermute | solution.py:256
  11.7 25.6 %collective-permute-start.1 = (bf16[4096,384]{1,0:T(8,128)(2,1)}, bf16[4096,384]{1,0:T(8,128)(2,1)}, u32[]{:S(2)}, u32[]{:S(2)}) collective-permute-start(bf16[4096,384]{1,0:T(8,128)(2,1)} %bitcast.54), channel_id=1, source_target_pairs={{0,1},{1,0},{2,3},{3,2},{4,5},{5,4},{6,7},{7,6},{8,9},{9,8},{10,11... | collective-permute-start | bytes 9437192 | tf_op jit(solution)/shard_map/ppermute | solution.py:256
  11.8 25.5 %collective-permute-start.3 = (bf16[72,4096]{1,0:T(8,128)(2,1)}, bf16[72,4096]{1,0:T(8,128)(2,1)S(1)}, u32[]{:S(2)}, u32[]{:S(2)}) collective-permute-start(bf16[72,4096]{1,0:T(8,128)(2,1)} %fusion.3.refs_0_.refs_2_), channel_id=1, source_target_pairs={{0,56},{8,0},{16,8},{24,16},{32,24},{40,32},{48,40},{56,48},{1,57}... | collective-permute-start | bytes 1769480 | tf_op jit(solution)/shard_map/ppermute | solution.py:252
  37.3 0.8 copy-start.1
  76.3 7.8 %copy-start = (bf16[16,16,4096]{2,1,0:T(8,128)(2,1)}, bf16[16,16,4096]{2,1,0:T(8,128)(2,1)S(1)}, u32[]{:S(2)}) copy-start(bf16[16,16,4096]{2,1,0:T(8,128)(2,1)S(1)} %all_to_all.20) | copy-start | bytes 6291460
  84.1 97.8 %slice-start = ((s8[6291456]{0:T(1024)(128)(4,1)}), s8[4194304]{0:T(1024)(128)(4,1)S(1)}, s32[]{:S(2)}) async-start(s8[6291456]{0:T(1024)(128)(4,1)} %bitcast.49), calls=%async_computation.7 | async-start | bytes 8388608
  162.7 19.1 %slice-start.1 = ((s8[6291456]{0:T(1024)(128)(4,1)}), s8[2097152]{0:T(1024)(128)(4,1)S(1)}, s32[]{:S(2)}) async-start(s8[6291456]{0:T(1024)(128)(4,1)} %bitcast.49), calls=%async_computation.8 | async-start | bytes 4194304
  272.0 1.0 copy-start.2
  314.4 20.5 %collective-permute-start.4 = (bf16[64,4096]{1,0:T(8,128)(2,1)}, bf16[64,4096]{1,0:T(8,128)(2,1)S(1)}, u32[]{:S(2)}, u32[]{:S(2)}) collective-permute-start(bf16[64,4096]{1,0:T(8,128)(2,1)} %get-tuple-element.32), channel_id=1, source_target_pairs={{0,8},{8,16},{16,24},{24,32},{32,40},{40,48},{48,56},{56,0},{1,9},... | collective-permute-start | bytes 1572872 | tf_op jit(solution)/shard_map/ppermute | solution.py:277
Sparse Core Ops, SparseCore 0:
  11.2 64.1 all-gather.2
  272.2 59.1 reduce-scatter.1

commit v11 on v10

--- a/solution.py
+++ b/solution.py
@@ -10,9 +10,9 @@
 from jax.sharding import PartitionSpec as P
 
 DEPTH = 512
-STEP = 1024
+STEP = 2048
 LISTS = 512
-NEAR = (0, 1)
+NEAR = (0, -1, 1)
 
 
 def slot_table(routes, gate_probs, sizes, capacity):
@@ -241,7 +241,7 @@
     def flat(rows):
         return rows.reshape(-1, model_width)
 
-    offsets = [*NEAR, *range(len(NEAR), z_size)]
+    offsets = [*NEAR, *(d for d in range(2, z_size - 1))]
     near_count, far_count = len(NEAR), z_size - len(NEAR)
     order = jnp.stack([my_z + d for d in offsets]) % z_size
 
@@ -249,7 +249,7 @@
     table = jnp.pad(table, ((0, 0), (0, model_width - table.shape[1])))
     block = jnp.concatenate([tokens, table], axis=0)
     blocks = lax.all_gather(block, "z", axis=0, tiled=False)
-    near_blocks = [block, lax.ppermute(block, "z", down_ring)]
+    near_blocks = [block, lax.ppermute(block, "z", up_ring), lax.ppermute(block, "z", down_ring)]
 
     swap = [(0, 1), (1, 0)]
     weights = [gate_w[0], up_w[0]]
@@ -273,9 +273,9 @@
 
     answers = dot(hidden_near, w_down).astype(jnp.bfloat16)
     answers = in_plane(answers, near_count)
-    own, over = mix_near(order, near_blocks, answers, tok_count)
-    over = lax.ppermute(over, "z", up_ring)
-    total = total.astype(jnp.float32) + own + over.astype(jnp.float32)
+    own, under, over = mix_near(order, near_blocks, answers, tok_count)
+    under, over = lax.ppermute(under, "z", down_ring), lax.ppermute(over, "z", up_ring)
+    total = total.astype(jnp.float32) + own + under.astype(jnp.float32) + over.astype(jnp.float32)
     return total.astype(jnp.bfloat16)
 
 

time: 345 us -> 329 us (0.954)
  blocking collectives: 220 us -> 203 us
  starting transfers between devices: 6.59 us -> 17.1 us
  waiting for transfers between devices: 33.2 us -> 27.9 us
  Pallas kernels: 43.1 us -> 38.7 us
    all_to_all x4, blocking collectives: 220 us -> 203 us  [in_plane(): lax.all_to_all(rows, ('x', 'y'), split_axis=0, concat_axis=0, tiled=True)]
    ppermute x2 -> x4, starting transfers between devices: 5.86 us -> 16.4 us  [the longest x1 10.5 us: body(): lax.ppermute(under, 'z', down_ring)]
    ppermute x2 -> x4, waiting for transfers between devices: 33.2 us -> 27.9 us  [the longest x1 12.6 us: body(): lax.ppermute(block, 'z', down_ring)]
  transfers between devices with their start and end apart: 7 -> 9, of which waited for: 2 -> 4; matrix products, arithmetic and copies ran while one was open for 4% -> 4% of each run, Pallas kernels for 3% -> 3%
where the time goes in v11:
time: 329 us; the launch traced here: 328 us
  blocking collectives  203 us (62%)
  Pallas kernels  38.7 us (12%)
  waiting for transfers between devices  27.9 us (8%)
  starting transfers between devices  17.1 us (5%)
  between operations  13.5 us (4%)
  other arithmetic  12.8 us (4%)
  matrix products  11.3 us (3%)
  local copies, waits for them, and re-layouts  3.46 us (1%)
    all_to_all x4, blocking collectives, in_plane(): lax.all_to_all(rows, ('x', 'y'), split_axis=0, concat_axis=0, tiled=True)  203 us
    pallas_call x1, Pallas kernels, hidden_of(): pl.pallas_call(hidden_kernel, grid=(depth // DEPTH,), in_specs=[pl.BlockS...  19.1 us
    ppermute x1, waiting for transfers between devices, body(): lax.ppermute(block, 'z', down_ring)  12.6 us
    dot_general x2, matrix products, dot(): return jnp.dot(a, b, preferred_element_type=jnp.float32)  11.3 us
    ppermute x1, starting transfers between devices, body(): lax.ppermute(under, 'z', down_ring)  10.5 us
    ppermute x1, waiting for transfers between devices, body(): lax.ppermute(under, 'z', down_ring)  8.63 us
  transfers between devices with their start and end apart: 9, of which 4 were waited for; matrix products, arithmetic and copies ran while one was open for 4% of the time, Pallas kernels for 3%

profile of v11, /device:TPU:2, one launch (start us, length us, event | category | flops | bytes accessed | tf_op | source)
XLA Modules:
  0.0 328.0 jit_solution(750820045811956831)
XLA Ops:
  6.5 0.0 all-gather.3.cloned.1.call-start
  6.5 0.8 reshape.159
  7.3 0.8 broadcast_in_dim.27
  8.1 0.3 convert_reduce_fusion
  8.4 0.6 select_reduce_fusion.1
  9.1 1.9 fusion.4.refs_0_.refs_3_
  11.0 0.0 all-gather.3.cloned.1.call-update
  11.0 0.0 reduce-scatter.2.cloned.1.call-start
  11.1 0.1 collective-permute-start.2
  11.2 0.5 collective-permute-start
  11.7 0.1 collective-permute-start.1
  11.8 5.9 %collective-permute-start.4 = (bf16[72,4096]{1,0:T(8,128)(2,1)}, bf16[72,4096]{1,0:T(8,128)(2,1)S(1)}, u32[]{:S(2)}, u32[]{:S(2)}) collective-permute-start(bf16[72,4096]{1,0:T(8,128)(2,1)} %fusion.4.refs_0_.refs_3_), channel_id=1, source_target_pairs={{0,56},{8,0},{16,8},{24,16},{32,24},{40,32},{48,40},{56,48},{1,57}... | collective-permute-start | bytes 1769480 | tf_op jit(solution)/shard_map/ppermute | solution.py:252
  17.6 0.0 collective-permute-start.3
  17.6 0.1 stack.45
  17.7 0.6 and_select_fusion.order_ref
  18.3 0.0 collective-permute-done.2
  18.3 6.3 %pad_maximum_fusion = bf16[768,4096]{1,0:T(8,128)(2,1)} fusion(bf16[384,4096]{1,0:T(8,128)(2,1)} %collective-permute-done.2, bf16[384,4096]{1,0:T(8,128)(2,1)} %bitcast.58), kind=kLoop, calls=%fused_computation.1 | loop fusion | flops 12582912 | bytes 12582912 | tf_op jit(solution)/shard_map/concatenate | solution.py:257
  24.6 12.6 %collective-permute-done.4.refs_2_.refs_5_ = bf16[72,4096]{1,0:T(8,128)(2,1)S(1)} collective-permute-done((bf16[72,4096]{1,0:T(8,128)(2,1)}, bf16[72,4096]{1,0:T(8,128)(2,1)S(1)}, u32[]{:S(2)}, u32[]{:S(2)}) %collective-permute-start.4) | collective-permute-done | bytes 589856 | tf_op jit(solution)/shard_map/ppermute | solution.py:252
  37.3 0.0 copy-start.1
  37.3 3.3 collective-permute-done.3.refs_1_.refs_4_
  40.5 0.0 copy-start.2
  40.5 0.0 collective-permute-done.refs_1_
  40.6 0.0 collective-permute-done.1.refs_3_
  40.6 0.0 copy-done.1
  40.6 0.8 copy-done.2
  41.4 4.3 %pack_near.1 = bf16[16,3,8,4096]{3,2,1,0:T(8,128)(2,1)} custom-call(s32[8]{0:T(128)} %and_select_fusion.order_ref, bf16[72,4096]{1,0:T(8,128)(2,1)} %fusion.4.refs_0_.refs_3_, bf16[72,4096]{1,0:T(8,128)(2,1)} %copy-done.2, bf16[72,4096]{1,0:T(8,128)(2,1)} %copy-done.1, bf16[72,4096]{1,0:T(8,128)(2,1)} %fusion.4.refs_0_.refs_3_, bf16[72,4096]{1,0:T(8,128)(2,1)} %copy-done.2, ...), custom_call_target="tpu_custom_call" | custom-call | tf_op jit(solution)/shard_map/pack_near/pallas_call | solution.py:78
  45.7 43.1 %all_to_all.20 = bf16[16,24,4096]{2,1,0:T(8,128)(2,1)S(1)} all-to-all(bf16[16,24,4096]{2,1,0:T(8,128)(2,1)} %bitcast.48), channel_id=1, replica_groups=mesh['x'=4,'z'=8,'y'=4,'dp'=2] {'x','y'}, dimensions={0} | all-to-all | bytes 6291456 | tf_op jit(solution)/shard_map/all_to_all | solution.py:238
  88.7 0.0 copy-start
  88.7 0.6 slice_add_fusion._
  89.4 5.6 %pack_far.1 = bf16[16,5,8,4096]{3,2,1,0:T(8,128)(2,1)} custom-call(s32[8]{0:T(128)} %and_select_fusion.order_ref, bf16[8,72,4096]{2,1,0:T(8,128)(2,1)} %bitcast.39, bf16[8,72,4096]{2,1,0:T(8,128)(2,1)} %bitcast.40, bf16[8,128]{1,0:T(8,128)(2,1)} %slice_add_fusion._), custom_call_target="tpu_custom_call" | custom-call | tf_op jit(solution)/shard_map/pack_far/pallas_call | solution.py:104
  95.0 0.0 copy-done
  95.0 63.7 %all_to_all.21 = bf16[16,40,4096]{2,1,0:T(8,128)(2,1)} all-to-all(bf16[16,40,4096]{2,1,0:T(8,128)(2,1)} %bitcast.43), channel_id=1, replica_groups=mesh['x'=4,'z'=8,'y'=4,'dp'=2] {'x','y'}, dimensions={0} | all-to-all | bytes 10485760 | tf_op jit(solution)/shard_map/all_to_all | solution.py:238
  158.7 19.1 %hidden.1 = (bf16[384,768]{1,0:T(8,128)(2,1)}, bf16[640,768]{1,0:T(8,128)(2,1)}) custom-call(bf16[384,4096]{1,0:T(8,128)(2,1)} %bitcast.46, bf16[640,4096]{1,0:T(8,128)(2,1)} %bitcast.42, bf16[4096,384]{1,0:T(8,128)(2,1)} %bitcast.53, bf16[4096,384]{1,0:T(8,128)(2,1)} %collective-permute-done.refs_1_, bf16[4096,384]{1,0:T(8,128)(2,1)} %bitcast.55, ...), custom_call_target="tpu_custom_call" | custom-call | tf_op jit(solution)/shard_map/hidden/pallas_call | solution.py:209
  177.8 0.0 slice-done
  177.8 0.0 slice-done.1
  177.8 5.6 %convolution_convert_fusion = bf16[640,4096]{1,0:T(8,128)(2,1)S(1)} fusion(bf16[640,768]{1,0:T(8,128)(2,1)} %get-tuple-element.29, bf16[768,4096]{1,0:T(8,128)(2,1)S(1)} %bitcast.50), kind=kOutput, calls=%fused_computation | convolution fusion | flops 4029153280 | bytes 12517376 | tf_op jit(solution)/shard_map/dot_general | solution.py:223
  183.5 60.0 %all_to_all.22 = bf16[16,40,4096]{2,1,0:T(8,128)(2,1)} all-to-all(bf16[16,40,4096]{2,1,0:T(8,128)(2,1)S(1)} %bitcast.51), channel_id=1, replica_groups=mesh['x'=4,'z'=8,'y'=4,'dp'=2] {'x','y'}, dimensions={0} | all-to-all | bytes 10485760 | tf_op jit(solution)/shard_map/all_to_all | solution.py:238
  243.4 5.5 %mix_far.1 = bf16[8,64,4096]{2,1,0:T(8,128)(2,1)} custom-call(s32[8]{0:T(128)} %and_select_fusion.order_ref, bf16[8,72,4096]{2,1,0:T(8,128)(2,1)} %bitcast.41, bf16[16,5,8,4096]{3,2,1,0:T(8,128)(2,1)} %bitcast.44), custom_call_target="tpu_custom_call" | custom-call | tf_op jit(solution)/shard_map/mix_far/pallas_call | solution.py:135
  249.0 0.0 reduce-scatter.2.cloned.1.call-update
  249.0 1.0 copy-done.3
  250.0 5.6 %convolution_convert_fusion.1 = bf16[384,4096]{1,0:T(8,128)(2,1)S(1)} fusion(bf16[384,768]{1,0:T(8,128)(2,1)S(1)} %copy-done.3, bf16[768,4096]{1,0:T(8,128)(2,1)} %pad_maximum_fusion), kind=kOutput, calls=%fused_computation.2 | convolution fusion | flops 2417491968 | bytes 10027008 | tf_op jit(solution)/shard_map/dot_general | solution.py:223
  255.7 36.5 %all_to_all.23 = bf16[16,24,4096]{2,1,0:T(8,128)(2,1)} all-to-all(bf16[16,24,4096]{2,1,0:T(8,128)(2,1)S(1)} %bitcast.56), channel_id=1, replica_groups=mesh['x'=4,'z'=8,'y'=4,'dp'=2] {'x','y'}, dimensions={0} | all-to-all | bytes 6291456 | tf_op jit(solution)/shard_map/all_to_all | solution.py:238
  292.2 4.1 %mix_near.1 = (f32[64,4096]{1,0:T(8,128)}, bf16[64,4096]{1,0:T(8,128)(2,1)}, bf16[64,4096]{1,0:T(8,128)(2,1)}) custom-call(s32[8]{0:T(128)} %and_select_fusion.order_ref, bf16[72,4096]{1,0:T(8,128)(2,1)} %fusion.4.refs_0_.refs_3_, bf16[72,4096]{1,0:T(8,128)(2,1)} %copy-done.2, bf16[72,4096]{1,0:T(8,128)(2,1)} %copy-done.1, bf16[16,3,8,4096]{3,2,1,0:T(8,128)(2,1)} %bitcast.47), custom_call_target="tpu_custom_call" | custom-call | tf_op jit(solution)/shard_map/mix_near/pallas_call | solution.py:165
  296.3 10.5 %collective-permute-start.5 = (bf16[64,4096]{1,0:T(8,128)(2,1)}, bf16[64,4096]{1,0:T(8,128)(2,1)S(1)}, u32[]{:S(2)}, u32[]{:S(2)}) collective-permute-start(bf16[64,4096]{1,0:T(8,128)(2,1)} %get-tuple-element.35), channel_id=1, source_target_pairs={{0,56},{8,0},{16,8},{24,16},{32,24},{40,32},{48,40},{56,48},{1,57}... | collective-permute-start | bytes 1572872 | tf_op jit(solution)/shard_map/ppermute | solution.py:277
  306.8 0.0 collective-permute-start.6
  306.8 8.6 %collective-permute-done.5 = bf16[64,4096]{1,0:T(8,128)(2,1)S(1)} collective-permute-done((bf16[64,4096]{1,0:T(8,128)(2,1)}, bf16[64,4096]{1,0:T(8,128)(2,1)S(1)}, u32[]{:S(2)}, u32[]{:S(2)}) %collective-permute-start.5) | collective-permute-done | bytes 524320 | tf_op jit(solution)/shard_map/ppermute | solution.py:277
  315.4 3.3 %collective-permute-done.6 = bf16[64,4096]{1,0:T(8,128)(2,1)S(1)} collective-permute-done((bf16[64,4096]{1,0:T(8,128)(2,1)}, bf16[64,4096]{1,0:T(8,128)(2,1)S(1)}, u32[]{:S(2)}, u32[]{:S(2)}) %collective-permute-start.6) | collective-permute-done | bytes 524320 | tf_op jit(solution)/shard_map/ppermute | solution.py:277
  318.7 2.4 fusion.3
  (10 shorter events, 0.1 us)
Async XLA Ops:
  6.5 82.8 %all-gather.3.cloned.1.call-start = ((), (), s32[]{:S(2)}) async-start(), calls=%async_computation.6 | async-start | bytes 5308416 | tf_op jit(solution)/shard_map/all_gather | solution.py:251
  11.0 307.7 %reduce-scatter.2.cloned.1.call-start = ((), (), s32[]{:S(2)}) async-start(), calls=%async_computation.5 | async-start | bytes 4718592 | tf_op jit(solution)/shard_map/reduce_scatter | solution.py:272
  11.1 7.3 %collective-permute-start.2 = (bf16[384,4096]{1,0:T(8,128)(2,1)}, bf16[384,4096]{1,0:T(8,128)(2,1)}, u32[]{:S(2)}, u32[]{:S(2)}) collective-permute-start(bf16[384,4096]{1,0:T(8,128)(2,1)} %bitcast.57), channel_id=1, source_target_pairs={{0,1},{1,0},{2,3},{3,2},{4,5},{5,4},{6,7},{7,6},{8,9},{9,8},{10,11... | collective-permute-start | bytes 9437192 | tf_op jit(solution)/shard_map/ppermute | solution.py:257
  11.2 29.4 %collective-permute-start = (bf16[4096,384]{1,0:T(8,128)(2,1)}, bf16[4096,384]{1,0:T(8,128)(2,1)}, u32[]{:S(2)}, u32[]{:S(2)}) collective-permute-start(bf16[4096,384]{1,0:T(8,128)(2,1)} %bitcast.52), channel_id=1, source_target_pairs={{0,1},{1,0},{2,3},{3,2},{4,5},{5,4},{6,7},{7,6},{8,9},{9,8},{10,11... | collective-permute-start | bytes 9437192 | tf_op jit(solution)/shard_map/ppermute | solution.py:256
  11.7 28.9 %collective-permute-start.1 = (bf16[4096,384]{1,0:T(8,128)(2,1)}, bf16[4096,384]{1,0:T(8,128)(2,1)}, u32[]{:S(2)}, u32[]{:S(2)}) collective-permute-start(bf16[4096,384]{1,0:T(8,128)(2,1)} %bitcast.54), channel_id=1, source_target_pairs={{0,1},{1,0},{2,3},{3,2},{4,5},{5,4},{6,7},{7,6},{8,9},{9,8},{10,11... | collective-permute-start | bytes 9437192 | tf_op jit(solution)/shard_map/ppermute | solution.py:256
  11.8 25.5 %collective-permute-start.4 = (bf16[72,4096]{1,0:T(8,128)(2,1)}, bf16[72,4096]{1,0:T(8,128)(2,1)S(1)}, u32[]{:S(2)}, u32[]{:S(2)}) collective-permute-start(bf16[72,4096]{1,0:T(8,128)(2,1)} %fusion.4.refs_0_.refs_3_), channel_id=1, source_target_pairs={{0,56},{8,0},{16,8},{24,16},{32,24},{40,32},{48,40},{56,48},{1,57}... | collective-permute-start | bytes 1769480 | tf_op jit(solution)/shard_map/ppermute | solution.py:252
  17.6 22.9 %collective-permute-start.3 = (bf16[72,4096]{1,0:T(8,128)(2,1)}, bf16[72,4096]{1,0:T(8,128)(2,1)S(1)}, u32[]{:S(2)}, u32[]{:S(2)}) collective-permute-start(bf16[72,4096]{1,0:T(8,128)(2,1)} %fusion.4.refs_0_.refs_3_), channel_id=1, source_target_pairs={{0,8},{8,16},{16,24},{24,32},{32,40},{40,48},{48,56},{56,0},{1,9},... | collective-permute-start | bytes 1769480 | tf_op jit(solution)/shard_map/ppermute | solution.py:252
  37.3 3.3 %copy-start.1 = (bf16[72,4096]{1,0:T(8,128)(2,1)}, bf16[72,4096]{1,0:T(8,128)(2,1)S(1)}, u32[]{:S(2)}) copy-start(bf16[72,4096]{1,0:T(8,128)(2,1)S(1)} %collective-permute-done.4.refs_2_.refs_5_) | copy-start | bytes 1769476
  40.5 0.8 copy-start.2
  88.7 6.3 %copy-start = (bf16[16,24,4096]{2,1,0:T(8,128)(2,1)}, bf16[16,24,4096]{2,1,0:T(8,128)(2,1)S(1)}, u32[]{:S(2)}) copy-start(bf16[16,24,4096]{2,1,0:T(8,128)(2,1)S(1)} %all_to_all.20) | copy-start | bytes 9437188
  95.0 82.8 %slice-start = ((s8[6291456]{0:T(1024)(128)(4,1)}), s8[4194304]{0:T(1024)(128)(4,1)S(1)}, s32[]{:S(2)}) async-start(s8[6291456]{0:T(1024)(128)(4,1)} %bitcast.49), calls=%async_computation.7 | async-start | bytes 8388608
  158.7 19.1 %slice-start.1 = ((s8[6291456]{0:T(1024)(128)(4,1)}), s8[2097152]{0:T(1024)(128)(4,1)S(1)}, s32[]{:S(2)}) async-start(s8[6291456]{0:T(1024)(128)(4,1)} %bitcast.49), calls=%async_computation.8 | async-start | bytes 4194304
  249.0 1.1 copy-start.3
  296.3 19.2 %collective-permute-start.5 = (bf16[64,4096]{1,0:T(8,128)(2,1)}, bf16[64,4096]{1,0:T(8,128)(2,1)S(1)}, u32[]{:S(2)}, u32[]{:S(2)}) collective-permute-start(bf16[64,4096]{1,0:T(8,128)(2,1)} %get-tuple-element.35), channel_id=1, source_target_pairs={{0,56},{8,0},{16,8},{24,16},{32,24},{40,32},{48,40},{56,48},{1,57}... | collective-permute-start | bytes 1572872 | tf_op jit(solution)/shard_map/ppermute | solution.py:277
  306.8 11.9 %collective-permute-start.6 = (bf16[64,4096]{1,0:T(8,128)(2,1)}, bf16[64,4096]{1,0:T(8,128)(2,1)S(1)}, u32[]{:S(2)}, u32[]{:S(2)}) collective-permute-start(bf16[64,4096]{1,0:T(8,128)(2,1)} %get-tuple-element.36), channel_id=1, source_target_pairs={{0,8},{8,16},{16,24},{24,32},{32,40},{40,48},{48,56},{56,0},{1,9},... | collective-permute-start | bytes 1572872 | tf_op jit(solution)/shard_map/ppermute | solution.py:277
Sparse Core Ops, SparseCore 0:
  11.2 68.1 all-gather.2
  249.1 53.8 reduce-scatter.1

commit v12 on v11

--- a/solution.py
+++ b/solution.py
@@ -53,6 +53,15 @@
     return [rows[:, r * lanes : (r + 1) * lanes] for r in range(3)]
 
 
+def kept_lists(kept, i, rows_ref, me, lanes):
+    @pl.when(pl.program_id(0) == 0)
+    def _():
+        for r, part in enumerate(lists_of(rows_ref[...], me, lanes)):
+            kept[i, r : r + 1, :] = part
+
+    return [kept[i, r : r + 1, :] for r in range(3)]
+
+
 def mixed(lists, rows, tok_count):
     here = hits(lists[0], tok_count)
     both = jnp.concatenate([jnp.where(here, part, 0.0) for part in lists[1:]], axis=0)
@@ -61,12 +70,12 @@
 
 
 def pack_near_kernel(order_ref, *refs):
-    *list_refs, out_ref = refs
+    *list_refs, out_ref, kept = refs
     count = len(list_refs) // 2
     plane, _, capacity, width = out_ref.shape
     for i in range(count):
         token_ref = list_refs[count + i]
-        lists = lists_of(list_refs[i][...], order_ref[0], plane * capacity)
+        lists = kept_lists(kept, i, list_refs[i], order_ref[0], plane * capacity)
         rows = place_rows(hits(lists[0], token_ref.shape[0]), token_ref[...])
         out_ref[:, i] = rows.reshape(plane, capacity, width)
 
@@ -83,17 +92,18 @@
             in_specs=[below] * count
             + [pl.BlockSpec((tok_count, STEP), lambda i, order: (0, i))] * count,
             out_specs=pl.BlockSpec((plane, count, capacity, STEP), lambda i, order: (0, 0, 0, i)),
+            scratch_shapes=[pltpu.VMEM((count, 3, plane * capacity), jnp.float32)],
         ),
         out_shape=jax.ShapeDtypeStruct((plane, count, capacity, width), jnp.bfloat16),
         name="pack_near",
     )(order, *blocks, *blocks)
 
 
-def pack_far_kernel(order_ref, lists_ref, tok_ref, _, out_ref):
+def pack_far_kernel(order_ref, lists_ref, tok_ref, _, out_ref, kept):
     plane, count, capacity, width = out_ref.shape
     for i in range(count):
         src = order_ref[len(NEAR) + i]
-        lists = lists_of(lists_ref[src], order_ref[0], plane * capacity)
+        lists = kept_lists(kept, i, lists_ref.at[src], order_ref[0], plane * capacity)
         rows = place_rows(hits(lists[0], tok_ref.shape[1]), tok_ref[src])
         out_ref[:, i] = rows.reshape(plane, capacity, width)
 
@@ -112,19 +122,20 @@
                 pl.BlockSpec(after.shape, lambda i, order: (0, 0)),
             ],
             out_specs=pl.BlockSpec((plane, count, capacity, STEP), lambda i, order: (0, 0, 0, i)),
+            scratch_shapes=[pltpu.VMEM((count, 3, plane * capacity), jnp.float32)],
         ),
         out_shape=jax.ShapeDtypeStruct((plane, count, capacity, width), jnp.bfloat16),
         name="pack_far",
     )(order, blocks, blocks, after)
 
 
-def mix_far_kernel(order_ref, lists_ref, rows_ref, out_ref):
+def mix_far_kernel(order_ref, lists_ref, rows_ref, out_ref, kept):
     plane, count, capacity, width = rows_ref.shape
     for i in range(len(NEAR)):
         out_ref[order_ref[i]] = jnp.zeros(out_ref.shape[1:], out_ref.dtype)
     for i in range(count):
         src = order_ref[len(NEAR) + i]
-        lists = lists_of(lists_ref[src], order_ref[0], plane * capacity)
+        lists = kept_lists(kept, i, lists_ref.at[src], order_ref[0], plane * capacity)
         rows = rows_ref[:, i].reshape(plane * capacity, width)
         out_ref[src] = mixed(lists, rows, out_ref.shape[1]).astype(out_ref.dtype)
 
@@ -142,6 +153,7 @@
                 pl.BlockSpec((plane, count, capacity, STEP), lambda i, order: (0, 0, 0, i)),
             ],
             out_specs=pl.BlockSpec((z_size, tok_count, STEP), lambda i, order: (0, 0, i)),
+            scratch_shapes=[pltpu.VMEM((count, 3, plane * capacity), jnp.float32)],
         ),
         out_shape=jax.ShapeDtypeStruct((z_size, tok_count, width), jnp.bfloat16),
         name="mix_far",
@@ -150,10 +162,10 @@
 
 def mix_near_kernel(order_ref, *refs):
     count = len(NEAR)
-    rows_ref, outs = refs[count], refs[count + 1 :]
+    rows_ref, *outs, kept = refs[count:]
     plane, _, capacity, width = rows_ref.shape
     for i in range(count):
-        lists = lists_of(refs[i][...], order_ref[0], plane * capacity)
+        lists = kept_lists(kept, i, refs[i], order_ref[0], plane * capacity)
         rows = rows_ref[:, i].reshape(plane * capacity, width)
         outs[i][...] = mixed(lists, rows, outs[i].shape[0]).astype(outs[i].dtype)
 
@@ -171,6 +183,7 @@
             * count
             + [pl.BlockSpec((plane, count, capacity, STEP), lambda i, order: (0, 0, 0, i))],
             out_specs=[pl.BlockSpec((tok_count, STEP), lambda i, order: (0, i))] * count,
+            scratch_shapes=[pltpu.VMEM((count, 3, plane * capacity), jnp.float32)],
         ),
         out_shape=[jax.ShapeDtypeStruct((tok_count, width), kind) for kind in kinds],
         name="mix_near",

time: 329 us -> 333 us (1.012)
  Pallas kernels: 38.7 us -> 42.9 us
where the time goes in v12:
time: 333 us; the launch traced here: 332 us
  blocking collectives  203 us (61%)
  Pallas kernels  42.9 us (13%)
  waiting for transfers between devices  27.8 us (8%)
  starting transfers between devices  16.9 us (5%)
  between operations  13.5 us (4%)
  other arithmetic  12.8 us (4%)
  matrix products  11.2 us (3%)
  local copies, waits for them, and re-layouts  3.46 us (1%)
    all_to_all x4, blocking collectives, in_plane(): lax.all_to_all(rows, ('x', 'y'), split_axis=0, concat_axis=0, tiled=True)  203 us
    pallas_call x1, Pallas kernels, hidden_of(): pl.pallas_call(hidden_kernel, grid=(depth // DEPTH,), in_specs=[pl.BlockS...  19.1 us
    ppermute x1, waiting for transfers between devices, body(): lax.ppermute(block, 'z', down_ring)  12.6 us
    dot_general x2, matrix products, dot(): return jnp.dot(a, b, preferred_element_type=jnp.float32)  11.2 us
    ppermute x1, starting transfers between devices, body(): lax.ppermute(under, 'z', down_ring)  10.4 us
    ppermute x1, waiting for transfers between devices, body(): lax.ppermute(under, 'z', down_ring)  8.51 us
    pallas_call x1, Pallas kernels, pack_far(): pl.pallas_call(pack_far_kernel, grid_spec=pltpu.PrefetchScalarGridSpec(nu...  7.22 us
    pallas_call x1, Pallas kernels, mix_far(): pl.pallas_call(mix_far_kernel, grid_spec=pltpu.PrefetchScalarGridSpec(num...  6.83 us
  transfers between devices with their start and end apart: 9, of which 4 were waited for; matrix products, arithmetic and copies ran while one was open for 4% of the time, Pallas kernels for 3%

profile of v12, /device:TPU:2, one launch (start us, length us, event | category | flops | bytes accessed | tf_op | source)
XLA Modules:
  0.0 332.0 jit_solution(7466173281052308916)
XLA Ops:
  6.5 0.0 all-gather.3.cloned.1.call-start
  6.5 0.8 reshape.159
  7.3 0.8 broadcast_in_dim.27
  8.1 0.3 convert_reduce_fusion
  8.4 0.6 select_reduce_fusion.1
  9.1 1.9 fusion.4.refs_0_.refs_3_
  11.0 0.0 all-gather.3.cloned.1.call-update
  11.0 0.0 reduce-scatter.2.cloned.1.call-start
  11.1 0.1 collective-permute-start.2
  11.2 0.5 collective-permute-start
  11.7 0.1 collective-permute-start.1
  11.8 5.9 %collective-permute-start.4 = (bf16[72,4096]{1,0:T(8,128)(2,1)}, bf16[72,4096]{1,0:T(8,128)(2,1)S(1)}, u32[]{:S(2)}, u32[]{:S(2)}) collective-permute-start(bf16[72,4096]{1,0:T(8,128)(2,1)} %fusion.4.refs_0_.refs_3_), channel_id=1, source_target_pairs={{0,56},{8,0},{16,8},{24,16},{32,24},{40,32},{48,40},{56,48},{1,57}... | collective-permute-start | bytes 1769480 | tf_op jit(solution)/shard_map/ppermute | solution.py:265
  17.6 0.0 collective-permute-start.3
  17.6 0.1 stack.45
  17.7 0.6 and_select_fusion.order_ref
  18.3 0.0 collective-permute-done.2
  18.3 6.3 %pad_maximum_fusion = bf16[768,4096]{1,0:T(8,128)(2,1)} fusion(bf16[384,4096]{1,0:T(8,128)(2,1)} %collective-permute-done.2, bf16[384,4096]{1,0:T(8,128)(2,1)} %bitcast.58), kind=kLoop, calls=%fused_computation.1 | loop fusion | flops 12582912 | bytes 12582912 | tf_op jit(solution)/shard_map/concatenate | solution.py:270
  24.6 12.6 %collective-permute-done.4.refs_2_.refs_5_ = bf16[72,4096]{1,0:T(8,128)(2,1)S(1)} collective-permute-done((bf16[72,4096]{1,0:T(8,128)(2,1)}, bf16[72,4096]{1,0:T(8,128)(2,1)S(1)}, u32[]{:S(2)}, u32[]{:S(2)}) %collective-permute-start.4) | collective-permute-done | bytes 589856 | tf_op jit(solution)/shard_map/ppermute | solution.py:265
  37.3 0.0 copy-start.1
  37.3 3.3 collective-permute-done.3.refs_1_.refs_4_
  40.5 0.0 copy-start.2
  40.5 0.0 collective-permute-done.refs_1_
  40.6 0.0 collective-permute-done.1.refs_3_
  40.6 0.0 copy-done.1
  40.6 0.8 copy-done.2
  41.4 5.1 %pack_near.1 = bf16[16,3,8,4096]{3,2,1,0:T(8,128)(2,1)} custom-call(s32[8]{0:T(128)} %and_select_fusion.order_ref, bf16[72,4096]{1,0:T(8,128)(2,1)} %fusion.4.refs_0_.refs_3_, bf16[72,4096]{1,0:T(8,128)(2,1)} %copy-done.2, bf16[72,4096]{1,0:T(8,128)(2,1)} %copy-done.1, bf16[72,4096]{1,0:T(8,128)(2,1)} %fusion.4.refs_0_.refs_3_, bf16[72,4096]{1,0:T(8,128)(2,1)} %copy-done.2, ...), custom_call_target="tpu_custom_call" | custom-call | tf_op jit(solution)/shard_map/pack_near/pallas_call | solution.py:87
  46.5 43.1 %all_to_all.20 = bf16[16,24,4096]{2,1,0:T(8,128)(2,1)S(1)} all-to-all(bf16[16,24,4096]{2,1,0:T(8,128)(2,1)} %bitcast.48), channel_id=1, replica_groups=mesh['x'=4,'z'=8,'y'=4,'dp'=2] {'x','y'}, dimensions={0} | all-to-all | bytes 6291456 | tf_op jit(solution)/shard_map/all_to_all | solution.py:251
  89.5 0.0 copy-start
  89.5 0.6 slice_add_fusion._
  90.1 7.2 %pack_far.1 = bf16[16,5,8,4096]{3,2,1,0:T(8,128)(2,1)} custom-call(s32[8]{0:T(128)} %and_select_fusion.order_ref, bf16[8,72,4096]{2,1,0:T(8,128)(2,1)} %bitcast.39, bf16[8,72,4096]{2,1,0:T(8,128)(2,1)} %bitcast.40, bf16[8,128]{1,0:T(8,128)(2,1)} %slice_add_fusion._), custom_call_target="tpu_custom_call" | custom-call | tf_op jit(solution)/shard_map/pack_far/pallas_call | solution.py:114
  97.4 0.0 copy-done
  97.4 63.7 %all_to_all.21 = bf16[16,40,4096]{2,1,0:T(8,128)(2,1)} all-to-all(bf16[16,40,4096]{2,1,0:T(8,128)(2,1)} %bitcast.43), channel_id=1, replica_groups=mesh['x'=4,'z'=8,'y'=4,'dp'=2] {'x','y'}, dimensions={0} | all-to-all | bytes 10485760 | tf_op jit(solution)/shard_map/all_to_all | solution.py:251
  161.1 19.1 %hidden.1 = (bf16[384,768]{1,0:T(8,128)(2,1)}, bf16[640,768]{1,0:T(8,128)(2,1)}) custom-call(bf16[384,4096]{1,0:T(8,128)(2,1)} %bitcast.46, bf16[640,4096]{1,0:T(8,128)(2,1)} %bitcast.42, bf16[4096,384]{1,0:T(8,128)(2,1)} %bitcast.53, bf16[4096,384]{1,0:T(8,128)(2,1)} %collective-permute-done.refs_1_, bf16[4096,384]{1,0:T(8,128)(2,1)} %bitcast.55, ...), custom_call_target="tpu_custom_call" | custom-call | tf_op jit(solution)/shard_map/hidden/pallas_call | solution.py:222
  180.2 0.0 slice-done
  180.2 0.0 slice-done.1
  180.2 5.6 %convolution_convert_fusion = bf16[640,4096]{1,0:T(8,128)(2,1)S(1)} fusion(bf16[640,768]{1,0:T(8,128)(2,1)} %get-tuple-element.29, bf16[768,4096]{1,0:T(8,128)(2,1)S(1)} %bitcast.50), kind=kOutput, calls=%fused_computation | convolution fusion | flops 4029153280 | bytes 12517376 | tf_op jit(solution)/shard_map/dot_general | solution.py:236
  185.8 60.0 %all_to_all.22 = bf16[16,40,4096]{2,1,0:T(8,128)(2,1)} all-to-all(bf16[16,40,4096]{2,1,0:T(8,128)(2,1)S(1)} %bitcast.51), channel_id=1, replica_groups=mesh['x'=4,'z'=8,'y'=4,'dp'=2] {'x','y'}, dimensions={0} | all-to-all | bytes 10485760 | tf_op jit(solution)/shard_map/all_to_all | solution.py:251
  245.9 6.8 %mix_far.1 = bf16[8,64,4096]{2,1,0:T(8,128)(2,1)} custom-call(s32[8]{0:T(128)} %and_select_fusion.order_ref, bf16[8,72,4096]{2,1,0:T(8,128)(2,1)} %bitcast.41, bf16[16,5,8,4096]{3,2,1,0:T(8,128)(2,1)} %bitcast.44), custom_call_target="tpu_custom_call" | custom-call | tf_op jit(solution)/shard_map/mix_far/pallas_call | solution.py:146
  252.7 0.0 reduce-scatter.2.cloned.1.call-update
  252.7 1.0 copy-done.3
  253.8 5.6 %convolution_convert_fusion.1 = bf16[384,4096]{1,0:T(8,128)(2,1)S(1)} fusion(bf16[384,768]{1,0:T(8,128)(2,1)S(1)} %copy-done.3, bf16[768,4096]{1,0:T(8,128)(2,1)} %pad_maximum_fusion), kind=kOutput, calls=%fused_computation.2 | convolution fusion | flops 2417491968 | bytes 10027008 | tf_op jit(solution)/shard_map/dot_general | solution.py:236
  259.4 36.6 %all_to_all.23 = bf16[16,24,4096]{2,1,0:T(8,128)(2,1)} all-to-all(bf16[16,24,4096]{2,1,0:T(8,128)(2,1)S(1)} %bitcast.56), channel_id=1, replica_groups=mesh['x'=4,'z'=8,'y'=4,'dp'=2] {'x','y'}, dimensions={0} | all-to-all | bytes 6291456 | tf_op jit(solution)/shard_map/all_to_all | solution.py:251
  296.0 4.6 %mix_near.1 = (f32[64,4096]{1,0:T(8,128)}, bf16[64,4096]{1,0:T(8,128)(2,1)}, bf16[64,4096]{1,0:T(8,128)(2,1)}) custom-call(s32[8]{0:T(128)} %and_select_fusion.order_ref, bf16[72,4096]{1,0:T(8,128)(2,1)} %fusion.4.refs_0_.refs_3_, bf16[72,4096]{1,0:T(8,128)(2,1)} %copy-done.2, bf16[72,4096]{1,0:T(8,128)(2,1)} %copy-done.1, bf16[16,3,8,4096]{3,2,1,0:T(8,128)(2,1)} %bitcast.47), custom_call_target="tpu_custom_call" | custom-call | tf_op jit(solution)/shard_map/mix_near/pallas_call | solution.py:177
  300.6 10.4 %collective-permute-start.5 = (bf16[64,4096]{1,0:T(8,128)(2,1)}, bf16[64,4096]{1,0:T(8,128)(2,1)S(1)}, u32[]{:S(2)}, u32[]{:S(2)}) collective-permute-start(bf16[64,4096]{1,0:T(8,128)(2,1)} %get-tuple-element.35), channel_id=1, source_target_pairs={{0,56},{8,0},{16,8},{24,16},{32,24},{40,32},{48,40},{56,48},{1,57}... | collective-permute-start | bytes 1572872 | tf_op jit(solution)/shard_map/ppermute | solution.py:290
  310.9 0.0 collective-permute-start.6
  310.9 8.5 %collective-permute-done.5 = bf16[64,4096]{1,0:T(8,128)(2,1)S(1)} collective-permute-done((bf16[64,4096]{1,0:T(8,128)(2,1)}, bf16[64,4096]{1,0:T(8,128)(2,1)S(1)}, u32[]{:S(2)}, u32[]{:S(2)}) %collective-permute-start.5) | collective-permute-done | bytes 524320 | tf_op jit(solution)/shard_map/ppermute | solution.py:290
  319.4 3.3 collective-permute-done.6
  322.7 2.4 fusion.3
  (10 shorter events, 0.1 us)
Async XLA Ops:
  6.5 83.6 %all-gather.3.cloned.1.call-start = ((), (), s32[]{:S(2)}) async-start(), calls=%async_computation.6 | async-start | bytes 5308416 | tf_op jit(solution)/shard_map/all_gather | solution.py:264
  11.0 311.7 %reduce-scatter.2.cloned.1.call-start = ((), (), s32[]{:S(2)}) async-start(), calls=%async_computation.5 | async-start | bytes 4718592 | tf_op jit(solution)/shard_map/reduce_scatter | solution.py:285
  11.1 7.3 %collective-permute-start.2 = (bf16[384,4096]{1,0:T(8,128)(2,1)}, bf16[384,4096]{1,0:T(8,128)(2,1)}, u32[]{:S(2)}, u32[]{:S(2)}) collective-permute-start(bf16[384,4096]{1,0:T(8,128)(2,1)} %bitcast.57), channel_id=1, source_target_pairs={{0,1},{1,0},{2,3},{3,2},{4,5},{5,4},{6,7},{7,6},{8,9},{9,8},{10,11... | collective-permute-start | bytes 9437192 | tf_op jit(solution)/shard_map/ppermute | solution.py:270
  11.2 29.4 %collective-permute-start = (bf16[4096,384]{1,0:T(8,128)(2,1)}, bf16[4096,384]{1,0:T(8,128)(2,1)}, u32[]{:S(2)}, u32[]{:S(2)}) collective-permute-start(bf16[4096,384]{1,0:T(8,128)(2,1)} %bitcast.52), channel_id=1, source_target_pairs={{0,1},{1,0},{2,3},{3,2},{4,5},{5,4},{6,7},{7,6},{8,9},{9,8},{10,11... | collective-permute-start | bytes 9437192 | tf_op jit(solution)/shard_map/ppermute | solution.py:269
  11.7 28.9 %collective-permute-start.1 = (bf16[4096,384]{1,0:T(8,128)(2,1)}, bf16[4096,384]{1,0:T(8,128)(2,1)}, u32[]{:S(2)}, u32[]{:S(2)}) collective-permute-start(bf16[4096,384]{1,0:T(8,128)(2,1)} %bitcast.54), channel_id=1, source_target_pairs={{0,1},{1,0},{2,3},{3,2},{4,5},{5,4},{6,7},{7,6},{8,9},{9,8},{10,11... | collective-permute-start | bytes 9437192 | tf_op jit(solution)/shard_map/ppermute | solution.py:269
  11.8 25.5 %collective-permute-start.4 = (bf16[72,4096]{1,0:T(8,128)(2,1)}, bf16[72,4096]{1,0:T(8,128)(2,1)S(1)}, u32[]{:S(2)}, u32[]{:S(2)}) collective-permute-start(bf16[72,4096]{1,0:T(8,128)(2,1)} %fusion.4.refs_0_.refs_3_), channel_id=1, source_target_pairs={{0,56},{8,0},{16,8},{24,16},{32,24},{40,32},{48,40},{56,48},{1,57}... | collective-permute-start | bytes 1769480 | tf_op jit(solution)/shard_map/ppermute | solution.py:265
  17.6 22.9 %collective-permute-start.3 = (bf16[72,4096]{1,0:T(8,128)(2,1)}, bf16[72,4096]{1,0:T(8,128)(2,1)S(1)}, u32[]{:S(2)}, u32[]{:S(2)}) collective-permute-start(bf16[72,4096]{1,0:T(8,128)(2,1)} %fusion.4.refs_0_.refs_3_), channel_id=1, source_target_pairs={{0,8},{8,16},{16,24},{24,32},{32,40},{40,48},{48,56},{56,0},{1,9},... | collective-permute-start | bytes 1769480 | tf_op jit(solution)/shard_map/ppermute | solution.py:265
  37.3 3.3 copy-start.1
  40.5 0.8 copy-start.2
  89.5 7.8 %copy-start = (bf16[16,24,4096]{2,1,0:T(8,128)(2,1)}, bf16[16,24,4096]{2,1,0:T(8,128)(2,1)S(1)}, u32[]{:S(2)}) copy-start(bf16[16,24,4096]{2,1,0:T(8,128)(2,1)S(1)} %all_to_all.20) | copy-start | bytes 9437188
  97.4 82.8 %slice-start = ((s8[6291456]{0:T(1024)(128)(4,1)}), s8[4194304]{0:T(1024)(128)(4,1)S(1)}, s32[]{:S(2)}) async-start(s8[6291456]{0:T(1024)(128)(4,1)} %bitcast.49), calls=%async_computation.7 | async-start | bytes 8388608
  161.0 19.1 %slice-start.1 = ((s8[6291456]{0:T(1024)(128)(4,1)}), s8[2097152]{0:T(1024)(128)(4,1)S(1)}, s32[]{:S(2)}) async-start(s8[6291456]{0:T(1024)(128)(4,1)} %bitcast.49), calls=%async_computation.8 | async-start | bytes 4194304
  252.7 1.1 copy-start.3
  300.6 18.9 %collective-permute-start.5 = (bf16[64,4096]{1,0:T(8,128)(2,1)}, bf16[64,4096]{1,0:T(8,128)(2,1)S(1)}, u32[]{:S(2)}, u32[]{:S(2)}) collective-permute-start(bf16[64,4096]{1,0:T(8,128)(2,1)} %get-tuple-element.35), channel_id=1, source_target_pairs={{0,56},{8,0},{16,8},{24,16},{32,24},{40,32},{48,40},{56,48},{1,57}... | collective-permute-start | bytes 1572872 | tf_op jit(solution)/shard_map/ppermute | solution.py:290
  310.9 11.8 %collective-permute-start.6 = (bf16[64,4096]{1,0:T(8,128)(2,1)}, bf16[64,4096]{1,0:T(8,128)(2,1)S(1)}, u32[]{:S(2)}, u32[]{:S(2)}) collective-permute-start(bf16[64,4096]{1,0:T(8,128)(2,1)} %get-tuple-element.36), channel_id=1, source_target_pairs={{0,8},{8,16},{16,24},{24,32},{32,40},{40,48},{48,56},{56,0},{1,9},... | collective-permute-start | bytes 1572872 | tf_op jit(solution)/shard_map/ppermute | solution.py:290
Sparse Core Ops, SparseCore 0:
  11.2 68.1 all-gather.2
  252.8 53.8 reduce-scatter.1
